TPU v7x, 128 devices: a whole 4x4x4 slice. The times are simulated.
128 devices in a mesh: re: 32 (over y, x, z_lo), rp: 4 (over z_hi, core).
Axes of the slice: x: 4, y: 4, z: 4 (z_hi: 2, z_lo: 2; z = z_hi * 2 + z_lo), core: 2. Of those that a mesh axis runs over, the one named last changes fastest.
Arguments:
- wannier_table: bfloat16 [1024, 128, 1536], P('re', 'rp'), may hold values from -0.0078125 to 0.0078125
- mode_matrix: float32 [2, 12, 12], replicated, may hold values from -1.75 to 1.75
- re_coords: int32 [3, 1024], replicated, may hold values from -8 to 8
- rp_coords: int32 [3, 128], P(None, 'rp'), may hold values from -6 to 6
- q_coords: int32 [3, 2], replicated, may hold values from 0 to 63
- k_coords: int32 [3, 16384], P(None, 're'), may hold values from 0 to 63
- rotations: bfloat16 [16384, 128], P('re'), may hold values from -1.5 to 1.5
- kq_owner: int32 [2, 16384, 1], P(None, 're'), may hold values from 0 to 31; in each aligned block of 512 rows (0 to 511, 512 to 1023, ..., all dimensions but the last counted through in order) at most 24 rows name the same one
- kq_row: int32 [2, 16384], P(None, 're'), may hold values from 0 to 511
Outputs:
- couplings: bfloat16 [2, 12, 2, 64, 16384], P(None, 'rp', None, None, 're')
Inputs may be any that keep to these rules, and one draw needn't show every extreme that they name: `kq_owner`: for each wavevector, among the 512 k-rows of one device no owner is named more than 24 times, a bound that some block reaches.
All inputs are finite; a program needn't handle non-finite values.
Results may differ from a plain program's by a relative error of at most 0.0057.
Values may be sent and summed in bfloat16 or wider, within the bound.
No kernel may reach another device: no remote copies, remote signals or barrier semaphores. Data moves between devices by JAX's collectives and lax.ppermute only.
A program may use at most 128 MiB of HBM per device.

v0:
```python
import math

import jax
import jax.numpy as jnp
from jax import lax
from jax.sharding import PartitionSpec as P

NB = 8
MODES = 12
Q = 2
GRID = 64


def phases(left, right):
    products = jnp.sum(left[:, :, None] * right[:, None, :], axis=0)
    angles = jnp.mod(products, GRID).astype(jnp.float32) * (2.0 * math.pi / GRID)
    return (jnp.cos(angles).astype(jnp.bfloat16), jnp.sin(angles).astype(jnp.bfloat16))


def rotate(coupling, right_rot, left_rot):
    highest = lax.Precision.HIGHEST
    coupling_real = coupling[:, :, 0]
    coupling_imag = coupling[:, :, 1]
    right_real = right_rot[0]
    right_imag = right_rot[1]
    half_real = jnp.einsum(
        "qvabk,bnk->qvank", coupling_real, right_real, precision=highest
    ) - jnp.einsum("qvabk,bnk->qvank", coupling_imag, right_imag, precision=highest)
    half_imag = jnp.einsum(
        "qvabk,bnk->qvank", coupling_real, right_imag, precision=highest
    ) + jnp.einsum("qvabk,bnk->qvank", coupling_imag, right_real, precision=highest)
    left_real = left_rot[:, 0]
    left_imag = left_rot[:, 1]
    result_real = jnp.einsum(
        "qamk,qvank->qvmnk", left_real, half_real, precision=highest
    ) + jnp.einsum("qamk,qvank->qvmnk", left_imag, half_imag, precision=highest)
    result_imag = jnp.einsum(
        "qamk,qvank->qvmnk", left_real, half_imag, precision=highest
    ) - jnp.einsum("qamk,qvank->qvmnk", left_imag, half_real, precision=highest)
    return jnp.stack([result_real, result_imag], axis=2)


def local(
    wannier_table,
    mode_matrix,
    re_coords,
    rp_coords,
    q_coords,
    k_coords,
    rotations,
    kq_owner,
    kq_row,
):
    re_local = wannier_table.shape[0]
    rp_local = wannier_table.shape[1]
    k_local = k_coords.shape[1]
    width = MODES * NB * NB
    cosine_q, sine_q = phases(q_coords, rp_coords)
    values = wannier_table.reshape(re_local, rp_local, 2, width)
    with_cos = jnp.einsum("qr,ercw->eqcw", cosine_q, values, preferred_element_type=jnp.float32)
    with_sin = jnp.einsum("qr,ercw->eqcw", sine_q, values, preferred_element_type=jnp.float32)
    summed = jnp.stack(
        [with_cos[:, :, 0] - with_sin[:, :, 1], with_sin[:, :, 0] + with_cos[:, :, 1]], axis=2
    )
    summed = summed.reshape(re_local, Q, 2, MODES, NB * NB)
    mixed = jnp.einsum("eqcmz,qmn->eqcnz", summed, mode_matrix, precision=lax.Precision.HIGHEST)
    owned = lax.psum_scatter(mixed, "rp", scatter_dimension=3, tiled=True)
    modes_local = owned.shape[3]
    coupling_q = owned.astype(jnp.bfloat16).reshape(re_local, Q, 2, modes_local * NB * NB)
    k_block = min(512, k_local)
    block_count = k_local // k_block
    block_coords = k_coords.reshape(3, block_count, k_block).transpose(1, 0, 2)
    shard_piece = lax.all_gather(coupling_q, "re", axis=0, tiled=True)

    def one_block(coords_block):
        cosine_k, sine_k = phases(re_coords, coords_block)
        part_cos = jnp.einsum(
            "eqcz,ek->qczk", shard_piece, cosine_k, preferred_element_type=jnp.float32
        )
        part_sin = jnp.einsum(
            "eqcz,ek->qczk", shard_piece, sine_k, preferred_element_type=jnp.float32
        )
        return jnp.stack([part_cos[:, 0] - part_sin[:, 1], part_sin[:, 0] + part_cos[:, 1]], axis=1)

    summed_k = lax.map(one_block, block_coords)
    coupling = summed_k.reshape(block_count, Q, 2, modes_local, NB, NB, k_block)
    coupling = coupling.transpose(1, 3, 2, 4, 5, 0, 6).reshape(Q, modes_local, 2, NB, NB, k_local)
    devices = lax.axis_size("re")
    capacity = 3 * k_local // (2 * devices)
    owners = kq_owner[:, :, 0]
    one_hot = (owners[:, :, None] == jnp.arange(devices, dtype=jnp.int32)[None, None, :]).astype(
        jnp.int32
    )
    ranks = jnp.sum(one_hot * (jnp.cumsum(one_hot, axis=1) - 1), axis=2)
    slots = owners * (Q * capacity) + jnp.arange(Q, dtype=jnp.int32)[:, None] * capacity + ranks
    slots = slots.reshape(-1)
    requests = jnp.zeros((devices * Q * capacity,), jnp.int32).at[slots].set(kq_row.reshape(-1))
    requests = requests.reshape(devices, Q, capacity)
    looked_up = rotations[lax.all_to_all(requests, "re", split_axis=0, concat_axis=0, tiled=True)]
    replies = lax.all_to_all(looked_up, "re", split_axis=0, concat_axis=0, tiled=True)
    far_rotation = replies.reshape(-1, 2 * NB * NB)[slots].reshape(Q, k_local, 2 * NB * NB)
    far_rot = far_rotation.astype(jnp.float32).transpose(0, 2, 1).reshape(Q, 2, NB, NB, k_local)
    local_rot = rotations.astype(jnp.float32).T.reshape(2, NB, NB, k_local)
    result = rotate(coupling, local_rot, far_rot)
    return result.reshape(Q, modes_local, 2, NB * NB, k_local).astype(jnp.bfloat16)


def solution(mesh):
    in_specs = (
        P("re", "rp", None),
        P(),
        P(),
        P(None, "rp"),
        P(),
        P(None, "re"),
        P("re", None),
        P(None, "re", None),
        P(None, "re"),
    )
    out_specs = P(None, "rp", None, None, "re")
    return jax.shard_map(local, mesh=mesh, in_specs=in_specs, out_specs=out_specs, check_vma=False)
```

profile of v0, /device:TPU:0, one launch (start us, length us, event | category | flops | bytes accessed | tf_op | source)
XLA Modules:
  0.0 394.7 jit_solution(16396865698377199612)
XLA Ops:
  6.5 0.9 copy.79
  7.5 0.8 multiply_reduce_fusion.1
  8.3 2.5 fusion.31
  10.7 0.6 fusion.34
  11.3 0.2 slice_subtract_fusion.1
  11.5 0.3 reshape.159
  11.8 0.3 reshape.160
  12.1 1.1 convolution_bitcast_fusion
  13.2 1.3 copy.87
  14.6 32.9 %reduce-scatter.2.cloned.1.call-done = f32[32,2,2,3,64]{4,0,2,1,3:T(8,128)} async-done(((f32[32,2,2,12,64]{4,0,2,1,3:T(8,128)}), f32[32,2,2,3,64]{4,0,2,1,3:T(8,128)}) %reduce-scatter.2.cloned.1.call-update) | async-done | bytes 98320 | tf_op jit(solution)/shard_map/reduce_scatter | solution.py:67
  47.5 0.9 convert_element_type.35
  48.6 0.8 reshape.114
  49.4 2.3 reduce-window.6
  51.7 0.3 slice_reduce_fusion
  52.1 0.1 fusion.47
  52.3 4.3 %scatter_custom_fusion = s32[1536]{0:T(1024)S(1)} fusion(s32[1024]{0:T(1024)S(1)} %bitcast.158, s32[1024]{0:T(1024)S(1)} %bitcast.164, s32[]{:T(128)} %constant.30.clone.1), kind=kCustom, calls=%fused_computation.72 | custom fusion | bytes 6148 | tf_op jit(solution)/shard_map/scatter | solution.py:97
  56.7 0.7 reshape.118
  57.4 7.2 %all-to-all-start = ((s32[32,2,24]{2,1,0:T(2,128)}), s32[32,2,24]{2,1,0:T(2,128)S(1)}, u32[]{:S(2)}, u32[]{:S(2)}) async-start(s32[32,2,24]{2,1,0:T(2,128)} %reshape.118), calls=%async_computation.1 | async-start | bytes 65536 | tf_op jit(solution)/shard_map/all_to_all | solution.py:99
  64.6 0.1 copy.91
  64.7 0.7 copy.112
  65.5 1.6 copy.113
  67.1 5.8 %all-to-all-done = s32[32,2,24]{2,1,0:T(2,128)S(1)} async-done(((s32[32,2,24]{2,1,0:T(2,128)}), s32[32,2,24]{2,1,0:T(2,128)S(1)}, u32[]{:S(2)}, u32[]{:S(2)}) %all-to-all-start) | async-done | bytes 6176 | tf_op jit(solution)/shard_map/all_to_all | solution.py:99
  73.1 4.1 %gather_fusion = bf16[1536,128]{1,0:T(8,128)(2,1)} fusion(bf16[512,128]{1,0:T(8,128)(2,1)S(1)} %copy-done.3, s32[2048]{0:T(1024)S(1)} %pad_clamp_fusion), kind=kCustom, calls=%fused_computation | custom fusion | bytes 792576 | tf_op jit(solution)/shard_map/gather | solution.py:99
  77.1 4.3 %all-to-all-start.1 = ((bf16[32,2,24,128]{3,2,1,0:T(8,128)(2,1)}), bf16[32,2,24,128]{3,2,1,0:T(8,128)(2,1)S(1)}, u32[]{:S(2)}, u32[]{:S(2)}) async-start(bf16[32,2,24,128]{3,2,1,0:T(8,128)(2,1)} %bitcast.29), calls=%async_computation.2 | async-start | bytes 786432 | tf_op jit(solution)/shard_map/all_to_all | solution.py:100
  81.5 2.1 multiply_reduce_fusion
  83.6 8.2 %all-to-all-done.1 = bf16[32,2,24,128]{3,2,1,0:T(8,128)(2,1)S(1)} async-done(((bf16[32,2,24,128]{3,2,1,0:T(8,128)(2,1)}), bf16[32,2,24,128]{3,2,1,0:T(8,128)(2,1)S(1)}, u32[]{:S(2)}, u32[]{:S(2)}) %all-to-all-start.1) | async-done | bytes 393248 | tf_op jit(solution)/shard_map/all_to_all | solution.py:100
  91.9 3.2 gather_fusion.1
  95.1 0.1 copy.95
  95.3 1.5 copy.143
  96.8 2.4 copy.142
  99.1 103.0 %all-gather.2.cloned.1.call-done = bf16[1024,2,2,192]{3,0,2,1:T(8,128)(2,1)} async-done(((bf16[32,2,2,192]{3,0,2,1:T(8,128)(2,1)}), bf16[1024,2,2,192]{3,0,2,1:T(8,128)(2,1)}) %all-gather.2.cloned.1.call-update) | async-done | bytes 1572880 | tf_op jit(solution)/shard_map/all_gather | solution.py:73
  202.2 10.5 %fusion.38 = f32[2,2,192,512]{3,2,1,0:T(8,128)S(1)} fusion(bf16[1024,2,2,192]{3,0,2,1:T(8,128)(2,1)} %all-gather.2.cloned.1.call-done, s32[1024,512]{1,0:T(8,128)} %multiply_reduce_fusion), kind=kOutput, calls=%fused_computation.47 | convolution fusion | flops 812646400 | bytes 5242880 | tf_op jit(solution)/shard_map/while/body/eval_jaxpr/eqcz,ek->qczk/dot_general | solution.py:77
  212.7 8.4 %fusion.41 = f32[2,2,192,512]{3,2,1,0:T(8,128)S(1)} fusion(bf16[1024,2,2,192]{3,0,2,1:T(8,128)(2,1)S(1)} %copy-done.12, s32[1024,512]{1,0:T(8,128)S(1)} %copy-done.7), kind=kOutput, calls=%fused_computation.49 | convolution fusion | flops 812646400 | bytes 5242880 | tf_op jit(solution)/shard_map/while/body/eval_jaxpr/eqcz,ek->qczk/dot_general | solution.py:80
  221.1 1.5 slice_subtract_fusion
  222.6 9.6 %copy.89 = f32[1,2,1,3,8,8,512]{5,4,3,1,6,2,0:T(8,128)} copy(f32[1,2,1,3,8,8,512]{6,5,4,3,1,2,0:T(8,128)} %bitcast.149) | data formatting | bytes 1572864 | tf_op jit(solution)/shard_map/while/body/eval_jaxpr/stack | solution.py:83
  232.2 9.6 %copy.90 = f32[1,2,1,3,8,8,512]{5,4,3,1,6,2,0:T(8,128)} copy(f32[1,2,1,3,8,8,512]{6,5,4,3,1,2,0:T(8,128)} %bitcast.148) | data formatting | bytes 1572864 | tf_op jit(solution)/shard_map/while/body/eval_jaxpr/stack | solution.py:83
  241.8 17.4 %maximum_bitcast_fusion = f32[2,3,2,8,8,512]{4,3,1,0,5,2:T(8,128)} fusion(f32[1,2,1,3,8,8,512]{5,4,3,1,6,2,0:T(8,128)} %copy.90, f32[1,2,1,3,8,8,512]{5,4,3,1,6,2,0:T(8,128)} %copy.89), kind=kLoop, calls=%fused_computation.3 | loop fusion | flops 393216 | bytes 3145728 | tf_op jit(solution)/shard_map/reshape | solution.py:87
  259.2 11.8 %fusion.1 = f32[512,2,3,8,8]{4,3,2,1,0:T(8,128)} fusion(bf16[8,8,512,1,1]{1,0,4,3,2:T(8,128)(2,1)S(1)} %copy.112, f32[2,3,2,8,8,512]{4,3,1,0,5,2:T(8,128)} %maximum_bitcast_fusion), kind=kOutput, calls=%fused_computation.11 | convolution fusion | flops 18874368 | bytes 13434880 | tf_op jit(solution)/shard_map/qvabk,bnk->qvank/dot_general | solution.py:26
  270.9 11.8 %fusion = f32[512,2,3,8,8]{4,3,2,1,0:T(8,128)} fusion(bf16[8,8,512,1,1]{1,0,4,3,2:T(8,128)(2,1)S(1)} %copy-done.6, f32[2,3,2,8,8,512]{4,3,1,0,5,2:T(8,128)} %maximum_bitcast_fusion), kind=kOutput, calls=%fused_computation.10 | convolution fusion | flops 18874368 | bytes 13434880 | tf_op jit(solution)/shard_map/qvabk,bnk->qvank/dot_general | solution.py:29
  282.7 14.1 %subtract_bitcast_fusion = f32[2,3,8,8,512]{3,2,1,0,4:T(8,128)} fusion(f32[512,2,3,8,8]{4,3,2,1,0:T(8,128)} %fusion.1, bf16[8,8,512,1,1]{1,0,4,3,2:T(8,128)(2,1)S(1)} %copy-done.6, f32[2,3,2,8,8,512]{4,3,1,0,5,2:T(8,128)} %maximum_bitcast_fusion), kind=kOutput, calls=%fused_computation.9 | convolution fusion | flops 19070976 | bytes 26017792 | tf_op jit(solution)/shard_map/qvabk,bnk->qvank/dot_general | solution.py:28
  296.8 14.4 %add_bitcast_fusion = f32[2,3,8,8,512]{3,2,1,0,4:T(8,128)} fusion(f32[512,2,3,8,8]{4,3,2,1,0:T(8,128)} %fusion, bf16[8,8,512,1,1]{1,0,4,3,2:T(8,128)(2,1)S(1)} %copy.112, f32[2,3,2,8,8,512]{4,3,1,0,5,2:T(8,128)} %maximum_bitcast_fusion), kind=kOutput, calls=%fused_computation.8 | convolution fusion | flops 19070976 | bytes 26017792 | tf_op jit(solution)/shard_map/qvabk,bnk->qvank/dot_general | solution.py:31
  311.3 16.2 %fusion.6 = f32[2,512,3,8,8]{4,3,2,1,0:T(8,128)} fusion(f32[2,3,8,8,512]{3,2,1,0,4:T(8,128)} %add_bitcast_fusion, bf16[2,1,8,8,512]{3,2,4,0,1:T(8,128)(2,1)S(1)} %copy.143), kind=kOutput, calls=%fused_computation.16 | convolution fusion | flops 18874368 | bytes 1703936 | tf_op jit(solution)/shard_map/qamk,qvank->qvmnk/dot_general | solution.py:36
  327.4 15.2 %fusion.4 = f32[2,512,3,8,8]{4,3,2,1,0:T(8,128)} fusion(f32[2,3,8,8,512]{3,2,1,0,4:T(8,128)S(1)} %copy-done.2, bf16[2,1,8,8,512]{3,2,4,0,1:T(8,128)(2,1)S(1)} %copy-done.4), kind=kOutput, calls=%fused_computation.14 | convolution fusion | flops 18874368 | bytes 1703936 | tf_op jit(solution)/shard_map/qamk,qvank->qvmnk/dot_general | solution.py:37
  342.7 14.4 %fusion.12 = bf16[2,3,8,8,512]{2,3,1,4,0:T(8,128)(2,1)} fusion(f32[2,512,3,8,8]{4,3,2,1,0:T(8,128)} %fusion.6, f32[2,3,8,8,512]{3,2,1,0,4:T(8,128)S(1)} %bitcast.144, bf16[2,1,8,8,512]{3,2,4,0,1:T(8,128)(2,1)S(1)} %copy-done.4), kind=kOutput, calls=%fused_computation.22 | convolution fusion | flops 19267584 | bytes 2097152 | tf_op jit(solution)/shard_map/qamk,qvank->qvmnk/dot_general | solution.py:34
  357.1 6.8 %copy.102 = bf16[2,3,8,8,512]{4,3,2,1,0:T(8,128)(2,1)S(1)} copy(bf16[2,3,8,8,512]{2,3,1,4,0:T(8,128)(2,1)} %fusion.12) | data formatting | bytes 786432 | tf_op jit(solution)/shard_map/add | solution.py:34
  363.9 15.7 %fusion.13 = bf16[2,3,8,8,512]{2,3,1,4,0:T(8,128)(2,1)} fusion(f32[2,512,3,8,8]{4,3,2,1,0:T(8,128)} %fusion.4, f32[2,3,8,8,512]{3,2,1,0,4:T(8,128)} %subtract_bitcast_fusion, bf16[2,1,8,8,512]{3,2,4,0,1:T(8,128)(2,1)S(1)} %copy.143), kind=kOutput, calls=%fused_computation.23 | convolution fusion | flops 19267584 | bytes 2097152 | tf_op jit(solution)/shard_map/qamk,qvank->qvmnk/dot_general | solution.py:39
  379.6 6.8 %copy.105 = bf16[2,3,8,8,512]{4,3,2,1,0:T(8,128)(2,1)S(1)} copy(bf16[2,3,8,8,512]{2,3,1,4,0:T(8,128)(2,1)} %fusion.13) | data formatting | bytes 786432 | tf_op jit(solution)/shard_map/sub | solution.py:37
  386.5 0.9 copy.106
  (56 shorter events, 0.6 us)
Async XLA Ops:
  6.5 5.5 %copy-start = (f32[2,12,12]{2,0,1:T(2,128)S(1)}, f32[2,12,12]{2,0,1:T(2,128)}, u32[]{:S(2)}) copy-start(f32[2,12,12]{2,0,1:T(2,128)} %param.10) | copy-start | bytes 3460
  6.5 4.2 %copy-start.5 = (bf16[32,32,1536]{2,1,0:T(8,128)(2,1)S(1)}, bf16[32,32,1536]{2,1,0:T(8,128)(2,1)}, u32[]{:S(2)}) copy-start(bf16[32,32,1536]{2,1,0:T(8,128)(2,1)} %param.9) | copy-start | bytes 9437188
  6.5 41.0 %reduce-scatter.2.cloned.1.call-start = ((), (), s32[]{:S(2)}) async-start(), calls=%async_computation.3 | async-start | bytes 983040 | tf_op jit(solution)/shard_map/reduce_scatter | solution.py:67
  11.8 37.6 %copy-start.8 = (s32[2,512,1]{1,2,0:T(1,128)S(1)}, s32[2,512,1]{1,2,0:T(1,128)}, u32[]{:S(2)}) copy-start(s32[2,512,1]{1,2,0:T(1,128)} %param.16) | copy-start | bytes 12292
  12.1 40.2 %copy-start.11 = (s32[2,512]{1,0:T(2,128)S(1)}, s32[2,512]{1,0:T(2,128)}, u32[]{:S(2)}) copy-start(s32[2,512]{1,0:T(2,128)} %param.17) | copy-start | bytes 12292
  12.1 52.5 %copy-start.3 = (bf16[512,128]{1,0:T(8,128)(2,1)S(1)}, bf16[512,128]{1,0:T(8,128)(2,1)}, u32[]{:S(2)}) copy-start(bf16[512,128]{1,0:T(8,128)(2,1)} %param.15) | copy-start | bytes 393220
  14.6 187.6 %all-gather.2.cloned.1.call-start = ((), (), s32[]{:S(2)}) async-start(), calls=%async_computation.4 | async-start | bytes 2162688 | tf_op jit(solution)/shard_map/all_gather | solution.py:73
  57.4 15.5 %all-to-all-start = ((s32[32,2,24]{2,1,0:T(2,128)}), s32[32,2,24]{2,1,0:T(2,128)S(1)}, u32[]{:S(2)}, u32[]{:S(2)}) async-start(s32[32,2,24]{2,1,0:T(2,128)} %reshape.118), calls=%async_computation.1 | async-start | bytes 65536 | tf_op jit(solution)/shard_map/all_to_all | solution.py:99
  64.7 16.8 %copy-start.9 = (s32[3,1024]{1,0:T(4,128)S(1)}, s32[3,1024]{1,0:T(4,128)}, u32[]{:S(2)}) copy-start(s32[3,1024]{1,0:T(4,128)} %param.11) | copy-start | bytes 36868
  64.7 16.8 %copy-start.10 = (s32[3,512]{1,0:T(4,128)S(1)}, s32[3,512]{1,0:T(4,128)}, u32[]{:S(2)}) copy-start(s32[3,512]{1,0:T(4,128)} %param.14) | copy-start | bytes 18436
  77.1 14.7 %all-to-all-start.1 = ((bf16[32,2,24,128]{3,2,1,0:T(8,128)(2,1)}), bf16[32,2,24,128]{3,2,1,0:T(8,128)(2,1)S(1)}, u32[]{:S(2)}, u32[]{:S(2)}) async-start(bf16[32,2,24,128]{3,2,1,0:T(8,128)(2,1)} %bitcast.29), calls=%async_computation.2 | async-start | bytes 786432 | tf_op jit(solution)/shard_map/all_to_all | solution.py:100
  202.2 10.5 %copy-start.7 = (s32[1024,512]{1,0:T(8,128)S(1)}, s32[1024,512]{1,0:T(8,128)}, u32[]{:S(2)}) copy-start(s32[1024,512]{1,0:T(8,128)} %multiply_reduce_fusion) | copy-start | bytes 6291460
  202.2 10.5 %copy-start.12 = (bf16[1024,2,2,192]{3,0,2,1:T(8,128)(2,1)S(1)}, bf16[1024,2,2,192]{3,0,2,1:T(8,128)(2,1)}, u32[]{:S(2)}) copy-start(bf16[1024,2,2,192]{3,0,2,1:T(8,128)(2,1)} %all-gather.2.cloned.1.call-done) | copy-start | bytes 4718596
  259.2 11.8 %copy-start.6 = (bf16[8,8,512,1,1]{1,0,4,3,2:T(8,128)(2,1)S(1)}, bf16[8,8,512,1,1]{1,0,4,3,2:T(8,128)(2,1)}, u32[]{:S(2)}) copy-start(bf16[8,8,512,1,1]{1,0,4,3,2:T(8,128)(2,1)} %copy.113) | copy-start | bytes 196612
  311.2 16.2 %copy-start.2 = (f32[2,3,8,8,512]{3,2,1,0,4:T(8,128)S(1)}, f32[2,3,8,8,512]{3,2,1,0,4:T(8,128)}, u32[]{:S(2)}) copy-start(f32[2,3,8,8,512]{3,2,1,0,4:T(8,128)} %add_bitcast_fusion) | copy-start | bytes 2359300
  311.2 16.2 %copy-start.4 = (bf16[2,1,8,8,512]{3,2,4,0,1:T(8,128)(2,1)S(1)}, bf16[2,1,8,8,512]{3,2,4,0,1:T(8,128)(2,1)}, u32[]{:S(2)}) copy-start(bf16[2,1,8,8,512]{3,2,4,0,1:T(8,128)(2,1)} %copy.142) | copy-start | bytes 393220
  311.2 31.4 %slice-start = ((s8[12582912]{0:T(1024)(128)(4,1)}), s8[4194304]{0:T(1024)(128)(4,1)S(1)}, s32[]{:S(2)}) async-start(s8[12582912]{0:T(1024)(128)(4,1)} %bitcast.143), calls=%async_computation.5 | async-start | bytes 8388608
  311.2 31.4 %slice-start.1 = ((s8[12582912]{0:T(1024)(128)(4,1)}), s8[4194304]{0:T(1024)(128)(4,1)S(1)}, s32[]{:S(2)}) async-start(s8[12582912]{0:T(1024)(128)(4,1)} %bitcast.143), calls=%async_computation.6 | async-start | bytes 8388608
  327.4 15.2 %slice-start.2 = ((s8[12582912]{0:T(1024)(128)(4,1)}), s8[4194304]{0:T(1024)(128)(4,1)S(1)}, s32[]{:S(2)}) async-start(s8[12582912]{0:T(1024)(128)(4,1)} %bitcast.143), calls=%async_computation.7 | async-start | bytes 8388608
  379.6 7.8 %copy-start.1 = (f32[2,12,12]{2,0,1:T(2,128)S(1)}, f32[2,12,12]{2,0,1:T(2,128)}, u32[]{:S(2)}) copy-start(f32[2,12,12]{2,0,1:T(2,128)} %param.10) | copy-start | bytes 3460
Sparse Core Ops, SparseCore 0:
  14.7 32.7 reduce-scatter.1
  49.5 152.6 all-gather.1
where the time goes:
time: 401 us; the launch traced here: 395 us
  waiting for transfers between devices  150 us (37%)
  matrix products  137 us (34%)
  local copies, waits for them, and re-layouts  56.8 us (14%)
  other arithmetic  25.5 us (6%)
  between operations  14.2 us (4%)
  starting transfers between devices  11.6 us (3%)
    all_gather x1, waiting for transfers between devices, local(): shard_piece = lax.all_gather(coupling_q, 're', axis=0, tiled=True)  103 us
    reduce_scatter x1, waiting for transfers between devices, local(): owned = lax.psum_scatter(mixed, 'rp', scatter_dimension=3, tiled=True)  32.9 us
    another operation x2, local copies, waits for them, and re-layouts, one_block(): jnp.stack([part_cos[:, 0] - part_sin[:, 1], part_sin[:, 0] + part_cos[:,...  19.2 us
    reshape x1, other arithmetic, local(): coupling.transpose(1, 3, 2, 4, 5, 0, 6)  17.4 us
    dot_general x1, matrix products, rotate(): jnp.einsum('qamk,qvank->qvmnk', left_imag, half_imag, precision=highest)  16.2 us
    dot_general x1, matrix products, rotate(): jnp.einsum('qamk,qvank->qvmnk', left_imag, half_real, precision=highest)  15.7 us
    dot_general x1, matrix products, rotate(): jnp.einsum('qamk,qvank->qvmnk', left_real, half_imag, precision=highest)  15.2 us
    dot_general x1, matrix products, rotate(): jnp.einsum('qamk,qvank->qvmnk', left_real, half_real, precision=highest)  14.4 us
  transfers between devices with their start and end apart: 4, of which 4 were waited for; matrix products, arithmetic and copies ran while one was open for 6% of the time, Pallas kernels for 0%

commit v1 on v0

v1 whole, which is shorter than its diff:
```python
import functools
import math

import jax
import jax.numpy as jnp
from jax import lax
from jax.experimental import pallas as pl
from jax.experimental.pallas import tpu as pltpu
from jax.sharding import PartitionSpec as P

NB = 8
MODES = 12
Q = 2
GRID = 64
RE = 1024
RE_LOCAL = 32
RP_LOCAL = 32
K = 512
N_RE = 32
N_RP = 4
M_LOCAL = MODES // N_RP
CAP = 24
SLOTS = Q * CAP
ROWS = Q * M_LOCAL * RE_LOCAL
PACK = ROWS + SLOTS
LANES = 128
TURN = 2.0 * math.pi
SINE = [TURN ** n * s / math.factorial(n) for n, s in ((1, 1), (3, -1), (5, 1), (7, -1), (9, 1), (11, -1))]
BF = jnp.bfloat16
F32 = jnp.float32
I32 = jnp.int32


def sine_poly(t):
    s = t * t
    value = jnp.full_like(s, SINE[-1])
    for c in SINE[-2::-1]:
        value = value * s + c
    return value * t


def cos_sin(products):
    turns = products * (1.0 / GRID)
    frac = turns - jnp.floor(turns + 0.5)
    size = jnp.abs(frac)
    shifted = 0.25 - size
    cosine = sine_poly(shifted)
    folded = 0.25 - jnp.abs(shifted)
    sine = sine_poly(jnp.where(frac < 0.0, -folded, folded))
    return cosine, sine


def requests_kernel(owner_ref, row_ref, request_ref, slot_ref):
    before = (lax.broadcasted_iota(I32, (K, K), 0) < lax.broadcasted_iota(I32, (K, K), 1)).astype(F32).astype(BF)
    total = jnp.zeros((N_RE, LANES), F32)
    for q in range(Q):
        owner = owner_ref[q : q + 1, :]
        row = row_ref[q : q + 1, :]
        hit = lax.broadcasted_iota(I32, (N_RE, K), 0) == owner
        one_hot = hit.astype(F32)
        earlier = jnp.dot(one_hot.astype(BF), before, preferred_element_type=F32)
        rank = jnp.sum(one_hot * earlier, axis=0, keepdims=True).astype(I32) + q * CAP
        slot_ref[q : q + 1, :] = owner * SLOTS + rank
        place = (lax.broadcasted_iota(I32, (LANES, K), 0) == rank).astype(F32).astype(BF)
        high = (one_hot * (row >> 4).astype(F32)).astype(BF)
        low = (one_hot * (row & 15).astype(F32)).astype(BF)
        contract = (((1,), (1,)), ((), ()))
        total += 16.0 * lax.dot_general(high, place, contract, preferred_element_type=F32)
        total += lax.dot_general(low, place, contract, preferred_element_type=F32)
    total = total.astype(I32)
    for o in range(N_RE):
        request_ref[o] = jnp.broadcast_to(total[o : o + 1, :], (8, LANES))


def mix_kernel(mode_ref, q_ref, rank_ref, rp_ref, table_ref, *out_refs):
    group = 8
    width = group * RP_LOCAL
    coords = rp_ref[...]
    lane_group = lax.broadcasted_iota(I32, (group, width), 1) // RP_LOCAL
    own = lane_group == lax.broadcasted_iota(I32, (group, width), 0)
    cosines, sines = [], []
    for q in range(Q):
        products = sum(q_ref[d, q] * coords[d : d + 1, :] for d in range(3)).astype(F32)
        cosine, sine = cos_sin(jnp.broadcast_to(products, (group, width)))
        cosines.append(jnp.where(own, cosine, 0.0))
        sines.append(jnp.where(own, sine, 0.0))
    left = jnp.concatenate(cosines + sines, axis=0).astype(BF)
    half = MODES * NB * NB
    low_lanes = lax.broadcasted_iota(I32, (group, LANES), 1) < LANES // 2
    rank = rank_ref[0]
    parts = [[[] for _ in range(Q * M_LOCAL)] for _ in range(N_RP)]
    for h in range(table_ref.shape[0] // group):
        values = table_ref[h * group : (h + 1) * group].reshape(width, 2 * half)
        sums = jnp.dot(left, values, preferred_element_type=F32)
        for q in range(Q):
            with_cos = sums[q * group : (q + 1) * group]
            with_sin = sums[(Q + q) * group : (Q + q + 1) * group]
            packed = []
            for p in range(MODES // 2):
                re_lanes = slice(p * LANES, (p + 1) * LANES)
                im_lanes = slice(half + p * LANES, half + (p + 1) * LANES)
                real = with_cos[:, re_lanes] - with_sin[:, im_lanes]
                imag = with_sin[:, re_lanes] + with_cos[:, im_lanes]
                packed.append(jnp.where(low_lanes, real, pltpu.roll(imag, LANES // 2, 1)))
                packed.append(jnp.where(low_lanes, pltpu.roll(real, LANES // 2, 1), imag))
            for s in range(N_RP):
                first = (rank ^ s) * M_LOCAL
                for n in range(M_LOCAL):
                    value = mode_ref[q, 0, first + n] * packed[0]
                    for mu in range(1, MODES):
                        value += mode_ref[q, mu, first + n] * packed[mu]
                    parts[s][q * M_LOCAL + n].append(value)
    for s in range(N_RP):
        for i in range(Q * M_LOCAL):
            out_refs[s][i] = jnp.concatenate(parts[s][i], axis=0).astype(BF)


def pack_kernel(own_ref, one_ref, two_ref, three_ref, request_ref, rotations_ref, out_ref):
    total = own_ref[...].astype(F32) + one_ref[...].astype(F32)
    total += two_ref[...].astype(F32) + three_ref[...].astype(F32)
    total = total.astype(BF)
    peers = out_ref.shape[0]
    wanted = request_ref[:, 0, :].T
    rows = lax.broadcasted_iota(I32, (SLOTS, K), 1)
    rotations = rotations_ref[...]
    for p in range(peers):
        out_ref[p, :ROWS, :] = total
        one_hot = (wanted[:SLOTS, p : p + 1] == rows).astype(F32).astype(BF)
        found = jnp.dot(one_hot, rotations, preferred_element_type=F32)
        out_ref[p, ROWS:, :] = found.astype(BF)


def phase_kernel(re_ref, k_ref, cos_ref, sin_ref):
    left = re_ref[...].astype(F32).astype(BF)
    right = k_ref[...].astype(F32).astype(BF)
    products = lax.dot_general(left, right, (((0,), (0,)), ((), ())), preferred_element_type=F32)
    cosine, sine = cos_sin(products)
    cos_ref[...] = cosine.astype(BF)
    sin_ref[...] = sine.astype(BF)


def final_kernel(slot_ref, rotations_ref, cos_ref, sin_ref, reply_ref, block_ref, out_ref, far_ref, near_ref, coupling_ref):
    step = pl.program_id(0)
    size = NB * NB

    @pl.when(step == 0)
    def _():
        near_ref[...] = rotations_ref[...].astype(F32).T
        replies = reply_ref[...].reshape(N_RE * SLOTS, LANES)
        for q in range(Q):
            slots = lax.broadcasted_iota(I32, (N_RE * SLOTS, K), 0)
            one_hot = (slots == slot_ref[q : q + 1, :]).astype(F32).astype(BF)
            far_ref[q] = lax.dot_general(replies, one_hot, (((0,), (0,)), ((), ())), preferred_element_type=F32)

    block = block_ref[...].reshape(RE, LANES)
    contract = (((0,), (0,)), ((), ()))
    with_cos = lax.dot_general(block, cos_ref[...], contract, preferred_element_type=F32)
    with_sin = lax.dot_general(block, sin_ref[...], contract, preferred_element_type=F32)
    coupling_ref[0:size] = with_cos[0:size] - with_sin[size:]
    coupling_ref[size:] = with_sin[0:size] + with_cos[size:]
    q = step // M_LOCAL
    for t in range(K // LANES):
        lanes = slice(t * LANES, (t + 1) * LANES)
        u_re = [near_ref[b * NB : (b + 1) * NB, lanes] for b in range(NB)]
        u_im = [near_ref[size + b * NB : size + (b + 1) * NB, lanes] for b in range(NB)]
        h_re, h_im = [], []
        for a in range(NB):
            acc_re = acc_im = None
            for b in range(NB):
                row = a * NB + b
                c_re = coupling_ref[row : row + 1, lanes]
                c_im = coupling_ref[size + row : size + row + 1, lanes]
                add_re = c_re * u_re[b] - c_im * u_im[b]
                add_im = c_re * u_im[b] + c_im * u_re[b]
                acc_re = add_re if acc_re is None else acc_re + add_re
                acc_im = add_im if acc_im is None else acc_im + add_im
            h_re.append(acc_re)
            h_im.append(acc_im)
        for pair in range(NB // 2):
            real, imag = [], []
            for m in (2 * pair, 2 * pair + 1):
                acc_re = acc_im = None
                for a in range(NB):
                    row = a * NB + m
                    v_re = far_ref[q, row : row + 1, lanes]
                    v_im = far_ref[q, size + row : size + row + 1, lanes]
                    add_re = v_re * h_re[a] + v_im * h_im[a]
                    add_im = v_re * h_im[a] - v_im * h_re[a]
                    acc_re = add_re if acc_re is None else acc_re + add_re
                    acc_im = add_im if acc_im is None else acc_im + add_im
                real.append(acc_re)
                imag.append(acc_im)
            rows = slice(pair * 16, pair * 16 + 16)
            out_ref[0, 0, rows, lanes] = jnp.concatenate(real, axis=0).astype(BF)
            out_ref[0, 1, rows, lanes] = jnp.concatenate(imag, axis=0).astype(BF)


def whole(shape):
    return pl.BlockSpec(shape, lambda *_: (0,) * len(shape))


def smem():
    return pl.BlockSpec(memory_space=pltpu.SMEM)


def params():
    return pltpu.CompilerParams(vmem_limit_bytes=48 << 20)


def local(
    wannier_table,
    mode_matrix,
    re_coords,
    rp_coords,
    q_coords,
    k_coords,
    rotations,
    kq_owner,
    kq_row,
):
    requests, slots = pl.pallas_call(
        requests_kernel,
        out_shape=(
            jax.ShapeDtypeStruct((N_RE, 8, LANES), I32),
            jax.ShapeDtypeStruct((Q, K), I32),
        ),
        compiler_params=params(),
        name="requests",
    )(kq_owner.reshape(Q, K), kq_row)
    wanted = lax.all_to_all(requests, "re", split_axis=0, concat_axis=0, tiled=True)

    chunk = 16
    block = (Q * M_LOCAL, chunk, LANES)
    parts = pl.pallas_call(
        mix_kernel,
        grid=(RE_LOCAL // chunk,),
        in_specs=[
            smem(),
            smem(),
            smem(),
            whole((3, 8 * RP_LOCAL)),
            pl.BlockSpec((chunk, RP_LOCAL, 2 * MODES * NB * NB), lambda i: (i, 0, 0)),
        ],
        out_specs=[pl.BlockSpec(block, lambda i: (0, i, 0))] * N_RP,
        out_shape=[jax.ShapeDtypeStruct((Q * M_LOCAL, RE_LOCAL, LANES), BF)] * N_RP,
        compiler_params=params(),
        name="mix",
    )(
        mode_matrix,
        q_coords,
        lax.axis_index("rp").reshape(1),
        jnp.tile(rp_coords, (1, 8)),
        wannier_table,
    )
    own = parts[0].reshape(ROWS, LANES)
    others = [
        lax.ppermute(parts[s].reshape(ROWS, LANES), "rp", [(j, j ^ s) for j in range(N_RP)])
        for s in range(1, N_RP)
    ]

    peers = 8
    packed = pl.pallas_call(
        pack_kernel,
        grid=(N_RE // peers,),
        in_specs=[whole((ROWS, LANES))] * N_RP
        + [pl.BlockSpec((peers, 8, LANES), lambda i: (i, 0, 0)), whole((K, LANES))],
        out_specs=pl.BlockSpec((peers, PACK, LANES), lambda i: (i, 0, 0)),
        out_shape=jax.ShapeDtypeStruct((N_RE, PACK, LANES), BF),
        compiler_params=params(),
        name="pack",
    )(own, *others, wanted, rotations)
    gathered = lax.all_to_all(packed, "re", split_axis=0, concat_axis=0, tiled=True)

    cosine, sine = pl.pallas_call(
        phase_kernel,
        grid=(4,),
        in_specs=[pl.BlockSpec((3, RE // 4), lambda i: (0, i)), whole((3, K))],
        out_specs=[pl.BlockSpec((RE // 4, K), lambda i: (i, 0))] * 2,
        out_shape=[jax.ShapeDtypeStruct((RE, K), BF)] * 2,
        compiler_params=params(),
        name="phase",
    )(re_coords, k_coords)

    result = pl.pallas_call(
        final_kernel,
        grid=(Q * M_LOCAL,),
        in_specs=[
            whole((Q, K)),
            whole((K, LANES)),
            whole((RE, K)),
            whole((RE, K)),
            pl.BlockSpec((N_RE, SLOTS, LANES), lambda i: (0, ROWS // SLOTS, 0)),
            pl.BlockSpec((N_RE, RE_LOCAL, LANES), lambda i: (0, i, 0)),
        ],
        out_specs=pl.BlockSpec((1, 2, NB * NB, K), lambda i: (i, 0, 0, 0)),
        out_shape=jax.ShapeDtypeStruct((Q * M_LOCAL, 2, NB * NB, K), BF),
        scratch_shapes=[
            pltpu.VMEM((Q, LANES, K), F32),
            pltpu.VMEM((LANES, K), F32),
            pltpu.VMEM((LANES, K), F32),
        ],
        compiler_params=params(),
        name="final",
    )(slots, rotations, cosine, sine, gathered, gathered)
    return result.reshape(Q, M_LOCAL, 2, NB * NB, K)


def solution(mesh):
    in_specs = (
        P("re", "rp", None),
        P(),
        P(),
        P(None, "rp"),
        P(),
        P(None, "re"),
        P("re", None),
        P(None, "re", None),
        P(None, "re"),
    )
    out_specs = P(None, "rp", None, None, "re")
    return jax.shard_map(local, mesh=mesh, in_specs=in_specs, out_specs=out_specs, check_vma=False)
```

time: 401 us -> 77.4 us (0.19); the launches traced: 395 us -> 76.9 us
  matrix products: 137 us -> 0 us
  waiting for transfers between devices: 150 us -> 29.5 us
  local copies, waits for them, and re-layouts: 56.8 us -> 9.04 us
  other arithmetic: 25.5 us -> 0 us
  Pallas kernels: 0 us -> 17.9 us
  between operations: 14.2 us -> 0.1 us
  starting transfers between devices: 11.6 us -> 20.4 us
    dot_general x13 -> x0, matrix products: 137 us -> none  [the longest x1 16.2 us: rotate(): jnp.einsum('qamk,qvank->qvmnk', left_imag, half_imag, precision=highest)]
    all_gather x1 -> x0, waiting for transfers between devices: 103 us -> none  [local(): shard_piece = lax.all_gather(coupling_q, 're', axis=0, tiled=True)]
    reduce_scatter x1 -> x0, waiting for transfers between devices: 32.9 us -> none  [local(): owned = lax.psum_scatter(mixed, 'rp', scatter_dimension=3, tiled=True)]
    another operation x7 -> x2, local copies, waits for them, and re-layouts: 21 us -> 0.76 us  [local(): jnp.tile(rp_coords, (1, 8))]
    pallas_call x0 -> x5, Pallas kernels: none -> 17.9 us  [the longest x1 9.14 us: local(): pl.pallas_call(final_kernel, grid=(Q * M_LOCAL,), in_specs=[whole((Q, K))...]
    reshape x1 -> x0, other arithmetic: 17.4 us -> none  [local(): coupling.transpose(1, 3, 2, 4, 5, 0, 6)]
    all_to_all x1, waiting for transfers between devices: 8.24 us -> 24.4 us  [local(): lax.all_to_all(packed, 're', split_axis=0, concat_axis=0, tiled=True)]
    gather x2 -> x0, local copies, waits for them, and re-layouts: 7.27 us -> none  [the longest x1 4.07 us: local(): rotations[lax.all_to_all(requests, 're', split_axis=0, concat_axis=0, til...]
  transfers between devices with their start and end apart: 4 -> 5, of which waited for: 4 -> 3; matrix products, arithmetic and copies ran while one was open for 6% -> 3% of each run, Pallas kernels for 0% -> 7%
where the time goes in v1:
time: 77.4 us; the launch traced here: 76.9 us
  waiting for transfers between devices  29.5 us (38%)
  starting transfers between devices  20.4 us (26%)
  Pallas kernels  17.9 us (23%)
  local copies, waits for them, and re-layouts  9.04 us (12%)
    all_to_all x1, waiting for transfers between devices, local(): lax.all_to_all(packed, 're', split_axis=0, concat_axis=0, tiled=True)  24.4 us
    pallas_call x1, Pallas kernels, local(): pl.pallas_call(final_kernel, grid=(Q * M_LOCAL,), in_specs=[whole((Q, K))...  9.14 us
    all_to_all x1, starting transfers between devices, local(): lax.all_to_all(requests, 're', split_axis=0, concat_axis=0, tiled=True)  8.76 us
    unnamed x19, local copies, waits for them, and re-layouts  8.28 us
    all_to_all x1, starting transfers between devices, local(): lax.all_to_all(packed, 're', split_axis=0, concat_axis=0, tiled=True)  7.8 us
    ppermute x3, waiting for transfers between devices, local(): lax.ppermute(parts[s].reshape(ROWS, LANES), 'rp', [(j, j ^ s) for j in ra...  5.15 us
    ppermute x3, starting transfers between devices, local(): lax.ppermute(parts[s].reshape(ROWS, LANES), 'rp', [(j, j ^ s) for j in ra...  3.8 us
    pallas_call x1, Pallas kernels, local(): pl.pallas_call(phase_kernel, grid=(4,), in_specs=[pl.BlockSpec((3, RE //...  3.23 us
  transfers between devices with their start and end apart: 5, of which 3 were waited for; matrix products, arithmetic and copies ran while one was open for 3% of the time, Pallas kernels for 7%

profile of v1, /device:TPU:0, one launch (start us, length us, event | category | flops | bytes accessed | tf_op | source)
XLA Modules:
  0.0 76.9 jit_solution(5908372537677698106)
XLA Ops:
  0.0 0.0 copy-start.4
  0.0 0.7 copy.14
  0.7 0.0 copy-start.7
  0.7 0.7 copy-done.7
  1.4 1.3 %requests.1 = (s32[32,8,128]{2,1,0:T(8,128)}, s32[2,512]{1,0:T(2,128)S(1)}) custom-call(s32[2,512]{1,0:T(2,128)S(1)} %bitcast.10, s32[2,512]{1,0:T(2,128)S(1)} %copy-done.7), custom_call_target="tpu_custom_call" | custom-call | tf_op jit(solution)/shard_map/requests/pallas_call | solution.py:221
  2.7 8.8 %all-to-all-start = ((s32[32,8,128]{2,1,0:T(8,128)}), s32[32,8,128]{2,1,0:T(8,128)S(1)}, u32[]{:S(2)}, u32[]{:S(2)}) async-start(s32[32,8,128]{2,1,0:T(8,128)} %get-tuple-element.20), calls=%async_computation | async-start | bytes 262144 | tf_op jit(solution)/shard_map/all_to_all | solution.py:230
  11.5 0.8 copy.11.q_ref
  12.3 0.7 tile.4
  12.9 0.1 tile.10.rp_ref
  13.0 0.7 copy.10.mode_ref
  13.7 0.0 copy-start.1
  13.7 1.9 %copy-done.1 = bf16[32,32,1536]{2,1,0:T(8,128)(2,1)S(1)} copy-done((bf16[32,32,1536]{2,1,0:T(8,128)(2,1)S(1)}, bf16[32,32,1536]{2,1,0:T(8,128)(2,1)}, u32[]{:S(2)}) %copy-start.1) | copy-done | bytes 3145752
  15.6 2.5 %mix.1 = (bf16[6,32,128]{2,1,0:T(8,128)(2,1)S(1)}, bf16[6,32,128]{2,1,0:T(8,128)(2,1)S(1)}, bf16[6,32,128]{2,1,0:T(8,128)(2,1)S(1)}, bf16[6,32,128]{2,1,0:T(8,128)(2,1)S(1)}) custom-call(f32[2,12,12]{2,1,0:T(8,128)S(1)} %copy.10.mode_ref, s32[3,2]{1,0:T(4,128)S(1)} %copy.11.q_ref, s32[1]{0:T(128)} %bitcast.rank_ref, s32[3,256]{1,0:T(4,128)S(1)} %tile.10.rp_ref, ...), custom_call_target="tpu_custom_call" | custom-call | tf_op jit(solution)/shard_map/mix/pallas_call | solution.py:234
  18.1 0.1 collective-permute-start
  18.2 3.7 %collective-permute-start.1 = (bf16[192,128]{1,0:T(8,128)(2,1)S(1)}, bf16[192,128]{1,0:T(8,128)(2,1)S(1)}, u32[]{:S(2)}, u32[]{:S(2)}) collective-permute-start(bf16[192,128]{1,0:T(8,128)(2,1)S(1)} %bitcast.12), channel_id=1, source_target_pairs={{0,2},{1,3},{2,0},{3,1},{4,6},{5,7},{6,4},{7,5},{8,10},{9,11},{10,... | collective-permute-start | bytes 147464 | tf_op jit(solution)/shard_map/ppermute | solution.py:257
  21.9 0.1 collective-permute-start.2
  21.9 0.0 collective-permute-done.one_ref
  21.9 2.3 %collective-permute-done.1.two_ref = bf16[192,128]{1,0:T(8,128)(2,1)S(1)} collective-permute-done((bf16[192,128]{1,0:T(8,128)(2,1)S(1)}, bf16[192,128]{1,0:T(8,128)(2,1)S(1)}, u32[]{:S(2)}, u32[]{:S(2)}) %collective-permute-start.1) | collective-permute-done | bytes 49184 | tf_op jit(solution)/shard_map/ppermute | solution.py:257
  24.2 2.9 %collective-permute-done.2.three_ref = bf16[192,128]{1,0:T(8,128)(2,1)S(1)} collective-permute-done((bf16[192,128]{1,0:T(8,128)(2,1)S(1)}, bf16[192,128]{1,0:T(8,128)(2,1)S(1)}, u32[]{:S(2)}, u32[]{:S(2)}) %collective-permute-start.2) | collective-permute-done | bytes 49184 | tf_op jit(solution)/shard_map/ppermute | solution.py:257
  27.1 0.0 all-to-all-done.request_ref
  27.1 0.0 copy-done.4
  27.1 1.8 %pack.1 = bf16[32,240,128]{2,1,0:T(8,128)(2,1)S(1)} custom-call(bf16[192,128]{1,0:T(8,128)(2,1)S(1)} %bitcast.9, bf16[192,128]{1,0:T(8,128)(2,1)S(1)} %collective-permute-done.one_ref, bf16[192,128]{1,0:T(8,128)(2,1)S(1)} %collective-permute-done.1.two_ref, bf16[192,128]{1,0:T(8,128)(2,1)S(1)} %collective-permute-done.2.three_ref, ...), custom_call_target="tpu_custom_call" | custom-call | tf_op jit(solution)/shard_map/pack/pallas_call | solution.py:262
  28.9 0.0 copy-start
  28.9 1.3 %copy-done = bf16[32,240,128]{2,1,0:T(8,128)(2,1)} copy-done((bf16[32,240,128]{2,1,0:T(8,128)(2,1)}, bf16[32,240,128]{2,1,0:T(8,128)(2,1)S(1)}, u32[]{:S(2)}) %copy-start) | copy-done | bytes 1966104
  30.2 0.0 copy-start.5
  30.2 0.0 copy-start.6
  30.2 7.8 %all-to-all-start.1 = ((bf16[32,240,128]{2,1,0:T(8,128)(2,1)}), bf16[32,240,128]{2,1,0:T(8,128)(2,1)S(1)}, u32[]{:S(2)}, u32[]{:S(2)}) async-start(bf16[32,240,128]{2,1,0:T(8,128)(2,1)} %copy-done), calls=%async_computation.1 | async-start | bytes 3932160 | tf_op jit(solution)/shard_map/all_to_all | solution.py:272
  38.0 0.0 copy-done.5
  38.0 0.0 copy-done.6
  38.0 3.2 %phase.1 = (bf16[1024,512]{1,0:T(8,128)(2,1)S(1)}, bf16[1024,512]{1,0:T(8,128)(2,1)S(1)}) custom-call(s32[3,1024]{1,0:T(4,128)S(1)} %copy-done.5, s32[3,512]{1,0:T(4,128)S(1)} %copy-done.6), custom_call_target="tpu_custom_call" | custom-call | tf_op jit(solution)/shard_map/phase/pallas_call | solution.py:274
  41.2 0.0 copy-start.2
  41.2 1.0 %copy-done.2 = bf16[1024,512]{1,0:T(8,128)(2,1)} copy-done((bf16[1024,512]{1,0:T(8,128)(2,1)}, bf16[1024,512]{1,0:T(8,128)(2,1)S(1)}, u32[]{:S(2)}) %copy-start.2) | copy-done | bytes 1048600
  42.2 24.4 %all-to-all-done.1.reply_ref.block_ref = bf16[32,240,128]{2,1,0:T(8,128)(2,1)S(1)} async-done(((bf16[32,240,128]{2,1,0:T(8,128)(2,1)}), bf16[32,240,128]{2,1,0:T(8,128)(2,1)S(1)}, u32[]{:S(2)}, u32[]{:S(2)}) %all-to-all-start.1) | async-done | bytes 1966112 | tf_op jit(solution)/shard_map/all_to_all | solution.py:272
  66.6 0.0 copy-start.3
  66.6 1.2 %copy-done.3 = bf16[1024,512]{1,0:T(8,128)(2,1)S(1)} copy-done((bf16[1024,512]{1,0:T(8,128)(2,1)S(1)}, bf16[1024,512]{1,0:T(8,128)(2,1)}, u32[]{:S(2)}) %copy-start.3) | copy-done | bytes 1048600
  67.8 9.1 %final.1 = bf16[6,2,64,512]{3,2,1,0:T(8,128)(2,1)} custom-call(s32[2,512]{1,0:T(2,128)S(1)} %get-tuple-element.13.slot_ref, bf16[512,128]{1,0:T(8,128)(2,1)S(1)} %copy-done.4, bf16[1024,512]{1,0:T(8,128)(2,1)S(1)} %get-tuple-element.14.cos_ref, bf16[1024,512]{1,0:T(8,128)(2,1)S(1)} %copy-done.3, ...), custom_call_target="tpu_custom_call" | custom-call | tf_op jit(solution)/shard_map/final/pallas_call | solution.py:284
Async XLA Ops:
  0.0 27.1 %copy-start.4 = (bf16[512,128]{1,0:T(8,128)(2,1)S(1)}, bf16[512,128]{1,0:T(8,128)(2,1)}, u32[]{:S(2)}) copy-start(bf16[512,128]{1,0:T(8,128)(2,1)} %rotations_ref.3) | copy-start | bytes 393220
  0.7 0.7 copy-start.7
  2.7 24.4 %all-to-all-start = ((s32[32,8,128]{2,1,0:T(8,128)}), s32[32,8,128]{2,1,0:T(8,128)S(1)}, u32[]{:S(2)}, u32[]{:S(2)}) async-start(s32[32,8,128]{2,1,0:T(8,128)} %get-tuple-element.20), calls=%async_computation | async-start | bytes 262144 | tf_op jit(solution)/shard_map/all_to_all | solution.py:230
  13.7 1.9 %copy-start.1 = (bf16[32,32,1536]{2,1,0:T(8,128)(2,1)S(1)}, bf16[32,32,1536]{2,1,0:T(8,128)(2,1)}, u32[]{:S(2)}) copy-start(bf16[32,32,1536]{2,1,0:T(8,128)(2,1)} %table_ref.1) | copy-start | bytes 9437188
  18.1 3.8 %collective-permute-start = (bf16[192,128]{1,0:T(8,128)(2,1)S(1)}, bf16[192,128]{1,0:T(8,128)(2,1)S(1)}, u32[]{:S(2)}, u32[]{:S(2)}) collective-permute-start(bf16[192,128]{1,0:T(8,128)(2,1)S(1)} %bitcast.13), channel_id=1, source_target_pairs={{0,1},{1,0},{2,3},{3,2},{4,5},{5,4},{6,7},{7,6},{8,9},{9,8},{10,11... | collective-permute-start | bytes 147464 | tf_op jit(solution)/shard_map/ppermute | solution.py:257
  18.2 6.0 %collective-permute-start.1 = (bf16[192,128]{1,0:T(8,128)(2,1)S(1)}, bf16[192,128]{1,0:T(8,128)(2,1)S(1)}, u32[]{:S(2)}, u32[]{:S(2)}) collective-permute-start(bf16[192,128]{1,0:T(8,128)(2,1)S(1)} %bitcast.12), channel_id=1, source_target_pairs={{0,2},{1,3},{2,0},{3,1},{4,6},{5,7},{6,4},{7,5},{8,10},{9,11},{10,... | collective-permute-start | bytes 147464 | tf_op jit(solution)/shard_map/ppermute | solution.py:257
  21.9 5.2 %collective-permute-start.2 = (bf16[192,128]{1,0:T(8,128)(2,1)S(1)}, bf16[192,128]{1,0:T(8,128)(2,1)S(1)}, u32[]{:S(2)}, u32[]{:S(2)}) collective-permute-start(bf16[192,128]{1,0:T(8,128)(2,1)S(1)} %bitcast.11), channel_id=1, source_target_pairs={{0,3},{1,2},{2,1},{3,0},{4,7},{5,6},{6,5},{7,4},{8,11},{9,10},{10,... | collective-permute-start | bytes 147464 | tf_op jit(solution)/shard_map/ppermute | solution.py:257
  28.9 1.3 %copy-start = (bf16[32,240,128]{2,1,0:T(8,128)(2,1)}, bf16[32,240,128]{2,1,0:T(8,128)(2,1)S(1)}, u32[]{:S(2)}) copy-start(bf16[32,240,128]{2,1,0:T(8,128)(2,1)S(1)} %pack.1) | copy-start | bytes 5898244
  30.2 7.8 %copy-start.5 = (s32[3,1024]{1,0:T(4,128)S(1)}, s32[3,1024]{1,0:T(4,128)}, u32[]{:S(2)}) copy-start(s32[3,1024]{1,0:T(4,128)} %re_ref.1) | copy-start | bytes 36868
  30.2 7.8 %copy-start.6 = (s32[3,512]{1,0:T(4,128)S(1)}, s32[3,512]{1,0:T(4,128)}, u32[]{:S(2)}) copy-start(s32[3,512]{1,0:T(4,128)} %k_ref.1) | copy-start | bytes 18436
  30.2 36.4 %all-to-all-start.1 = ((bf16[32,240,128]{2,1,0:T(8,128)(2,1)}), bf16[32,240,128]{2,1,0:T(8,128)(2,1)S(1)}, u32[]{:S(2)}, u32[]{:S(2)}) async-start(bf16[32,240,128]{2,1,0:T(8,128)(2,1)} %copy-done), calls=%async_computation.1 | async-start | bytes 3932160 | tf_op jit(solution)/shard_map/all_to_all | solution.py:272
  41.2 1.0 %copy-start.2 = (bf16[1024,512]{1,0:T(8,128)(2,1)}, bf16[1024,512]{1,0:T(8,128)(2,1)S(1)}, u32[]{:S(2)}) copy-start(bf16[1024,512]{1,0:T(8,128)(2,1)S(1)} %get-tuple-element.15.sin_ref) | copy-start | bytes 3145732
  66.6 1.2 %copy-start.3 = (bf16[1024,512]{1,0:T(8,128)(2,1)S(1)}, bf16[1024,512]{1,0:T(8,128)(2,1)}, u32[]{:S(2)}) copy-start(bf16[1024,512]{1,0:T(8,128)(2,1)} %copy-done.2) | copy-start | bytes 3145732

commit v2 on v1

--- a/solution.py
+++ b/solution.py
@@ -1,4 +1,3 @@
-import functools
 import math
 
 import jax
@@ -54,7 +53,7 @@
     before = (lax.broadcasted_iota(I32, (K, K), 0) < lax.broadcasted_iota(I32, (K, K), 1)).astype(F32).astype(BF)
     total = jnp.zeros((N_RE, LANES), F32)
     for q in range(Q):
-        owner = owner_ref[q : q + 1, :]
+        owner = owner_ref[q]
         row = row_ref[q : q + 1, :]
         hit = lax.broadcasted_iota(I32, (N_RE, K), 0) == owner
         one_hot = hit.astype(F32)
@@ -75,12 +74,12 @@
 def mix_kernel(mode_ref, q_ref, rank_ref, rp_ref, table_ref, *out_refs):
     group = 8
     width = group * RP_LOCAL
-    coords = rp_ref[...]
+    coords = jnp.concatenate([rp_ref[...]] * group, axis=1)
     lane_group = lax.broadcasted_iota(I32, (group, width), 1) // RP_LOCAL
     own = lane_group == lax.broadcasted_iota(I32, (group, width), 0)
     cosines, sines = [], []
     for q in range(Q):
-        products = sum(q_ref[d, q] * coords[d : d + 1, :] for d in range(3)).astype(F32)
+        products = sum(q_ref[q, d] * coords[d : d + 1, :] for d in range(3)).astype(F32)
         cosine, sine = cos_sin(jnp.broadcast_to(products, (group, width)))
         cosines.append(jnp.where(own, cosine, 0.0))
         sines.append(jnp.where(own, sine, 0.0))
@@ -106,9 +105,9 @@
             for s in range(N_RP):
                 first = (rank ^ s) * M_LOCAL
                 for n in range(M_LOCAL):
-                    value = mode_ref[q, 0, first + n] * packed[0]
+                    value = mode_ref[0, q, first + n] * packed[0]
                     for mu in range(1, MODES):
-                        value += mode_ref[q, mu, first + n] * packed[mu]
+                        value += mode_ref[mu, q, first + n] * packed[mu]
                     parts[s][q * M_LOCAL + n].append(value)
     for s in range(N_RP):
         for i in range(Q * M_LOCAL):
@@ -130,46 +129,45 @@
         out_ref[p, ROWS:, :] = found.astype(BF)
 
 
-def phase_kernel(re_ref, k_ref, cos_ref, sin_ref):
+def phase_kernel(re_ref, k_ref, out_ref):
     left = re_ref[...].astype(F32).astype(BF)
     right = k_ref[...].astype(F32).astype(BF)
     products = lax.dot_general(left, right, (((0,), (0,)), ((), ())), preferred_element_type=F32)
     cosine, sine = cos_sin(products)
-    cos_ref[...] = cosine.astype(BF)
-    sin_ref[...] = sine.astype(BF)
-
-
-def final_kernel(slot_ref, rotations_ref, cos_ref, sin_ref, reply_ref, block_ref, out_ref, far_ref, near_ref, coupling_ref):
-    step = pl.program_id(0)
+    out_ref[0, :, :LANES] = cosine.astype(BF)
+    out_ref[0, :, LANES:] = sine.astype(BF)
+
+
+def final_kernel(slot_ref, rotations_ref, phase_ref, gathered_ref, out_ref, turned_ref, replies_ref, far_ref, near_ref, coupling_ref):
     size = NB * NB
 
-    @pl.when(step == 0)
+    @pl.when(pl.program_id(0) == 0)
     def _():
-        near_ref[...] = rotations_ref[...].astype(F32).T
-        replies = reply_ref[...].reshape(N_RE * SLOTS, LANES)
-        for q in range(Q):
-            slots = lax.broadcasted_iota(I32, (N_RE * SLOTS, K), 0)
-            one_hot = (slots == slot_ref[q : q + 1, :]).astype(F32).astype(BF)
-            far_ref[q] = lax.dot_general(replies, one_hot, (((0,), (0,)), ((), ())), preferred_element_type=F32)
-
-    block = block_ref[...].reshape(RE, LANES)
-    contract = (((0,), (0,)), ((), ()))
-    with_cos = lax.dot_general(block, cos_ref[...], contract, preferred_element_type=F32)
-    with_sin = lax.dot_general(block, sin_ref[...], contract, preferred_element_type=F32)
-    coupling_ref[0:size] = with_cos[0:size] - with_sin[size:]
-    coupling_ref[size:] = with_sin[0:size] + with_cos[size:]
-    q = step // M_LOCAL
-    for t in range(K // LANES):
-        lanes = slice(t * LANES, (t + 1) * LANES)
-        u_re = [near_ref[b * NB : (b + 1) * NB, lanes] for b in range(NB)]
-        u_im = [near_ref[size + b * NB : size + (b + 1) * NB, lanes] for b in range(NB)]
+        for i in range(Q * M_LOCAL):
+            block = gathered_ref[:, i * RE_LOCAL : (i + 1) * RE_LOCAL, :].reshape(RE, LANES)
+            turned_ref[i] = block.T
+        replies_ref[...] = gathered_ref[:, ROWS:, :].reshape(N_RE * SLOTS, LANES).T
+
+    near_ref[...] = rotations_ref[...].astype(F32).T
+    slots = lax.broadcasted_iota(I32, (N_RE * SLOTS, LANES), 0)
+    one_hot = [(slots == slot_ref[q : q + 1, :]).astype(F32).astype(BF) for q in range(Q)]
+    far = jnp.dot(replies_ref[...], jnp.concatenate(one_hot, axis=1), preferred_element_type=F32)
+    for q in range(Q):
+        far_ref[q] = far[:, q * LANES : (q + 1) * LANES]
+    u_re = [near_ref[b * NB : (b + 1) * NB] for b in range(NB)]
+    u_im = [near_ref[size + b * NB : size + (b + 1) * NB] for b in range(NB)]
+    for i in range(Q * M_LOCAL):
+        q = i // M_LOCAL
+        both = jnp.dot(turned_ref[i], phase_ref[0], preferred_element_type=F32)
+        coupling_ref[i, :size] = both[:size, :LANES] - both[size:, LANES:]
+        coupling_ref[i, size:] = both[:size, LANES:] + both[size:, :LANES]
         h_re, h_im = [], []
         for a in range(NB):
             acc_re = acc_im = None
             for b in range(NB):
                 row = a * NB + b
-                c_re = coupling_ref[row : row + 1, lanes]
-                c_im = coupling_ref[size + row : size + row + 1, lanes]
+                c_re = coupling_ref[i, row : row + 1]
+                c_im = coupling_ref[i, size + row : size + row + 1]
                 add_re = c_re * u_re[b] - c_im * u_im[b]
                 add_im = c_re * u_im[b] + c_im * u_re[b]
                 acc_re = add_re if acc_re is None else acc_re + add_re
@@ -182,8 +180,8 @@
                 acc_re = acc_im = None
                 for a in range(NB):
                     row = a * NB + m
-                    v_re = far_ref[q, row : row + 1, lanes]
-                    v_im = far_ref[q, size + row : size + row + 1, lanes]
+                    v_re = far_ref[q, row : row + 1]
+                    v_im = far_ref[q, size + row : size + row + 1]
                     add_re = v_re * h_re[a] + v_im * h_im[a]
                     add_im = v_re * h_im[a] - v_im * h_re[a]
                     acc_re = add_re if acc_re is None else acc_re + add_re
@@ -191,8 +189,8 @@
                 real.append(acc_re)
                 imag.append(acc_im)
             rows = slice(pair * 16, pair * 16 + 16)
-            out_ref[0, 0, rows, lanes] = jnp.concatenate(real, axis=0).astype(BF)
-            out_ref[0, 1, rows, lanes] = jnp.concatenate(imag, axis=0).astype(BF)
+            out_ref[i, 0, rows] = jnp.concatenate(real, axis=0).astype(BF)
+            out_ref[i, 1, rows] = jnp.concatenate(imag, axis=0).astype(BF)
 
 
 def whole(shape):
@@ -203,8 +201,12 @@
     return pl.BlockSpec(memory_space=pltpu.SMEM)
 
 
-def params():
-    return pltpu.CompilerParams(vmem_limit_bytes=48 << 20)
+def in_hbm(array):
+    return pltpu.with_memory_space_constraint(array, pltpu.HBM)
+
+
+def params(mebibytes):
+    return pltpu.CompilerParams(vmem_limit_bytes=mebibytes << 20)
 
 
 def local(
@@ -218,17 +220,6 @@
     kq_owner,
     kq_row,
 ):
-    requests, slots = pl.pallas_call(
-        requests_kernel,
-        out_shape=(
-            jax.ShapeDtypeStruct((N_RE, 8, LANES), I32),
-            jax.ShapeDtypeStruct((Q, K), I32),
-        ),
-        compiler_params=params(),
-        name="requests",
-    )(kq_owner.reshape(Q, K), kq_row)
-    wanted = lax.all_to_all(requests, "re", split_axis=0, concat_axis=0, tiled=True)
-
     chunk = 16
     block = (Q * M_LOCAL, chunk, LANES)
     parts = pl.pallas_call(
@@ -238,25 +229,36 @@
             smem(),
             smem(),
             smem(),
-            whole((3, 8 * RP_LOCAL)),
+            whole((3, RP_LOCAL)),
             pl.BlockSpec((chunk, RP_LOCAL, 2 * MODES * NB * NB), lambda i: (i, 0, 0)),
         ],
         out_specs=[pl.BlockSpec(block, lambda i: (0, i, 0))] * N_RP,
         out_shape=[jax.ShapeDtypeStruct((Q * M_LOCAL, RE_LOCAL, LANES), BF)] * N_RP,
-        compiler_params=params(),
+        compiler_params=params(16),
         name="mix",
     )(
-        mode_matrix,
-        q_coords,
+        in_hbm(mode_matrix.transpose(1, 0, 2)),
+        in_hbm(q_coords.T),
         lax.axis_index("rp").reshape(1),
-        jnp.tile(rp_coords, (1, 8)),
-        wannier_table,
+        in_hbm(rp_coords),
+        in_hbm(wannier_table),
     )
     own = parts[0].reshape(ROWS, LANES)
     others = [
         lax.ppermute(parts[s].reshape(ROWS, LANES), "rp", [(j, j ^ s) for j in range(N_RP)])
         for s in range(1, N_RP)
     ]
+
+    requests, slots = pl.pallas_call(
+        requests_kernel,
+        out_shape=(
+            jax.ShapeDtypeStruct((N_RE, 8, LANES), I32),
+            jax.ShapeDtypeStruct((Q, K), I32),
+        ),
+        compiler_params=params(16),
+        name="requests",
+    )(in_hbm(kq_owner.transpose(0, 2, 1)), in_hbm(kq_row))
+    wanted = lax.all_to_all(requests, "re", split_axis=0, concat_axis=0, tiled=True)
 
     peers = 8
     packed = pl.pallas_call(
@@ -265,43 +267,44 @@
         in_specs=[whole((ROWS, LANES))] * N_RP
         + [pl.BlockSpec((peers, 8, LANES), lambda i: (i, 0, 0)), whole((K, LANES))],
         out_specs=pl.BlockSpec((peers, PACK, LANES), lambda i: (i, 0, 0)),
-        out_shape=jax.ShapeDtypeStruct((N_RE, PACK, LANES), BF),
-        compiler_params=params(),
+        out_shape=pltpu.HBM((N_RE, PACK, LANES), BF),
+        compiler_params=params(16),
         name="pack",
     )(own, *others, wanted, rotations)
     gathered = lax.all_to_all(packed, "re", split_axis=0, concat_axis=0, tiled=True)
 
-    cosine, sine = pl.pallas_call(
+    tiles = K // LANES
+    phases = pl.pallas_call(
         phase_kernel,
-        grid=(4,),
-        in_specs=[pl.BlockSpec((3, RE // 4), lambda i: (0, i)), whole((3, K))],
-        out_specs=[pl.BlockSpec((RE // 4, K), lambda i: (i, 0))] * 2,
-        out_shape=[jax.ShapeDtypeStruct((RE, K), BF)] * 2,
-        compiler_params=params(),
+        grid=(tiles,),
+        in_specs=[whole((3, RE)), pl.BlockSpec((3, LANES), lambda t: (0, t))],
+        out_specs=pl.BlockSpec((1, RE, 2 * LANES), lambda t: (t, 0, 0)),
+        out_shape=pltpu.HBM((tiles, RE, 2 * LANES), BF),
+        compiler_params=params(16),
         name="phase",
-    )(re_coords, k_coords)
+    )(in_hbm(re_coords), in_hbm(k_coords))
 
     result = pl.pallas_call(
         final_kernel,
-        grid=(Q * M_LOCAL,),
+        grid=(tiles,),
         in_specs=[
-            whole((Q, K)),
-            whole((K, LANES)),
-            whole((RE, K)),
-            whole((RE, K)),
-            pl.BlockSpec((N_RE, SLOTS, LANES), lambda i: (0, ROWS // SLOTS, 0)),
-            pl.BlockSpec((N_RE, RE_LOCAL, LANES), lambda i: (0, i, 0)),
+            pl.BlockSpec((Q, LANES), lambda t: (0, t)),
+            pl.BlockSpec((LANES, LANES), lambda t: (t, 0)),
+            pl.BlockSpec((1, RE, 2 * LANES), lambda t: (t, 0, 0)),
+            pl.BlockSpec(memory_space=pltpu.VMEM),
         ],
-        out_specs=pl.BlockSpec((1, 2, NB * NB, K), lambda i: (i, 0, 0, 0)),
+        out_specs=pl.BlockSpec((Q * M_LOCAL, 2, NB * NB, LANES), lambda t: (0, 0, 0, t)),
         out_shape=jax.ShapeDtypeStruct((Q * M_LOCAL, 2, NB * NB, K), BF),
         scratch_shapes=[
-            pltpu.VMEM((Q, LANES, K), F32),
-            pltpu.VMEM((LANES, K), F32),
-            pltpu.VMEM((LANES, K), F32),
+            pltpu.VMEM((Q * M_LOCAL, LANES, RE), BF),
+            pltpu.VMEM((LANES, N_RE * SLOTS), BF),
+            pltpu.VMEM((Q, LANES, LANES), F32),
+            pltpu.VMEM((LANES, LANES), F32),
+            pltpu.VMEM((Q * M_LOCAL, LANES, LANES), F32),
         ],
-        compiler_params=params(),
+        compiler_params=params(16),
         name="final",
-    )(slots, rotations, cosine, sine, gathered, gathered)
+    )(slots, in_hbm(rotations), in_hbm(phases), gathered)
     return result.reshape(Q, M_LOCAL, 2, NB * NB, K)
 
 

time: 77.4 us -> 70.8 us (0.915)
  local copies, waits for them, and re-layouts: 9.04 us -> 0.01 us
  Pallas kernels: 17.9 us -> 21.3 us
    unnamed x19 -> x2, local copies, waits for them, and re-layouts: 8.28 us -> 0.01 us
    pallas_call x1, Pallas kernels: 1.77 us -> 2.85 us  [local(): pl.pallas_call(pack_kernel, grid=(N_RE // peers,), in_specs=[whole((ROWS,...]
    pallas_call x2, Pallas kernels: 12.4 us -> 13.3 us  [the longest x1 8.37 us: local(): pl.pallas_call(final_kernel, grid=(tiles,), in_specs=[pl.BlockSpec((Q, LA...]
  transfers between devices with their start and end apart: 5 -> 5, of which waited for: 3 -> 3; matrix products, arithmetic and copies ran while one was open for 3% -> 0% of each run, Pallas kernels for 7% -> 11%
where the time goes in v2:
time: 70.8 us; the launch traced here: 70.5 us
  waiting for transfers between devices  28.9 us (41%)
  Pallas kernels  21.3 us (30%)
  starting transfers between devices  20.2 us (29%)
    all_to_all x1, waiting for transfers between devices, local(): lax.all_to_all(packed, 're', split_axis=0, concat_axis=0, tiled=True)  23.7 us
    all_to_all x1, starting transfers between devices, local(): lax.all_to_all(requests, 're', split_axis=0, concat_axis=0, tiled=True)  8.76 us
    pallas_call x1, Pallas kernels, local(): pl.pallas_call(final_kernel, grid=(tiles,), in_specs=[pl.BlockSpec((Q, LA...  8.37 us
    all_to_all x1, starting transfers between devices, local(): lax.all_to_all(packed, 're', split_axis=0, concat_axis=0, tiled=True)  7.68 us
    ppermute x3, waiting for transfers between devices, local(): lax.ppermute(parts[s].reshape(ROWS, LANES), 'rp', [(j, j ^ s) for j in ra...  5.15 us
    pallas_call x1, Pallas kernels, local(): pl.pallas_call(phase_kernel, grid=(tiles,), in_specs=[whole((3, RE)), pl....  4.88 us
    ppermute x3, starting transfers between devices, local(): lax.ppermute(parts[s].reshape(ROWS, LANES), 'rp', [(j, j ^ s) for j in ra...  3.8 us
    pallas_call x1, Pallas kernels, local(): pl.pallas_call(mix_kernel, grid=(RE_LOCAL // chunk,), in_specs=[smem(), s...  3.19 us
  transfers between devices with their start and end apart: 5, of which 3 were waited for; matrix products, arithmetic and copies ran while one was open for 0% of the time, Pallas kernels for 11%

profile of v2, /device:TPU:0, one launch (start us, length us, event | category | flops | bytes accessed | tf_op | source)
XLA Modules:
  0.0 70.5 jit_solution(16686523026743325571)
XLA Ops:
  0.0 0.0 copy-start
  0.0 2.0 %requests.1 = (s32[32,8,128]{2,1,0:T(8,128)}, s32[2,512]{1,0:T(2,128)S(1)}) custom-call(s32[2,1,512]{2,1,0:T(1,128)} %bitcast.14, s32[2,512]{1,0:T(2,128)} %row_ref.1), custom_call_target="tpu_custom_call" | custom-call | tf_op jit(solution)/shard_map/requests/pallas_call | solution.py:252
  2.0 8.8 %all-to-all-start = ((s32[32,8,128]{2,1,0:T(8,128)}), s32[32,8,128]{2,1,0:T(8,128)S(1)}, u32[]{:S(2)}, u32[]{:S(2)}) async-start(s32[32,8,128]{2,1,0:T(8,128)} %get-tuple-element.16), calls=%async_computation | async-start | bytes 262144 | tf_op jit(solution)/shard_map/all_to_all | solution.py:261
  10.8 3.2 %mix.1 = (bf16[6,32,128]{2,1,0:T(8,128)(2,1)S(1)}, bf16[6,32,128]{2,1,0:T(8,128)(2,1)S(1)}, bf16[6,32,128]{2,1,0:T(8,128)(2,1)S(1)}, bf16[6,32,128]{2,1,0:T(8,128)(2,1)S(1)}) custom-call(f32[12,2,12]{2,1,0:T(2,128)} %bitcast.13, s32[2,3]{1,0:T(2,128)} %bitcast.15, s32[1]{0:T(128)} %bitcast.3.rank_ref, s32[3,32]{1,0:T(4,128)} %rp_ref.1, ...), custom_call_target="tpu_custom_call" | custom-call | tf_op jit(solution)/shard_map/mix/pallas_call | solution.py:225
  14.0 0.1 collective-permute-start
  14.1 3.7 %collective-permute-start.1 = (bf16[192,128]{1,0:T(8,128)(2,1)S(1)}, bf16[192,128]{1,0:T(8,128)(2,1)S(1)}, u32[]{:S(2)}, u32[]{:S(2)}) collective-permute-start(bf16[192,128]{1,0:T(8,128)(2,1)S(1)} %bitcast.11), channel_id=1, source_target_pairs={{0,2},{1,3},{2,0},{3,1},{4,6},{5,7},{6,4},{7,5},{8,10},{9,11},{10,... | collective-permute-start | bytes 147464 | tf_op jit(solution)/shard_map/ppermute | solution.py:248
  17.8 0.1 collective-permute-start.2
  17.8 0.0 collective-permute-done.one_ref
  17.8 2.6 %collective-permute-done.1.two_ref = bf16[192,128]{1,0:T(8,128)(2,1)S(1)} collective-permute-done((bf16[192,128]{1,0:T(8,128)(2,1)S(1)}, bf16[192,128]{1,0:T(8,128)(2,1)S(1)}, u32[]{:S(2)}, u32[]{:S(2)}) %collective-permute-start.1) | collective-permute-done | bytes 49184 | tf_op jit(solution)/shard_map/ppermute | solution.py:248
  20.4 2.5 %collective-permute-done.2.three_ref = bf16[192,128]{1,0:T(8,128)(2,1)S(1)} collective-permute-done((bf16[192,128]{1,0:T(8,128)(2,1)S(1)}, bf16[192,128]{1,0:T(8,128)(2,1)S(1)}, u32[]{:S(2)}, u32[]{:S(2)}) %collective-permute-start.2) | collective-permute-done | bytes 49184 | tf_op jit(solution)/shard_map/ppermute | solution.py:248
  23.0 0.0 all-to-all-done.request_ref
  23.0 0.0 copy-done
  23.0 2.9 %pack.1 = bf16[32,240,128]{2,1,0:T(8,128)(2,1)} custom-call(bf16[192,128]{1,0:T(8,128)(2,1)S(1)} %bitcast.9, bf16[192,128]{1,0:T(8,128)(2,1)S(1)} %collective-permute-done.one_ref, bf16[192,128]{1,0:T(8,128)(2,1)S(1)} %collective-permute-done.1.two_ref, bf16[192,128]{1,0:T(8,128)(2,1)S(1)} %collective-permute-done.2.three_ref, ...), custom_call_target="tpu_custom_call" | custom-call | tf_op jit(solution)/shard_map/pack/pallas_call | solution.py:264
  25.8 7.7 %all-to-all-start.1 = ((bf16[32,240,128]{2,1,0:T(8,128)(2,1)}), bf16[32,240,128]{2,1,0:T(8,128)(2,1)S(1)}, u32[]{:S(2)}, u32[]{:S(2)}) async-start(bf16[32,240,128]{2,1,0:T(8,128)(2,1)} %pack.1), calls=%async_computation.1 | async-start | bytes 3932160 | tf_op jit(solution)/shard_map/all_to_all | solution.py:274
  33.5 4.9 %phase.1.phase_ref = bf16[4,1024,256]{2,1,0:T(8,128)(2,1)} custom-call(s32[3,1024]{1,0:T(4,128)} %re_ref.1, s32[3,512]{1,0:T(4,128)} %k_ref.1), custom_call_target="tpu_custom_call" | custom-call | tf_op jit(solution)/shard_map/phase/pallas_call | solution.py:277
  38.4 23.7 %all-to-all-done.1.gathered_ref = bf16[32,240,128]{2,1,0:T(8,128)(2,1)S(1)} async-done(((bf16[32,240,128]{2,1,0:T(8,128)(2,1)}), bf16[32,240,128]{2,1,0:T(8,128)(2,1)S(1)}, u32[]{:S(2)}, u32[]{:S(2)}) %all-to-all-start.1) | async-done | bytes 1966112 | tf_op jit(solution)/shard_map/all_to_all | solution.py:274
  62.1 8.4 %final.1 = bf16[6,2,64,512]{3,2,1,0:T(8,128)(2,1)} custom-call(s32[2,512]{1,0:T(2,128)S(1)} %get-tuple-element.11.slot_ref, bf16[512,128]{1,0:T(8,128)(2,1)} %rotations_ref.3, bf16[4,1024,256]{2,1,0:T(8,128)(2,1)} %phase.1.phase_ref, bf16[32,240,128]{2,1,0:T(8,128)(2,1)S(1)} %all-to-all-done.1.gathered_ref), custom_call_target="tpu_custom_call" | custom-call | tf_op jit(solution)/shard_map/final/pallas_call | solution.py:287
Async XLA Ops:
  0.0 23.0 %copy-start = (bf16[512,128]{1,0:T(8,128)(2,1)S(1)}, bf16[512,128]{1,0:T(8,128)(2,1)}, u32[]{:S(2)}) copy-start(bf16[512,128]{1,0:T(8,128)(2,1)} %rotations_ref.3) | copy-start | bytes 393220
  2.0 20.9 %all-to-all-start = ((s32[32,8,128]{2,1,0:T(8,128)}), s32[32,8,128]{2,1,0:T(8,128)S(1)}, u32[]{:S(2)}, u32[]{:S(2)}) async-start(s32[32,8,128]{2,1,0:T(8,128)} %get-tuple-element.16), calls=%async_computation | async-start | bytes 262144 | tf_op jit(solution)/shard_map/all_to_all | solution.py:261
  14.0 3.8 %collective-permute-start = (bf16[192,128]{1,0:T(8,128)(2,1)S(1)}, bf16[192,128]{1,0:T(8,128)(2,1)S(1)}, u32[]{:S(2)}, u32[]{:S(2)}) collective-permute-start(bf16[192,128]{1,0:T(8,128)(2,1)S(1)} %bitcast.12), channel_id=1, source_target_pairs={{0,1},{1,0},{2,3},{3,2},{4,5},{5,4},{6,7},{7,6},{8,9},{9,8},{10,11... | collective-permute-start | bytes 147464 | tf_op jit(solution)/shard_map/ppermute | solution.py:248
  14.1 6.3 %collective-permute-start.1 = (bf16[192,128]{1,0:T(8,128)(2,1)S(1)}, bf16[192,128]{1,0:T(8,128)(2,1)S(1)}, u32[]{:S(2)}, u32[]{:S(2)}) collective-permute-start(bf16[192,128]{1,0:T(8,128)(2,1)S(1)} %bitcast.11), channel_id=1, source_target_pairs={{0,2},{1,3},{2,0},{3,1},{4,6},{5,7},{6,4},{7,5},{8,10},{9,11},{10,... | collective-permute-start | bytes 147464 | tf_op jit(solution)/shard_map/ppermute | solution.py:248
  17.8 5.2 %collective-permute-start.2 = (bf16[192,128]{1,0:T(8,128)(2,1)S(1)}, bf16[192,128]{1,0:T(8,128)(2,1)S(1)}, u32[]{:S(2)}, u32[]{:S(2)}) collective-permute-start(bf16[192,128]{1,0:T(8,128)(2,1)S(1)} %bitcast.10), channel_id=1, source_target_pairs={{0,3},{1,2},{2,1},{3,0},{4,7},{5,6},{6,5},{7,4},{8,11},{9,10},{10,... | collective-permute-start | bytes 147464 | tf_op jit(solution)/shard_map/ppermute | solution.py:248
  25.8 36.3 %all-to-all-start.1 = ((bf16[32,240,128]{2,1,0:T(8,128)(2,1)}), bf16[32,240,128]{2,1,0:T(8,128)(2,1)S(1)}, u32[]{:S(2)}, u32[]{:S(2)}) async-start(bf16[32,240,128]{2,1,0:T(8,128)(2,1)} %pack.1), calls=%async_computation.1 | async-start | bytes 3932160 | tf_op jit(solution)/shard_map/all_to_all | solution.py:274

commit v3 on v2

--- a/solution.py
+++ b/solution.py
@@ -68,7 +68,7 @@
         total += lax.dot_general(low, place, contract, preferred_element_type=F32)
     total = total.astype(I32)
     for o in range(N_RE):
-        request_ref[o] = jnp.broadcast_to(total[o : o + 1, :], (8, LANES))
+        request_ref[o] = total[o : o + 1, :]
 
 
 def mix_kernel(mode_ref, q_ref, rank_ref, rp_ref, table_ref, *out_refs):
@@ -252,7 +252,7 @@
     requests, slots = pl.pallas_call(
         requests_kernel,
         out_shape=(
-            jax.ShapeDtypeStruct((N_RE, 8, LANES), I32),
+            jax.ShapeDtypeStruct((N_RE, 1, LANES), I32),
             jax.ShapeDtypeStruct((Q, K), I32),
         ),
         compiler_params=params(16),
@@ -265,7 +265,7 @@
         pack_kernel,
         grid=(N_RE // peers,),
         in_specs=[whole((ROWS, LANES))] * N_RP
-        + [pl.BlockSpec((peers, 8, LANES), lambda i: (i, 0, 0)), whole((K, LANES))],
+        + [pl.BlockSpec((peers, 1, LANES), lambda i: (i, 0, 0)), whole((K, LANES))],
         out_specs=pl.BlockSpec((peers, PACK, LANES), lambda i: (i, 0, 0)),
         out_shape=pltpu.HBM((N_RE, PACK, LANES), BF),
         compiler_params=params(16),

time: 70.8 us -> 67.5 us (0.953)
  blocking collectives: 0 us -> 16.1 us
  starting transfers between devices: 20.2 us -> 8.18 us
  waiting for transfers between devices: 28.9 us -> 22.2 us
    all_to_all x0 -> x1, blocking collectives: none -> 16.1 us  [local(): lax.all_to_all(requests, 're', split_axis=0, concat_axis=0, tiled=True)]
    all_to_all x1 -> x0, starting transfers between devices: 8.76 us -> none  [local(): lax.all_to_all(requests, 're', split_axis=0, concat_axis=0, tiled=True)]
    ppermute x3, waiting for transfers between devices: 5.15 us -> 0.01 us  [local(): lax.ppermute(parts[s].reshape(ROWS, LANES), 'rp', [(j, j ^ s) for j in ra...]
    all_to_all x1, starting transfers between devices: 7.68 us -> 4 us  [local(): lax.all_to_all(packed, 're', split_axis=0, concat_axis=0, tiled=True)]
    all_to_all x1, waiting for transfers between devices: 23.7 us -> 22.2 us  [local(): lax.all_to_all(packed, 're', split_axis=0, concat_axis=0, tiled=True)]
    pallas_call x1, Pallas kernels: 2.04 us -> 1.31 us  [local(): pl.pallas_call(requests_kernel, out_shape=(jax.ShapeDtypeStruct((N_RE, 1,...]
  transfers between devices with their start and end apart: 5 -> 4, of which waited for: 3 -> 1; matrix products, arithmetic and copies ran while one was open for 0% -> 0% of each run, Pallas kernels for 11% -> 9%
where the time goes in v3:
time: 67.5 us; the launch traced here: 67.2 us
  waiting for transfers between devices  22.2 us (33%)
  Pallas kernels  20.6 us (31%)
  blocking collectives  16.1 us (24%)
  starting transfers between devices  8.18 us (12%)
    all_to_all x1, waiting for transfers between devices, local(): lax.all_to_all(packed, 're', split_axis=0, concat_axis=0, tiled=True)  22.2 us
    all_to_all x1, blocking collectives, local(): lax.all_to_all(requests, 're', split_axis=0, concat_axis=0, tiled=True)  16.1 us
    pallas_call x1, Pallas kernels, local(): pl.pallas_call(final_kernel, grid=(tiles,), in_specs=[pl.BlockSpec((Q, LA...  8.35 us
    pallas_call x1, Pallas kernels, local(): pl.pallas_call(phase_kernel, grid=(tiles,), in_specs=[whole((3, RE)), pl....  4.89 us
    ppermute x3, starting transfers between devices, local(): lax.ppermute(parts[s].reshape(ROWS, LANES), 'rp', [(j, j ^ s) for j in ra...  4.18 us
    all_to_all x1, starting transfers between devices, local(): lax.all_to_all(packed, 're', split_axis=0, concat_axis=0, tiled=True)  4 us
    pallas_call x1, Pallas kernels, local(): pl.pallas_call(mix_kernel, grid=(RE_LOCAL // chunk,), in_specs=[smem(), s...  3.2 us
    pallas_call x1, Pallas kernels, local(): pl.pallas_call(pack_kernel, grid=(N_RE // peers,), in_specs=[whole((ROWS,...  2.89 us
  transfers between devices with their start and end apart: 4, of which 1 were waited for; matrix products, arithmetic and copies ran while one was open for 0% of the time, Pallas kernels for 9%

profile of v3, /device:TPU:0, one launch (start us, length us, event | category | flops | bytes accessed | tf_op | source)
XLA Modules:
  0.0 67.2 jit_solution(326610632142955743)
XLA Ops:
  0.0 0.0 copy-start
  0.0 3.2 %mix.1 = (bf16[6,32,128]{2,1,0:T(8,128)(2,1)S(1)}, bf16[6,32,128]{2,1,0:T(8,128)(2,1)S(1)}, bf16[6,32,128]{2,1,0:T(8,128)(2,1)S(1)}, bf16[6,32,128]{2,1,0:T(8,128)(2,1)S(1)}) custom-call(f32[12,2,12]{2,1,0:T(2,128)} %bitcast.13, s32[2,3]{1,0:T(2,128)} %bitcast.15, s32[1]{0:T(128)} %bitcast.3.rank_ref, s32[3,32]{1,0:T(4,128)} %rp_ref.1, ...), custom_call_target="tpu_custom_call" | custom-call | tf_op jit(solution)/shard_map/mix/pallas_call | solution.py:225
  3.2 0.1 collective-permute-start
  3.3 4.0 %collective-permute-start.1 = (bf16[192,128]{1,0:T(8,128)(2,1)S(1)}, bf16[192,128]{1,0:T(8,128)(2,1)S(1)}, u32[]{:S(2)}, u32[]{:S(2)}) collective-permute-start(bf16[192,128]{1,0:T(8,128)(2,1)S(1)} %bitcast.11), channel_id=1, source_target_pairs={{0,2},{1,3},{2,0},{3,1},{4,6},{5,7},{6,4},{7,5},{8,10},{9,11},{10,... | collective-permute-start | bytes 147464 | tf_op jit(solution)/shard_map/ppermute | solution.py:248
  7.3 0.1 collective-permute-start.2
  7.4 1.3 %requests.1 = (s32[32,1,128]{2,1,0:T(1,128)S(1)}, s32[2,512]{1,0:T(2,128)S(1)}) custom-call(s32[2,1,512]{2,1,0:T(1,128)} %bitcast.14, s32[2,512]{1,0:T(2,128)} %row_ref.1), custom_call_target="tpu_custom_call" | custom-call | tf_op jit(solution)/shard_map/requests/pallas_call | solution.py:252
  8.7 16.1 %all_to_all.10.request_ref = s32[32,1,128]{2,1,0:T(1,128)S(1)} all-to-all(s32[32,1,128]{2,1,0:T(1,128)S(1)} %get-tuple-element.16), channel_id=1, replica_groups=mesh['re'=32,'rp'=4] {'re'}, dimensions={0} | all-to-all | bytes 32768 | tf_op jit(solution)/shard_map/all_to_all | solution.py:261
  24.8 0.0 collective-permute-done.one_ref
  24.8 0.0 collective-permute-done.1.two_ref
  24.8 0.0 collective-permute-done.2.three_ref
  24.8 0.0 copy-done
  24.8 2.9 %pack.1 = bf16[32,240,128]{2,1,0:T(8,128)(2,1)} custom-call(bf16[192,128]{1,0:T(8,128)(2,1)S(1)} %bitcast.9, bf16[192,128]{1,0:T(8,128)(2,1)S(1)} %collective-permute-done.one_ref, bf16[192,128]{1,0:T(8,128)(2,1)S(1)} %collective-permute-done.1.two_ref, bf16[192,128]{1,0:T(8,128)(2,1)S(1)} %collective-permute-done.2.three_ref, ...), custom_call_target="tpu_custom_call" | custom-call | tf_op jit(solution)/shard_map/pack/pallas_call | solution.py:264
  27.7 4.0 %all-to-all-start.1 = ((bf16[32,240,128]{2,1,0:T(8,128)(2,1)}), bf16[32,240,128]{2,1,0:T(8,128)(2,1)S(1)}, u32[]{:S(2)}, u32[]{:S(2)}) async-start(bf16[32,240,128]{2,1,0:T(8,128)(2,1)} %pack.1), calls=%async_computation.1 | async-start | bytes 3932160 | tf_op jit(solution)/shard_map/all_to_all | solution.py:274
  31.7 4.9 %phase.1.phase_ref = bf16[4,1024,256]{2,1,0:T(8,128)(2,1)} custom-call(s32[3,1024]{1,0:T(4,128)} %re_ref.1, s32[3,512]{1,0:T(4,128)} %k_ref.1), custom_call_target="tpu_custom_call" | custom-call | tf_op jit(solution)/shard_map/phase/pallas_call | solution.py:277
  36.6 22.2 %all-to-all-done.1.gathered_ref = bf16[32,240,128]{2,1,0:T(8,128)(2,1)S(1)} async-done(((bf16[32,240,128]{2,1,0:T(8,128)(2,1)}), bf16[32,240,128]{2,1,0:T(8,128)(2,1)S(1)}, u32[]{:S(2)}, u32[]{:S(2)}) %all-to-all-start.1) | async-done | bytes 1966112 | tf_op jit(solution)/shard_map/all_to_all | solution.py:274
  58.8 8.4 %final.1 = bf16[6,2,64,512]{3,2,1,0:T(8,128)(2,1)} custom-call(s32[2,512]{1,0:T(2,128)S(1)} %get-tuple-element.11.slot_ref, bf16[512,128]{1,0:T(8,128)(2,1)} %rotations_ref.3, bf16[4,1024,256]{2,1,0:T(8,128)(2,1)} %phase.1.phase_ref, bf16[32,240,128]{2,1,0:T(8,128)(2,1)S(1)} %all-to-all-done.1.gathered_ref), custom_call_target="tpu_custom_call" | custom-call | tf_op jit(solution)/shard_map/final/pallas_call | solution.py:287
Async XLA Ops:
  0.0 24.8 %copy-start = (bf16[512,128]{1,0:T(8,128)(2,1)S(1)}, bf16[512,128]{1,0:T(8,128)(2,1)}, u32[]{:S(2)}) copy-start(bf16[512,128]{1,0:T(8,128)(2,1)} %rotations_ref.3) | copy-start | bytes 393220
  3.2 21.6 %collective-permute-start = (bf16[192,128]{1,0:T(8,128)(2,1)S(1)}, bf16[192,128]{1,0:T(8,128)(2,1)S(1)}, u32[]{:S(2)}, u32[]{:S(2)}) collective-permute-start(bf16[192,128]{1,0:T(8,128)(2,1)S(1)} %bitcast.12), channel_id=1, source_target_pairs={{0,1},{1,0},{2,3},{3,2},{4,5},{5,4},{6,7},{7,6},{8,9},{9,8},{10,11... | collective-permute-start | bytes 147464 | tf_op jit(solution)/shard_map/ppermute | solution.py:248
  3.3 21.5 %collective-permute-start.1 = (bf16[192,128]{1,0:T(8,128)(2,1)S(1)}, bf16[192,128]{1,0:T(8,128)(2,1)S(1)}, u32[]{:S(2)}, u32[]{:S(2)}) collective-permute-start(bf16[192,128]{1,0:T(8,128)(2,1)S(1)} %bitcast.11), channel_id=1, source_target_pairs={{0,2},{1,3},{2,0},{3,1},{4,6},{5,7},{6,4},{7,5},{8,10},{9,11},{10,... | collective-permute-start | bytes 147464 | tf_op jit(solution)/shard_map/ppermute | solution.py:248
  7.3 17.5 %collective-permute-start.2 = (bf16[192,128]{1,0:T(8,128)(2,1)S(1)}, bf16[192,128]{1,0:T(8,128)(2,1)S(1)}, u32[]{:S(2)}, u32[]{:S(2)}) collective-permute-start(bf16[192,128]{1,0:T(8,128)(2,1)S(1)} %bitcast.10), channel_id=1, source_target_pairs={{0,3},{1,2},{2,1},{3,0},{4,7},{5,6},{6,5},{7,4},{8,11},{9,10},{10,... | collective-permute-start | bytes 147464 | tf_op jit(solution)/shard_map/ppermute | solution.py:248
  27.7 31.1 %all-to-all-start.1 = ((bf16[32,240,128]{2,1,0:T(8,128)(2,1)}), bf16[32,240,128]{2,1,0:T(8,128)(2,1)S(1)}, u32[]{:S(2)}, u32[]{:S(2)}) async-start(bf16[32,240,128]{2,1,0:T(8,128)(2,1)} %pack.1), calls=%async_computation.1 | async-start | bytes 3932160 | tf_op jit(solution)/shard_map/all_to_all | solution.py:274

commit v4 on v3

--- a/solution.py
+++ b/solution.py
@@ -23,6 +23,8 @@
 ROWS = Q * M_LOCAL * RE_LOCAL
 PACK = ROWS + SLOTS
 LANES = 128
+TILES = K // LANES
+SIZE = NB * NB
 TURN = 2.0 * math.pi
 SINE = [TURN ** n * s / math.factorial(n) for n, s in ((1, 1), (3, -1), (5, 1), (7, -1), (9, 1), (11, -1))]
 BF = jnp.bfloat16
@@ -59,7 +61,7 @@
         one_hot = hit.astype(F32)
         earlier = jnp.dot(one_hot.astype(BF), before, preferred_element_type=F32)
         rank = jnp.sum(one_hot * earlier, axis=0, keepdims=True).astype(I32) + q * CAP
-        slot_ref[q : q + 1, :] = owner * SLOTS + rank
+        slot_ref[q : q + 1, :] = owner * CAP + rank - q * CAP
         place = (lax.broadcasted_iota(I32, (LANES, K), 0) == rank).astype(F32).astype(BF)
         high = (one_hot * (row >> 4).astype(F32)).astype(BF)
         low = (one_hot * (row & 15).astype(F32)).astype(BF)
@@ -114,83 +116,120 @@
             out_refs[s][i] = jnp.concatenate(parts[s][i], axis=0).astype(BF)
 
 
-def pack_kernel(own_ref, one_ref, two_ref, three_ref, request_ref, rotations_ref, out_ref):
+def sum_kernel(own_ref, one_ref, two_ref, three_ref, out_ref):
     total = own_ref[...].astype(F32) + one_ref[...].astype(F32)
     total += two_ref[...].astype(F32) + three_ref[...].astype(F32)
-    total = total.astype(BF)
+    out_ref[...] = jnp.broadcast_to(total.astype(BF)[None], out_ref.shape)
+
+
+def lookup_kernel(packed_ref, request_ref, rotations_ref, out_ref):
     peers = out_ref.shape[0]
     wanted = request_ref[:, 0, :].T
     rows = lax.broadcasted_iota(I32, (SLOTS, K), 1)
-    rotations = rotations_ref[...]
-    for p in range(peers):
-        out_ref[p, :ROWS, :] = total
-        one_hot = (wanted[:SLOTS, p : p + 1] == rows).astype(F32).astype(BF)
-        found = jnp.dot(one_hot, rotations, preferred_element_type=F32)
-        out_ref[p, ROWS:, :] = found.astype(BF)
-
-
-def phase_kernel(re_ref, k_ref, out_ref):
+    one_hot = [(wanted[:SLOTS, p : p + 1] == rows).astype(F32).astype(BF) for p in range(peers)]
+    found = jnp.dot(jnp.concatenate(one_hot, axis=0), rotations_ref[...], preferred_element_type=F32)
+    out_ref[...] = found.reshape(peers, SLOTS, LANES).astype(BF)
+
+
+def phase_kernel(re_ref, k_ref, slot_ref, rotations_ref, out_ref, pick_ref, near_ref):
     left = re_ref[...].astype(F32).astype(BF)
     right = k_ref[...].astype(F32).astype(BF)
     products = lax.dot_general(left, right, (((0,), (0,)), ((), ())), preferred_element_type=F32)
     cosine, sine = cos_sin(products)
     out_ref[0, :, :LANES] = cosine.astype(BF)
     out_ref[0, :, LANES:] = sine.astype(BF)
-
-
-def final_kernel(slot_ref, rotations_ref, phase_ref, gathered_ref, out_ref, turned_ref, replies_ref, far_ref, near_ref, coupling_ref):
-    size = NB * NB
-
-    @pl.when(pl.program_id(0) == 0)
-    def _():
+    place = lax.broadcasted_iota(I32, (N_RE * CAP, LANES), 0)
+    for q in range(Q):
+        pick_ref[q] = (place == slot_ref[q : q + 1, :]).astype(F32).astype(BF)
+    near = rotations_ref[...].astype(F32).T
+    near_ref[: 2 * SIZE] = near
+    near_ref[2 * SIZE :] = near[:SIZE] + near[SIZE:]
+
+
+def chain(terms):
+    total = None
+    for term in terms:
+        total = term if total is None else total + term
+    return total
+
+
+def rotate(coupling_ref, far_ref, near_ref, out_ref, q, i, t):
+    lanes = slice(t * LANES, (t + 1) * LANES)
+    near = [[near_ref[o * SIZE + b * NB : o * SIZE + (b + 1) * NB, lanes] for b in range(NB)] for o in range(3)]
+    halves = []
+    for a in range(NB):
+        real, imag, both = [
+            chain(coupling_ref[o * SIZE + a * NB + b : o * SIZE + a * NB + b + 1] * near[o][b] for b in range(NB))
+            for o in range(3)
+        ]
+        half = real - imag, both - (real + imag)
+        halves.append((*half, half[0] + half[1]))
+    for pair in range(NB // 2):
+        results = [], []
+        for m in (2 * pair, 2 * pair + 1):
+            real, imag, both = [
+                chain(far_ref[q, o * SIZE + a * NB + m : o * SIZE + a * NB + m + 1, lanes] * halves[a][o] for a in range(NB))
+                for o in range(3)
+            ]
+            results[0].append(real + imag)
+            results[1].append(both - (real - imag))
+        rows = slice(pair * 2 * NB, (pair + 1) * 2 * NB)
+        for c in range(2):
+            out_ref[t, i, c, rows] = jnp.concatenate(results[c], axis=0).astype(BF)
+
+
+def final_kernel(
+    phase_hbm, pick_hbm, near_hbm, gathered_ref, out_hbm,
+    phase_ref, pick_ref, near_ref, turned_ref, far_ref, coupling_ref, out_ref, phase_sem, pick_sem, near_sem, out_sem,
+):
+    phase_copies = [pltpu.make_async_copy(phase_hbm.at[t], phase_ref.at[t], phase_sem.at[t]) for t in range(TILES)]
+    pick_copy = pltpu.make_async_copy(pick_hbm, pick_ref, pick_sem)
+    near_copy = pltpu.make_async_copy(near_hbm, near_ref, near_sem)
+    out_copies = [
+        pltpu.make_async_copy(out_ref.at[t], out_hbm.at[:, :, :, t * LANES : (t + 1) * LANES], out_sem.at[t])
+        for t in range(TILES)
+    ]
+    pick_copy.start()
+    phase_copies[0].start()
+    near_copy.start()
+    for t in range(1, TILES):
+        phase_copies[t].start()
+    replies = gathered_ref[:, ROWS:, :].astype(F32)
+    turned = []
+    for q in range(Q):
+        rows = replies[:, q * CAP : (q + 1) * CAP, :].reshape(N_RE * CAP, LANES)
+        turned.append(rows.T.astype(BF))
+    for i in range(Q * M_LOCAL):
+        block = gathered_ref[:, i * RE_LOCAL : (i + 1) * RE_LOCAL, :].reshape(RE, LANES)
+        turned_ref[i] = block.T
+    pick_copy.wait()
+    for q in range(Q):
+        far = jnp.dot(turned[q], pick_ref[q], preferred_element_type=F32)
+        far_ref[q, : 2 * SIZE] = far
+        far_ref[q, 2 * SIZE :] = far[:SIZE] - far[SIZE:]
+
+    def couple(t, i):
+        both = jnp.dot(turned_ref[i], phase_ref[t], preferred_element_type=F32)
+        real = both[:SIZE, :LANES] - both[SIZE:, LANES:]
+        imag = both[:SIZE, LANES:] + both[SIZE:, :LANES]
+        coupling_ref[t % 2, i, :SIZE] = real
+        coupling_ref[t % 2, i, SIZE : 2 * SIZE] = imag
+        coupling_ref[t % 2, i, 2 * SIZE :] = real + imag
+
+    phase_copies[0].wait()
+    for i in range(Q * M_LOCAL):
+        couple(0, i)
+    near_copy.wait()
+    for t in range(TILES):
+        if t + 1 < TILES:
+            phase_copies[t + 1].wait()
         for i in range(Q * M_LOCAL):
-            block = gathered_ref[:, i * RE_LOCAL : (i + 1) * RE_LOCAL, :].reshape(RE, LANES)
-            turned_ref[i] = block.T
-        replies_ref[...] = gathered_ref[:, ROWS:, :].reshape(N_RE * SLOTS, LANES).T
-
-    near_ref[...] = rotations_ref[...].astype(F32).T
-    slots = lax.broadcasted_iota(I32, (N_RE * SLOTS, LANES), 0)
-    one_hot = [(slots == slot_ref[q : q + 1, :]).astype(F32).astype(BF) for q in range(Q)]
-    far = jnp.dot(replies_ref[...], jnp.concatenate(one_hot, axis=1), preferred_element_type=F32)
-    for q in range(Q):
-        far_ref[q] = far[:, q * LANES : (q + 1) * LANES]
-    u_re = [near_ref[b * NB : (b + 1) * NB] for b in range(NB)]
-    u_im = [near_ref[size + b * NB : size + (b + 1) * NB] for b in range(NB)]
-    for i in range(Q * M_LOCAL):
-        q = i // M_LOCAL
-        both = jnp.dot(turned_ref[i], phase_ref[0], preferred_element_type=F32)
-        coupling_ref[i, :size] = both[:size, :LANES] - both[size:, LANES:]
-        coupling_ref[i, size:] = both[:size, LANES:] + both[size:, :LANES]
-        h_re, h_im = [], []
-        for a in range(NB):
-            acc_re = acc_im = None
-            for b in range(NB):
-                row = a * NB + b
-                c_re = coupling_ref[i, row : row + 1]
-                c_im = coupling_ref[i, size + row : size + row + 1]
-                add_re = c_re * u_re[b] - c_im * u_im[b]
-                add_im = c_re * u_im[b] + c_im * u_re[b]
-                acc_re = add_re if acc_re is None else acc_re + add_re
-                acc_im = add_im if acc_im is None else acc_im + add_im
-            h_re.append(acc_re)
-            h_im.append(acc_im)
-        for pair in range(NB // 2):
-            real, imag = [], []
-            for m in (2 * pair, 2 * pair + 1):
-                acc_re = acc_im = None
-                for a in range(NB):
-                    row = a * NB + m
-                    v_re = far_ref[q, row : row + 1]
-                    v_im = far_ref[q, size + row : size + row + 1]
-                    add_re = v_re * h_re[a] + v_im * h_im[a]
-                    add_im = v_re * h_im[a] - v_im * h_re[a]
-                    acc_re = add_re if acc_re is None else acc_re + add_re
-                    acc_im = add_im if acc_im is None else acc_im + add_im
-                real.append(acc_re)
-                imag.append(acc_im)
-            rows = slice(pair * 16, pair * 16 + 16)
-            out_ref[i, 0, rows] = jnp.concatenate(real, axis=0).astype(BF)
-            out_ref[i, 1, rows] = jnp.concatenate(imag, axis=0).astype(BF)
+            if t + 1 < TILES:
+                couple(t + 1, i)
+            rotate(coupling_ref.at[t % 2, i], far_ref, near_ref, out_ref, i // M_LOCAL, i, t)
+        out_copies[t].start()
+    for t in range(TILES):
+        out_copies[t].wait()
 
 
 def whole(shape):
@@ -261,50 +300,76 @@
     wanted = lax.all_to_all(requests, "re", split_axis=0, concat_axis=0, tiled=True)
 
     peers = 8
+    spread = pl.pallas_call(
+        sum_kernel,
+        grid=(N_RE // peers,),
+        in_specs=[whole((ROWS, LANES))] * N_RP,
+        out_specs=pl.BlockSpec((peers, ROWS, LANES), lambda i: (i, 0, 0)),
+        out_shape=pltpu.HBM((N_RE, PACK, LANES), BF),
+        compiler_params=params(8),
+        name="sum",
+    )(own, *others)
     packed = pl.pallas_call(
-        pack_kernel,
+        lookup_kernel,
         grid=(N_RE // peers,),
-        in_specs=[whole((ROWS, LANES))] * N_RP
-        + [pl.BlockSpec((peers, 1, LANES), lambda i: (i, 0, 0)), whole((K, LANES))],
-        out_specs=pl.BlockSpec((peers, PACK, LANES), lambda i: (i, 0, 0)),
+        in_specs=[
+            pl.BlockSpec(memory_space=pltpu.HBM),
+            pl.BlockSpec((peers, 1, LANES), lambda i: (i, 0, 0)),
+            whole((K, LANES)),
+        ],
+        out_specs=pl.BlockSpec((peers, SLOTS, LANES), lambda i: (i, ROWS // SLOTS, 0)),
         out_shape=pltpu.HBM((N_RE, PACK, LANES), BF),
-        compiler_params=params(16),
-        name="pack",
-    )(own, *others, wanted, rotations)
+        input_output_aliases={0: 0},
+        compiler_params=params(8),
+        name="lookup",
+    )(spread, wanted, rotations)
     gathered = lax.all_to_all(packed, "re", split_axis=0, concat_axis=0, tiled=True)
 
-    tiles = K // LANES
-    phases = pl.pallas_call(
+    phases, picks, near = pl.pallas_call(
         phase_kernel,
-        grid=(tiles,),
-        in_specs=[whole((3, RE)), pl.BlockSpec((3, LANES), lambda t: (0, t))],
-        out_specs=pl.BlockSpec((1, RE, 2 * LANES), lambda t: (t, 0, 0)),
-        out_shape=pltpu.HBM((tiles, RE, 2 * LANES), BF),
+        grid=(TILES,),
+        in_specs=[
+            whole((3, RE)),
+            pl.BlockSpec((3, LANES), lambda t: (0, t)),
+            pl.BlockSpec((Q, LANES), lambda t: (0, t)),
+            pl.BlockSpec((LANES, LANES), lambda t: (t, 0)),
+        ],
+        out_specs=[
+            pl.BlockSpec((1, RE, 2 * LANES), lambda t: (t, 0, 0)),
+            pl.BlockSpec((Q, N_RE * CAP, LANES), lambda t: (0, 0, t)),
+            pl.BlockSpec((3 * SIZE, LANES), lambda t: (0, t)),
+        ],
+        out_shape=[
+            pltpu.HBM((TILES, RE, 2 * LANES), BF),
+            pltpu.HBM((Q, N_RE * CAP, K), BF),
+            pltpu.HBM((3 * SIZE, K), F32),
+        ],
         compiler_params=params(16),
         name="phase",
-    )(in_hbm(re_coords), in_hbm(k_coords))
-
+    )(in_hbm(re_coords), in_hbm(k_coords), slots, in_hbm(rotations))
+
+    hbm = pl.BlockSpec(memory_space=pltpu.HBM)
     result = pl.pallas_call(
         final_kernel,
-        grid=(tiles,),
-        in_specs=[
-            pl.BlockSpec((Q, LANES), lambda t: (0, t)),
-            pl.BlockSpec((LANES, LANES), lambda t: (t, 0)),
-            pl.BlockSpec((1, RE, 2 * LANES), lambda t: (t, 0, 0)),
-            pl.BlockSpec(memory_space=pltpu.VMEM),
-        ],
-        out_specs=pl.BlockSpec((Q * M_LOCAL, 2, NB * NB, LANES), lambda t: (0, 0, 0, t)),
-        out_shape=jax.ShapeDtypeStruct((Q * M_LOCAL, 2, NB * NB, K), BF),
+        in_specs=[hbm, hbm, hbm, pl.BlockSpec(memory_space=pltpu.VMEM)],
+        out_specs=hbm,
+        out_shape=jax.ShapeDtypeStruct((Q * M_LOCAL, 2, SIZE, K), BF),
         scratch_shapes=[
+            pltpu.VMEM((TILES, RE, 2 * LANES), BF),
+            pltpu.VMEM((Q, N_RE * CAP, K), BF),
+            pltpu.VMEM((3 * SIZE, K), F32),
             pltpu.VMEM((Q * M_LOCAL, LANES, RE), BF),
-            pltpu.VMEM((LANES, N_RE * SLOTS), BF),
-            pltpu.VMEM((Q, LANES, LANES), F32),
-            pltpu.VMEM((LANES, LANES), F32),
-            pltpu.VMEM((Q * M_LOCAL, LANES, LANES), F32),
-        ],
-        compiler_params=params(16),
+            pltpu.VMEM((Q, 3 * SIZE, K), F32),
+            pltpu.VMEM((2, Q * M_LOCAL, 3 * SIZE, LANES), F32),
+            pltpu.VMEM((TILES, Q * M_LOCAL, 2, SIZE, LANES), BF),
+            pltpu.SemaphoreType.DMA((TILES,)),
+            pltpu.SemaphoreType.DMA,
+            pltpu.SemaphoreType.DMA,
+            pltpu.SemaphoreType.DMA((TILES,)),
+        ],
+        compiler_params=params(24),
         name="final",
-    )(slots, in_hbm(rotations), in_hbm(phases), gathered)
+    )(in_hbm(phases), in_hbm(picks), in_hbm(near), gathered)
     return result.reshape(Q, M_LOCAL, 2, NB * NB, K)
 
 

time: 67.5 us -> 67.7 us (level)
  blocking collectives: 16.1 us -> 0 us
  starting transfers between devices: 8.18 us -> 16.2 us
  waiting for transfers between devices: 22.2 us -> 27.8 us
  Pallas kernels: 20.6 us -> 23.2 us
    all_to_all x1 -> x0, blocking collectives: 16.1 us -> none  [local(): lax.all_to_all(requests, 're', split_axis=0, concat_axis=0, tiled=True)]
    all_to_all x0 -> x1, starting transfers between devices: none -> 8.04 us  [local(): lax.all_to_all(requests, 're', split_axis=0, concat_axis=0, tiled=True)]
    all_to_all x0 -> x1, waiting for transfers between devices: none -> 6.36 us  [local(): lax.all_to_all(requests, 're', split_axis=0, concat_axis=0, tiled=True)]
    pallas_call x3 -> x4, Pallas kernels: 16.1 us -> 18.1 us  [the longest x1 8.18 us: local(): pl.pallas_call(final_kernel, in_specs=[hbm, hbm, hbm, pl.BlockSpec(memory...]
    all_to_all x1, waiting for transfers between devices: 22.2 us -> 21.5 us  [local(): lax.all_to_all(packed, 're', split_axis=0, concat_axis=0, tiled=True)]
  transfers between devices with their start and end apart: 4 -> 5, of which waited for: 1 -> 2; matrix products, arithmetic and copies ran while one was open for 0% -> 0% of each run, Pallas kernels for 9% -> 14%
where the time goes in v4:
time: 67.7 us; the launch traced here: 67.3 us
  waiting for transfers between devices  27.8 us (41%)
  Pallas kernels  23.2 us (34%)
  starting transfers between devices  16.2 us (24%)
    all_to_all x1, waiting for transfers between devices, local(): lax.all_to_all(packed, 're', split_axis=0, concat_axis=0, tiled=True)  21.5 us
    pallas_call x1, Pallas kernels, local(): pl.pallas_call(final_kernel, in_specs=[hbm, hbm, hbm, pl.BlockSpec(memory...  8.18 us
    all_to_all x1, starting transfers between devices, local(): lax.all_to_all(requests, 're', split_axis=0, concat_axis=0, tiled=True)  8.04 us
    all_to_all x1, waiting for transfers between devices, local(): lax.all_to_all(requests, 're', split_axis=0, concat_axis=0, tiled=True)  6.36 us
    pallas_call x1, Pallas kernels, local(): pl.pallas_call(phase_kernel, grid=(TILES,), in_specs=[whole((3, RE)), pl....  5.63 us
    ppermute x3, starting transfers between devices, local(): lax.ppermute(parts[s].reshape(ROWS, LANES), 'rp', [(j, j ^ s) for j in ra...  4.18 us
    all_to_all x1, starting transfers between devices, local(): lax.all_to_all(packed, 're', split_axis=0, concat_axis=0, tiled=True)  4 us
    pallas_call x1, Pallas kernels, local(): pl.pallas_call(mix_kernel, grid=(RE_LOCAL // chunk,), in_specs=[smem(), s...  3.2 us
  transfers between devices with their start and end apart: 5, of which 2 were waited for; matrix products, arithmetic and copies ran while one was open for 0% of the time, Pallas kernels for 14%

profile of v4, /device:TPU:0, one launch (start us, length us, event | category | flops | bytes accessed | tf_op | source)
XLA Modules:
  0.0 67.3 jit_solution(720910971713386887)
XLA Ops:
  0.0 0.0 copy-start
  0.0 3.2 %mix.1 = (bf16[6,32,128]{2,1,0:T(8,128)(2,1)S(1)}, bf16[6,32,128]{2,1,0:T(8,128)(2,1)S(1)}, bf16[6,32,128]{2,1,0:T(8,128)(2,1)S(1)}, bf16[6,32,128]{2,1,0:T(8,128)(2,1)S(1)}) custom-call(f32[12,2,12]{2,1,0:T(2,128)} %bitcast.13, s32[2,3]{1,0:T(2,128)} %bitcast.15, s32[1]{0:T(128)} %bitcast.3.rank_ref, s32[3,32]{1,0:T(4,128)} %rp_ref.1, ...), custom_call_target="tpu_custom_call" | custom-call | tf_op jit(solution)/shard_map/mix/pallas_call | solution.py:264
  3.2 0.1 collective-permute-start
  3.3 4.0 %collective-permute-start.1 = (bf16[192,128]{1,0:T(8,128)(2,1)S(1)}, bf16[192,128]{1,0:T(8,128)(2,1)S(1)}, u32[]{:S(2)}, u32[]{:S(2)}) collective-permute-start(bf16[192,128]{1,0:T(8,128)(2,1)S(1)} %bitcast.11), channel_id=1, source_target_pairs={{0,2},{1,3},{2,0},{3,1},{4,6},{5,7},{6,4},{7,5},{8,10},{9,11},{10,... | collective-permute-start | bytes 147464 | tf_op jit(solution)/shard_map/ppermute | solution.py:287
  7.3 0.1 collective-permute-start.2
  7.4 1.9 %requests.1 = (s32[32,1,128]{2,1,0:T(1,128)}, s32[2,512]{1,0:T(2,128)S(1)}) custom-call(s32[2,1,512]{2,1,0:T(1,128)} %bitcast.14, s32[2,512]{1,0:T(2,128)} %row_ref.1), custom_call_target="tpu_custom_call" | custom-call | tf_op jit(solution)/shard_map/requests/pallas_call | solution.py:291
  9.3 8.0 %all-to-all-start = ((s32[32,1,128]{2,1,0:T(1,128)}), s32[32,1,128]{2,1,0:T(1,128)S(1)}, u32[]{:S(2)}, u32[]{:S(2)}) async-start(s32[32,1,128]{2,1,0:T(1,128)} %get-tuple-element.22), calls=%async_computation | async-start | bytes 32768 | tf_op jit(solution)/shard_map/all_to_all | solution.py:300
  17.4 0.0 collective-permute-done.one_ref
  17.4 0.0 collective-permute-done.1.two_ref
  17.4 0.0 collective-permute-done.2.three_ref
  17.4 1.8 %sum.1.packed_ref = bf16[32,240,128]{2,1,0:T(8,128)(2,1)} custom-call(bf16[192,128]{1,0:T(8,128)(2,1)S(1)} %bitcast.9, bf16[192,128]{1,0:T(8,128)(2,1)S(1)} %collective-permute-done.one_ref, bf16[192,128]{1,0:T(8,128)(2,1)S(1)} %collective-permute-done.1.two_ref, bf16[192,128]{1,0:T(8,128)(2,1)S(1)} %collective-permute-done.2.three_ref), custom_call_target="tpu_custom_call" | custom-call | tf_op jit(solution)/shard_map/sum/pallas_call | solution.py:303
  19.2 6.4 %all-to-all-done.request_ref = s32[32,1,128]{2,1,0:T(1,128)S(1)} async-done(((s32[32,1,128]{2,1,0:T(1,128)}), s32[32,1,128]{2,1,0:T(1,128)S(1)}, u32[]{:S(2)}, u32[]{:S(2)}) %all-to-all-start) | async-done | bytes 16416 | tf_op jit(solution)/shard_map/all_to_all | solution.py:300
  25.6 0.0 copy-done
  25.6 2.5 %lookup.1 = bf16[32,240,128]{2,1,0:T(8,128)(2,1)} custom-call(bf16[32,240,128]{2,1,0:T(8,128)(2,1)} %sum.1.packed_ref, s32[32,1,128]{2,1,0:T(1,128)S(1)} %all-to-all-done.request_ref, bf16[512,128]{1,0:T(8,128)(2,1)S(1)} %copy-done), custom_call_target="tpu_custom_call", output_to_operand_aliasing={{}: (0, {})} | custom-call | tf_op jit(solution)/shard_map/lookup/pallas_call | solution.py:312
  28.1 4.0 %all-to-all-start.1 = ((bf16[32,240,128]{2,1,0:T(8,128)(2,1)}), bf16[32,240,128]{2,1,0:T(8,128)(2,1)S(1)}, u32[]{:S(2)}, u32[]{:S(2)}) async-start(bf16[32,240,128]{2,1,0:T(8,128)(2,1)} %lookup.1), calls=%async_computation.1 | async-start | bytes 3932160 | tf_op jit(solution)/shard_map/all_to_all | solution.py:326
  32.1 5.6 %phase.1 = (bf16[4,1024,256]{2,1,0:T(8,128)(2,1)}, bf16[2,768,512]{2,1,0:T(8,128)(2,1)}, f32[192,512]{1,0:T(8,128)}) custom-call(s32[3,1024]{1,0:T(4,128)} %re_ref.1, s32[3,512]{1,0:T(4,128)} %k_ref.1, s32[2,512]{1,0:T(2,128)S(1)} %get-tuple-element.14.slot_ref, bf16[512,128]{1,0:T(8,128)(2,1)} %rotations_ref.3), custom_call_target="tpu_custom_call" | custom-call | tf_op jit(solution)/shard_map/phase/pallas_call | solution.py:328
  37.7 21.5 %all-to-all-done.1.gathered_ref = bf16[32,240,128]{2,1,0:T(8,128)(2,1)S(1)} async-done(((bf16[32,240,128]{2,1,0:T(8,128)(2,1)}), bf16[32,240,128]{2,1,0:T(8,128)(2,1)S(1)}, u32[]{:S(2)}, u32[]{:S(2)}) %all-to-all-start.1) | async-done | bytes 1966112 | tf_op jit(solution)/shard_map/all_to_all | solution.py:326
  59.2 8.2 %final.1 = bf16[6,2,64,512]{3,2,1,0:T(8,128)(2,1)} custom-call(bf16[4,1024,256]{2,1,0:T(8,128)(2,1)} %get-tuple-element.15.phase_hbm, bf16[2,768,512]{2,1,0:T(8,128)(2,1)} %get-tuple-element.16.pick_hbm, f32[192,512]{1,0:T(8,128)} %get-tuple-element.17.near_hbm, bf16[32,240,128]{2,1,0:T(8,128)(2,1)S(1)} %all-to-all-done.1.gathered_ref), custom_call_target="tpu_custom_call" | custom-call | tf_op jit(solution)/shard_map/final/pallas_call | solution.py:352
Async XLA Ops:
  0.0 25.6 %copy-start = (bf16[512,128]{1,0:T(8,128)(2,1)S(1)}, bf16[512,128]{1,0:T(8,128)(2,1)}, u32[]{:S(2)}) copy-start(bf16[512,128]{1,0:T(8,128)(2,1)} %rotations_ref.3) | copy-start | bytes 393220
  3.2 14.2 %collective-permute-start = (bf16[192,128]{1,0:T(8,128)(2,1)S(1)}, bf16[192,128]{1,0:T(8,128)(2,1)S(1)}, u32[]{:S(2)}, u32[]{:S(2)}) collective-permute-start(bf16[192,128]{1,0:T(8,128)(2,1)S(1)} %bitcast.12), channel_id=1, source_target_pairs={{0,1},{1,0},{2,3},{3,2},{4,5},{5,4},{6,7},{7,6},{8,9},{9,8},{10,11... | collective-permute-start | bytes 147464 | tf_op jit(solution)/shard_map/ppermute | solution.py:287
  3.3 14.1 %collective-permute-start.1 = (bf16[192,128]{1,0:T(8,128)(2,1)S(1)}, bf16[192,128]{1,0:T(8,128)(2,1)S(1)}, u32[]{:S(2)}, u32[]{:S(2)}) collective-permute-start(bf16[192,128]{1,0:T(8,128)(2,1)S(1)} %bitcast.11), channel_id=1, source_target_pairs={{0,2},{1,3},{2,0},{3,1},{4,6},{5,7},{6,4},{7,5},{8,10},{9,11},{10,... | collective-permute-start | bytes 147464 | tf_op jit(solution)/shard_map/ppermute | solution.py:287
  7.3 10.1 %collective-permute-start.2 = (bf16[192,128]{1,0:T(8,128)(2,1)S(1)}, bf16[192,128]{1,0:T(8,128)(2,1)S(1)}, u32[]{:S(2)}, u32[]{:S(2)}) collective-permute-start(bf16[192,128]{1,0:T(8,128)(2,1)S(1)} %bitcast.10), channel_id=1, source_target_pairs={{0,3},{1,2},{2,1},{3,0},{4,7},{5,6},{6,5},{7,4},{8,11},{9,10},{10,... | collective-permute-start | bytes 147464 | tf_op jit(solution)/shard_map/ppermute | solution.py:287
  9.3 16.2 %all-to-all-start = ((s32[32,1,128]{2,1,0:T(1,128)}), s32[32,1,128]{2,1,0:T(1,128)S(1)}, u32[]{:S(2)}, u32[]{:S(2)}) async-start(s32[32,1,128]{2,1,0:T(1,128)} %get-tuple-element.22), calls=%async_computation | async-start | bytes 32768 | tf_op jit(solution)/shard_map/all_to_all | solution.py:300
  28.1 31.1 %all-to-all-start.1 = ((bf16[32,240,128]{2,1,0:T(8,128)(2,1)}), bf16[32,240,128]{2,1,0:T(8,128)(2,1)S(1)}, u32[]{:S(2)}, u32[]{:S(2)}) async-start(bf16[32,240,128]{2,1,0:T(8,128)(2,1)} %lookup.1), calls=%async_computation.1 | async-start | bytes 3932160 | tf_op jit(solution)/shard_map/all_to_all | solution.py:326

commit v5 on v4

--- a/solution.py
+++ b/solution.py
@@ -24,6 +24,7 @@
 PACK = ROWS + SLOTS
 LANES = 128
 TILES = K // LANES
+FIRST = 2
 SIZE = NB * NB
 TURN = 2.0 * math.pi
 SINE = [TURN ** n * s / math.factorial(n) for n, s in ((1, 1), (3, -1), (5, 1), (7, -1), (9, 1), (11, -1))]
@@ -131,19 +132,14 @@
     out_ref[...] = found.reshape(peers, SLOTS, LANES).astype(BF)
 
 
-def phase_kernel(re_ref, k_ref, slot_ref, rotations_ref, out_ref, pick_ref, near_ref):
+def phase_kernel(re_ref, k_ref, out_ref):
     left = re_ref[...].astype(F32).astype(BF)
-    right = k_ref[...].astype(F32).astype(BF)
-    products = lax.dot_general(left, right, (((0,), (0,)), ((), ())), preferred_element_type=F32)
-    cosine, sine = cos_sin(products)
-    out_ref[0, :, :LANES] = cosine.astype(BF)
-    out_ref[0, :, LANES:] = sine.astype(BF)
-    place = lax.broadcasted_iota(I32, (N_RE * CAP, LANES), 0)
-    for q in range(Q):
-        pick_ref[q] = (place == slot_ref[q : q + 1, :]).astype(F32).astype(BF)
-    near = rotations_ref[...].astype(F32).T
-    near_ref[: 2 * SIZE] = near
-    near_ref[2 * SIZE :] = near[:SIZE] + near[SIZE:]
+    for t in range(out_ref.shape[0]):
+        right = k_ref[:, t * LANES : (t + 1) * LANES].astype(F32).astype(BF)
+        products = lax.dot_general(left, right, (((0,), (0,)), ((), ())), preferred_element_type=F32)
+        cosine, sine = cos_sin(products)
+        out_ref[t, :, :LANES] = cosine.astype(BF)
+        out_ref[t, :, LANES:] = sine.astype(BF)
 
 
 def chain(terms):
@@ -179,50 +175,45 @@
 
 
 def final_kernel(
-    phase_hbm, pick_hbm, near_hbm, gathered_ref, out_hbm,
-    phase_ref, pick_ref, near_ref, turned_ref, far_ref, coupling_ref, out_ref, phase_sem, pick_sem, near_sem, out_sem,
+    slot_ref, rotations_ref, first_ref, later_hbm, gathered_ref, out_hbm,
+    later_ref, near_ref, turned_ref, far_ref, coupling_ref, out_ref, later_sem, out_sem,
 ):
-    phase_copies = [pltpu.make_async_copy(phase_hbm.at[t], phase_ref.at[t], phase_sem.at[t]) for t in range(TILES)]
-    pick_copy = pltpu.make_async_copy(pick_hbm, pick_ref, pick_sem)
-    near_copy = pltpu.make_async_copy(near_hbm, near_ref, near_sem)
+    later = [pltpu.make_async_copy(later_hbm.at[t], later_ref.at[t], later_sem.at[t]) for t in range(TILES - FIRST)]
     out_copies = [
         pltpu.make_async_copy(out_ref.at[t], out_hbm.at[:, :, :, t * LANES : (t + 1) * LANES], out_sem.at[t])
         for t in range(TILES)
     ]
-    pick_copy.start()
-    phase_copies[0].start()
-    near_copy.start()
-    for t in range(1, TILES):
-        phase_copies[t].start()
+    for copy in later:
+        copy.start()
+    near = rotations_ref[...].astype(F32).T
+    near_ref[: 2 * SIZE] = near
+    near_ref[2 * SIZE :] = near[:SIZE] + near[SIZE:]
     replies = gathered_ref[:, ROWS:, :].astype(F32)
-    turned = []
+    place = lax.broadcasted_iota(I32, (N_RE * CAP, K), 0)
     for q in range(Q):
         rows = replies[:, q * CAP : (q + 1) * CAP, :].reshape(N_RE * CAP, LANES)
-        turned.append(rows.T.astype(BF))
+        one_hot = (place == slot_ref[q : q + 1, :]).astype(F32).astype(BF)
+        far = jnp.dot(rows.T.astype(BF), one_hot, preferred_element_type=F32)
+        far_ref[q, : 2 * SIZE] = far
+        far_ref[q, 2 * SIZE :] = far[:SIZE] - far[SIZE:]
     for i in range(Q * M_LOCAL):
         block = gathered_ref[:, i * RE_LOCAL : (i + 1) * RE_LOCAL, :].reshape(RE, LANES)
         turned_ref[i] = block.T
-    pick_copy.wait()
-    for q in range(Q):
-        far = jnp.dot(turned[q], pick_ref[q], preferred_element_type=F32)
-        far_ref[q, : 2 * SIZE] = far
-        far_ref[q, 2 * SIZE :] = far[:SIZE] - far[SIZE:]
 
     def couple(t, i):
-        both = jnp.dot(turned_ref[i], phase_ref[t], preferred_element_type=F32)
+        phase = first_ref[t] if t < FIRST else later_ref[t - FIRST]
+        both = jnp.dot(turned_ref[i], phase, preferred_element_type=F32)
         real = both[:SIZE, :LANES] - both[SIZE:, LANES:]
         imag = both[:SIZE, LANES:] + both[SIZE:, :LANES]
         coupling_ref[t % 2, i, :SIZE] = real
         coupling_ref[t % 2, i, SIZE : 2 * SIZE] = imag
         coupling_ref[t % 2, i, 2 * SIZE :] = real + imag
 
-    phase_copies[0].wait()
     for i in range(Q * M_LOCAL):
         couple(0, i)
-    near_copy.wait()
     for t in range(TILES):
-        if t + 1 < TILES:
-            phase_copies[t + 1].wait()
+        if FIRST <= t + 1 < TILES:
+            later[t + 1 - FIRST].wait()
         for i in range(Q * M_LOCAL):
             if t + 1 < TILES:
                 couple(t + 1, i)
@@ -311,13 +302,13 @@
     )(own, *others)
     packed = pl.pallas_call(
         lookup_kernel,
-        grid=(N_RE // peers,),
+        grid=(1,),
         in_specs=[
             pl.BlockSpec(memory_space=pltpu.HBM),
-            pl.BlockSpec((peers, 1, LANES), lambda i: (i, 0, 0)),
-            whole((K, LANES)),
+            pl.BlockSpec(memory_space=pltpu.VMEM),
+            pl.BlockSpec(memory_space=pltpu.VMEM),
         ],
-        out_specs=pl.BlockSpec((peers, SLOTS, LANES), lambda i: (i, ROWS // SLOTS, 0)),
+        out_specs=pl.BlockSpec((N_RE, SLOTS, LANES), lambda i: (0, ROWS // SLOTS, 0)),
         out_shape=pltpu.HBM((N_RE, PACK, LANES), BF),
         input_output_aliases={0: 0},
         compiler_params=params(8),
@@ -325,51 +316,38 @@
     )(spread, wanted, rotations)
     gathered = lax.all_to_all(packed, "re", split_axis=0, concat_axis=0, tiled=True)
 
-    phases, picks, near = pl.pallas_call(
-        phase_kernel,
-        grid=(TILES,),
-        in_specs=[
-            whole((3, RE)),
-            pl.BlockSpec((3, LANES), lambda t: (0, t)),
-            pl.BlockSpec((Q, LANES), lambda t: (0, t)),
-            pl.BlockSpec((LANES, LANES), lambda t: (t, 0)),
-        ],
-        out_specs=[
-            pl.BlockSpec((1, RE, 2 * LANES), lambda t: (t, 0, 0)),
-            pl.BlockSpec((Q, N_RE * CAP, LANES), lambda t: (0, 0, t)),
-            pl.BlockSpec((3 * SIZE, LANES), lambda t: (0, t)),
-        ],
-        out_shape=[
-            pltpu.HBM((TILES, RE, 2 * LANES), BF),
-            pltpu.HBM((Q, N_RE * CAP, K), BF),
-            pltpu.HBM((3 * SIZE, K), F32),
-        ],
-        compiler_params=params(16),
-        name="phase",
-    )(in_hbm(re_coords), in_hbm(k_coords), slots, in_hbm(rotations))
+    def phase_tiles(coords, space):
+        tiles = coords.shape[1] // LANES
+        return pl.pallas_call(
+            phase_kernel,
+            out_shape=space((tiles, RE, 2 * LANES), BF),
+            compiler_params=params(16),
+            name="phase",
+        )(in_hbm(re_coords), in_hbm(coords))
+
+    first = phase_tiles(k_coords[:, : FIRST * LANES], pltpu.VMEM)
+    later = phase_tiles(k_coords[:, FIRST * LANES :], pltpu.HBM)
 
     hbm = pl.BlockSpec(memory_space=pltpu.HBM)
+    vmem = pl.BlockSpec(memory_space=pltpu.VMEM)
     result = pl.pallas_call(
         final_kernel,
-        in_specs=[hbm, hbm, hbm, pl.BlockSpec(memory_space=pltpu.VMEM)],
+        in_specs=[vmem, vmem, vmem, hbm, vmem],
         out_specs=hbm,
         out_shape=jax.ShapeDtypeStruct((Q * M_LOCAL, 2, SIZE, K), BF),
         scratch_shapes=[
-            pltpu.VMEM((TILES, RE, 2 * LANES), BF),
-            pltpu.VMEM((Q, N_RE * CAP, K), BF),
+            pltpu.VMEM((TILES - FIRST, RE, 2 * LANES), BF),
             pltpu.VMEM((3 * SIZE, K), F32),
             pltpu.VMEM((Q * M_LOCAL, LANES, RE), BF),
             pltpu.VMEM((Q, 3 * SIZE, K), F32),
             pltpu.VMEM((2, Q * M_LOCAL, 3 * SIZE, LANES), F32),
             pltpu.VMEM((TILES, Q * M_LOCAL, 2, SIZE, LANES), BF),
-            pltpu.SemaphoreType.DMA((TILES,)),
-            pltpu.SemaphoreType.DMA,
-            pltpu.SemaphoreType.DMA,
+            pltpu.SemaphoreType.DMA((TILES - FIRST,)),
             pltpu.SemaphoreType.DMA((TILES,)),
         ],
         compiler_params=params(24),
         name="final",
-    )(in_hbm(phases), in_hbm(picks), in_hbm(near), gathered)
+    )(slots, rotations, first, in_hbm(later), gathered)
     return result.reshape(Q, M_LOCAL, 2, NB * NB, K)
 
 

time: 67.7 us -> 65.5 us (0.968)
  Pallas kernels: 23.2 us -> 20.6 us
    pallas_call x3 -> x4, Pallas kernels: 16.3 us -> 13.6 us  [the longest x1 6.76 us: local(): pl.pallas_call(final_kernel, in_specs=[vmem, vmem, vmem, hbm, vmem], out_...]
  transfers between devices with their start and end apart: 5 -> 5, of which waited for: 2 -> 2; matrix products, arithmetic and copies ran while one was open for 0% -> 1% of each run, Pallas kernels for 14% -> 14%
where the time goes in v5:
time: 65.5 us; the launch traced here: 65 us
  waiting for transfers between devices  27.4 us (42%)
  Pallas kernels  20.6 us (31%)
  starting transfers between devices  16.4 us (25%)
    all_to_all x1, waiting for transfers between devices, local(): lax.all_to_all(packed, 're', split_axis=0, concat_axis=0, tiled=True)  21.1 us
    all_to_all x1, starting transfers between devices, local(): lax.all_to_all(requests, 're', split_axis=0, concat_axis=0, tiled=True)  8.04 us
    pallas_call x1, Pallas kernels, local(): pl.pallas_call(final_kernel, in_specs=[vmem, vmem, vmem, hbm, vmem], out_...  6.76 us
    all_to_all x1, waiting for transfers between devices, local(): lax.all_to_all(requests, 're', split_axis=0, concat_axis=0, tiled=True)  6.32 us
    pallas_call x2, Pallas kernels, phase_tiles(): pl.pallas_call(phase_kernel, out_shape=space((tiles, RE, 2 * LANES), BF),...  5.39 us
    ppermute x3, starting transfers between devices, local(): lax.ppermute(parts[s].reshape(ROWS, LANES), 'rp', [(j, j ^ s) for j in ra...  4.18 us
    all_to_all x1, starting transfers between devices, local(): lax.all_to_all(packed, 're', split_axis=0, concat_axis=0, tiled=True)  4.13 us
    pallas_call x1, Pallas kernels, local(): pl.pallas_call(mix_kernel, grid=(RE_LOCAL // chunk,), in_specs=[smem(), s...  3.2 us
  transfers between devices with their start and end apart: 5, of which 2 were waited for; matrix products, arithmetic and copies ran while one was open for 1% of the time, Pallas kernels for 14%

profile of v5, /device:TPU:0, one launch (start us, length us, event | category | flops | bytes accessed | tf_op | source)
XLA Modules:
  0.0 65.0 jit_solution(13852535333736768852)
XLA Ops:
  0.0 0.0 copy-start
  0.0 3.2 %mix.1 = (bf16[6,32,128]{2,1,0:T(8,128)(2,1)S(1)}, bf16[6,32,128]{2,1,0:T(8,128)(2,1)S(1)}, bf16[6,32,128]{2,1,0:T(8,128)(2,1)S(1)}, bf16[6,32,128]{2,1,0:T(8,128)(2,1)S(1)}) custom-call(f32[12,2,12]{2,1,0:T(2,128)} %bitcast.13, s32[2,3]{1,0:T(2,128)} %bitcast.15, s32[1]{0:T(128)} %bitcast.3.rank_ref, s32[3,32]{1,0:T(4,128)} %rp_ref.1, ...), custom_call_target="tpu_custom_call" | custom-call | tf_op jit(solution)/shard_map/mix/pallas_call | solution.py:255
  3.2 0.1 collective-permute-start
  3.3 4.0 %collective-permute-start.1 = (bf16[192,128]{1,0:T(8,128)(2,1)S(1)}, bf16[192,128]{1,0:T(8,128)(2,1)S(1)}, u32[]{:S(2)}, u32[]{:S(2)}) collective-permute-start(bf16[192,128]{1,0:T(8,128)(2,1)S(1)} %bitcast.11), channel_id=1, source_target_pairs={{0,2},{1,3},{2,0},{3,1},{4,6},{5,7},{6,4},{7,5},{8,10},{9,11},{10,... | collective-permute-start | bytes 147464 | tf_op jit(solution)/shard_map/ppermute | solution.py:278
  7.3 0.1 collective-permute-start.2
  7.4 1.9 %requests.1 = (s32[32,1,128]{2,1,0:T(1,128)}, s32[2,512]{1,0:T(2,128)S(1)}) custom-call(s32[2,1,512]{2,1,0:T(1,128)} %bitcast.14, s32[2,512]{1,0:T(2,128)} %row_ref.1), custom_call_target="tpu_custom_call" | custom-call | tf_op jit(solution)/shard_map/requests/pallas_call | solution.py:282
  9.3 8.0 %all-to-all-start = ((s32[32,1,128]{2,1,0:T(1,128)}), s32[32,1,128]{2,1,0:T(1,128)S(1)}, u32[]{:S(2)}, u32[]{:S(2)}) async-start(s32[32,1,128]{2,1,0:T(1,128)} %get-tuple-element.16), calls=%async_computation | async-start | bytes 32768 | tf_op jit(solution)/shard_map/all_to_all | solution.py:291
  17.4 0.0 collective-permute-done.one_ref
  17.4 0.0 collective-permute-done.1.two_ref
  17.4 0.0 collective-permute-done.2.three_ref
  17.4 1.8 %sum.1.packed_ref = bf16[32,240,128]{2,1,0:T(8,128)(2,1)} custom-call(bf16[192,128]{1,0:T(8,128)(2,1)S(1)} %bitcast.9, bf16[192,128]{1,0:T(8,128)(2,1)S(1)} %collective-permute-done.one_ref, bf16[192,128]{1,0:T(8,128)(2,1)S(1)} %collective-permute-done.1.two_ref, bf16[192,128]{1,0:T(8,128)(2,1)S(1)} %collective-permute-done.2.three_ref), custom_call_target="tpu_custom_call" | custom-call | tf_op jit(solution)/shard_map/sum/pallas_call | solution.py:294
  19.2 6.3 %all-to-all-done.request_ref = s32[32,1,128]{2,1,0:T(1,128)S(1)} async-done(((s32[32,1,128]{2,1,0:T(1,128)}), s32[32,1,128]{2,1,0:T(1,128)S(1)}, u32[]{:S(2)}, u32[]{:S(2)}) %all-to-all-start) | async-done | bytes 16416 | tf_op jit(solution)/shard_map/all_to_all | solution.py:291
  25.6 0.0 copy-done
  25.6 1.5 %lookup.1 = bf16[32,240,128]{2,1,0:T(8,128)(2,1)} custom-call(bf16[32,240,128]{2,1,0:T(8,128)(2,1)} %sum.1.packed_ref, s32[32,1,128]{2,1,0:T(1,128)S(1)} %all-to-all-done.request_ref, bf16[512,128]{1,0:T(8,128)(2,1)S(1)} %copy-done), custom_call_target="tpu_custom_call", output_to_operand_aliasing={{}: (0, {})} | custom-call | tf_op jit(solution)/shard_map/lookup/pallas_call | solution.py:303
  27.0 0.0 copy-start.1
  27.0 4.1 %all-to-all-start.1 = ((bf16[32,240,128]{2,1,0:T(8,128)(2,1)}), bf16[32,240,128]{2,1,0:T(8,128)(2,1)S(1)}, u32[]{:S(2)}, u32[]{:S(2)}) async-start(bf16[32,240,128]{2,1,0:T(8,128)(2,1)} %lookup.1), calls=%async_computation.1 | async-start | bytes 3932160 | tf_op jit(solution)/shard_map/all_to_all | solution.py:317
  31.2 0.0 copy-done.1
  31.2 0.6 fusion
  31.8 2.2 %phase.2.first_ref = bf16[2,1024,256]{2,1,0:T(8,128)(2,1)S(1)} custom-call(s32[3,1024]{1,0:T(4,128)} %re_ref.3, s32[3,256]{1,0:T(4,128)} %get-tuple-element.18.k_ref), custom_call_target="tpu_custom_call" | custom-call | tf_op jit(solution)/shard_map/phase/pallas_call | solution.py:321
  34.0 3.2 %phase.3.later_hbm = bf16[2,1024,256]{2,1,0:T(8,128)(2,1)} custom-call(s32[3,1024]{1,0:T(4,128)} %re_ref.3, s32[3,256]{1,0:T(4,128)} %get-tuple-element.17.k_ref), custom_call_target="tpu_custom_call" | custom-call | tf_op jit(solution)/shard_map/phase/pallas_call | solution.py:321
  37.2 21.1 %all-to-all-done.1.gathered_ref = bf16[32,240,128]{2,1,0:T(8,128)(2,1)S(1)} async-done(((bf16[32,240,128]{2,1,0:T(8,128)(2,1)}), bf16[32,240,128]{2,1,0:T(8,128)(2,1)S(1)}, u32[]{:S(2)}, u32[]{:S(2)}) %all-to-all-start.1) | async-done | bytes 1966112 | tf_op jit(solution)/shard_map/all_to_all | solution.py:317
  58.3 6.8 %final.1 = bf16[6,2,64,512]{3,2,1,0:T(8,128)(2,1)} custom-call(s32[2,512]{1,0:T(2,128)S(1)} %get-tuple-element.11.slot_ref, bf16[512,128]{1,0:T(8,128)(2,1)S(1)} %copy-done, bf16[2,1024,256]{2,1,0:T(8,128)(2,1)S(1)} %phase.2.first_ref, bf16[2,1024,256]{2,1,0:T(8,128)(2,1)} %phase.3.later_hbm, bf16[32,240,128]{2,1,0:T(8,128)(2,1)S(1)} %all-to-all-done.1.gathered_ref), custom_call_target="tpu_custom_call" | custom-call | tf_op jit(solution)/shard_map/final/pallas_call | solution.py:333
Async XLA Ops:
  0.0 25.6 %copy-start = (bf16[512,128]{1,0:T(8,128)(2,1)S(1)}, bf16[512,128]{1,0:T(8,128)(2,1)}, u32[]{:S(2)}) copy-start(bf16[512,128]{1,0:T(8,128)(2,1)} %rotations_ref.3) | copy-start | bytes 393220
  3.2 14.2 %collective-permute-start = (bf16[192,128]{1,0:T(8,128)(2,1)S(1)}, bf16[192,128]{1,0:T(8,128)(2,1)S(1)}, u32[]{:S(2)}, u32[]{:S(2)}) collective-permute-start(bf16[192,128]{1,0:T(8,128)(2,1)S(1)} %bitcast.12), channel_id=1, source_target_pairs={{0,1},{1,0},{2,3},{3,2},{4,5},{5,4},{6,7},{7,6},{8,9},{9,8},{10,11... | collective-permute-start | bytes 147464 | tf_op jit(solution)/shard_map/ppermute | solution.py:278
  3.3 14.1 %collective-permute-start.1 = (bf16[192,128]{1,0:T(8,128)(2,1)S(1)}, bf16[192,128]{1,0:T(8,128)(2,1)S(1)}, u32[]{:S(2)}, u32[]{:S(2)}) collective-permute-start(bf16[192,128]{1,0:T(8,128)(2,1)S(1)} %bitcast.11), channel_id=1, source_target_pairs={{0,2},{1,3},{2,0},{3,1},{4,6},{5,7},{6,4},{7,5},{8,10},{9,11},{10,... | collective-permute-start | bytes 147464 | tf_op jit(solution)/shard_map/ppermute | solution.py:278
  7.3 10.1 %collective-permute-start.2 = (bf16[192,128]{1,0:T(8,128)(2,1)S(1)}, bf16[192,128]{1,0:T(8,128)(2,1)S(1)}, u32[]{:S(2)}, u32[]{:S(2)}) collective-permute-start(bf16[192,128]{1,0:T(8,128)(2,1)S(1)} %bitcast.10), channel_id=1, source_target_pairs={{0,3},{1,2},{2,1},{3,0},{4,7},{5,6},{6,5},{7,4},{8,11},{9,10},{10,... | collective-permute-start | bytes 147464 | tf_op jit(solution)/shard_map/ppermute | solution.py:278
  9.3 16.2 %all-to-all-start = ((s32[32,1,128]{2,1,0:T(1,128)}), s32[32,1,128]{2,1,0:T(1,128)S(1)}, u32[]{:S(2)}, u32[]{:S(2)}) async-start(s32[32,1,128]{2,1,0:T(1,128)} %get-tuple-element.16), calls=%async_computation | async-start | bytes 32768 | tf_op jit(solution)/shard_map/all_to_all | solution.py:291
  27.0 4.1 %copy-start.1 = (s32[3,512]{1,0:T(4,128)S(1)}, s32[3,512]{1,0:T(4,128)}, u32[]{:S(2)}) copy-start(s32[3,512]{1,0:T(4,128)} %param.14) | copy-start | bytes 18436
  27.0 31.2 %all-to-all-start.1 = ((bf16[32,240,128]{2,1,0:T(8,128)(2,1)}), bf16[32,240,128]{2,1,0:T(8,128)(2,1)S(1)}, u32[]{:S(2)}, u32[]{:S(2)}) async-start(bf16[32,240,128]{2,1,0:T(8,128)(2,1)} %lookup.1), calls=%async_computation.1 | async-start | bytes 3932160 | tf_op jit(solution)/shard_map/all_to_all | solution.py:317

commit v6 on v5

--- a/solution.py
+++ b/solution.py
@@ -25,6 +25,7 @@
 LANES = 128
 TILES = K // LANES
 FIRST = 2
+PIECES = 8
 SIZE = NB * NB
 TURN = 2.0 * math.pi
 SINE = [TURN ** n * s / math.factorial(n) for n, s in ((1, 1), (3, -1), (5, 1), (7, -1), (9, 1), (11, -1))]
@@ -52,7 +53,7 @@
     return cosine, sine
 
 
-def requests_kernel(owner_ref, row_ref, request_ref, slot_ref):
+def find_requests(owner_ref, row_ref, request_ref, slot_ref):
     before = (lax.broadcasted_iota(I32, (K, K), 0) < lax.broadcasted_iota(I32, (K, K), 1)).astype(F32).astype(BF)
     total = jnp.zeros((N_RE, LANES), F32)
     for q in range(Q):
@@ -61,9 +62,9 @@
         hit = lax.broadcasted_iota(I32, (N_RE, K), 0) == owner
         one_hot = hit.astype(F32)
         earlier = jnp.dot(one_hot.astype(BF), before, preferred_element_type=F32)
-        rank = jnp.sum(one_hot * earlier, axis=0, keepdims=True).astype(I32) + q * CAP
-        slot_ref[q : q + 1, :] = owner * CAP + rank - q * CAP
-        place = (lax.broadcasted_iota(I32, (LANES, K), 0) == rank).astype(F32).astype(BF)
+        rank = jnp.sum(one_hot * earlier, axis=0, keepdims=True).astype(I32)
+        slot_ref[q : q + 1, :] = owner * CAP + rank
+        place = (lax.broadcasted_iota(I32, (LANES, K), 0) == rank + q * CAP).astype(F32).astype(BF)
         high = (one_hot * (row >> 4).astype(F32)).astype(BF)
         low = (one_hot * (row & 15).astype(F32)).astype(BF)
         contract = (((1,), (1,)), ((), ()))
@@ -74,7 +75,21 @@
         request_ref[o] = total[o : o + 1, :]
 
 
-def mix_kernel(mode_ref, q_ref, rank_ref, rp_ref, table_ref, *out_refs):
+def mix_kernel(
+    mode_ref, q_ref, rank_ref, rp_ref, owner_ref, row_ref, table_hbm,
+    own_ref, one_ref, two_ref, three_ref, request_ref, slot_ref, table_ref, sem,
+):
+    out_refs = own_ref, one_ref, two_ref, three_ref
+    piece = RE_LOCAL // PIECES
+    copies = [
+        pltpu.make_async_copy(
+            table_hbm.at[c * piece : (c + 1) * piece], table_ref.at[c * piece : (c + 1) * piece], sem.at[c]
+        )
+        for c in range(PIECES)
+    ]
+    for copy in copies:
+        copy.start()
+    find_requests(owner_ref, row_ref, request_ref, slot_ref)
     group = 8
     width = group * RP_LOCAL
     coords = jnp.concatenate([rp_ref[...]] * group, axis=1)
@@ -90,37 +105,46 @@
     half = MODES * NB * NB
     low_lanes = lax.broadcasted_iota(I32, (group, LANES), 1) < LANES // 2
     rank = rank_ref[0]
-    parts = [[[] for _ in range(Q * M_LOCAL)] for _ in range(N_RP)]
-    for h in range(table_ref.shape[0] // group):
-        values = table_ref[h * group : (h + 1) * group].reshape(width, 2 * half)
-        sums = jnp.dot(left, values, preferred_element_type=F32)
-        for q in range(Q):
-            with_cos = sums[q * group : (q + 1) * group]
-            with_sin = sums[(Q + q) * group : (Q + q + 1) * group]
-            packed = []
-            for p in range(MODES // 2):
-                re_lanes = slice(p * LANES, (p + 1) * LANES)
-                im_lanes = slice(half + p * LANES, half + (p + 1) * LANES)
-                real = with_cos[:, re_lanes] - with_sin[:, im_lanes]
-                imag = with_sin[:, re_lanes] + with_cos[:, im_lanes]
-                packed.append(jnp.where(low_lanes, real, pltpu.roll(imag, LANES // 2, 1)))
-                packed.append(jnp.where(low_lanes, pltpu.roll(real, LANES // 2, 1), imag))
-            for s in range(N_RP):
-                first = (rank ^ s) * M_LOCAL
-                for n in range(M_LOCAL):
-                    value = mode_ref[0, q, first + n] * packed[0]
-                    for mu in range(1, MODES):
-                        value += mode_ref[mu, q, first + n] * packed[mu]
-                    parts[s][q * M_LOCAL + n].append(value)
-    for s in range(N_RP):
-        for i in range(Q * M_LOCAL):
-            out_refs[s][i] = jnp.concatenate(parts[s][i], axis=0).astype(BF)
-
-
-def sum_kernel(own_ref, one_ref, two_ref, three_ref, out_ref):
+    for pair in range(RE_LOCAL // (2 * group)):
+        parts = [[[] for _ in range(Q * M_LOCAL)] for _ in range(N_RP)]
+        for h in (2 * pair, 2 * pair + 1):
+            for copy in copies[h * group // piece : (h + 1) * group // piece]:
+                copy.wait()
+            values = table_ref[h * group : (h + 1) * group].reshape(width, 2 * half)
+            sums = jnp.dot(left, values, preferred_element_type=F32)
+            for q in range(Q):
+                with_cos = sums[q * group : (q + 1) * group]
+                with_sin = sums[(Q + q) * group : (Q + q + 1) * group]
+                packed = []
+                for p in range(MODES // 2):
+                    re_lanes = slice(p * LANES, (p + 1) * LANES)
+                    im_lanes = slice(half + p * LANES, half + (p + 1) * LANES)
+                    real = with_cos[:, re_lanes] - with_sin[:, im_lanes]
+                    imag = with_sin[:, re_lanes] + with_cos[:, im_lanes]
+                    packed.append(jnp.where(low_lanes, real, pltpu.roll(imag, LANES // 2, 1)))
+                    packed.append(jnp.where(low_lanes, pltpu.roll(real, LANES // 2, 1), imag))
+                for s in range(N_RP):
+                    first = (rank ^ s) * M_LOCAL
+                    for n in range(M_LOCAL):
+                        value = mode_ref[0, q, first + n] * packed[0]
+                        for mu in range(1, MODES):
+                            value += mode_ref[mu, q, first + n] * packed[mu]
+                        parts[s][q * M_LOCAL + n].append(value)
+        rows = slice(pair * 2 * group, (pair + 1) * 2 * group)
+        for s in range(N_RP):
+            for i in range(Q * M_LOCAL):
+                out_refs[s][i, rows] = jnp.concatenate(parts[s][i], axis=0).astype(BF)
+
+
+def sum_kernel(own_ref, one_ref, two_ref, three_ref, out_hbm, total_ref, sem):
     total = own_ref[...].astype(F32) + one_ref[...].astype(F32)
     total += two_ref[...].astype(F32) + three_ref[...].astype(F32)
-    out_ref[...] = jnp.broadcast_to(total.astype(BF)[None], out_ref.shape)
+    total_ref[...] = total.astype(BF)
+    copies = [pltpu.make_async_copy(total_ref, out_hbm.at[p, :ROWS, :], sem.at[p]) for p in range(N_RE)]
+    for copy in copies:
+        copy.start()
+    for copy in copies:
+        copy.wait()
 
 
 def lookup_kernel(packed_ref, request_ref, rotations_ref, out_ref):
@@ -250,20 +274,17 @@
     kq_owner,
     kq_row,
 ):
-    chunk = 16
-    block = (Q * M_LOCAL, chunk, LANES)
-    parts = pl.pallas_call(
+    hbm = pl.BlockSpec(memory_space=pltpu.HBM)
+    vmem = pl.BlockSpec(memory_space=pltpu.VMEM)
+    *parts, requests, slots = pl.pallas_call(
         mix_kernel,
-        grid=(RE_LOCAL // chunk,),
-        in_specs=[
-            smem(),
-            smem(),
-            smem(),
-            whole((3, RP_LOCAL)),
-            pl.BlockSpec((chunk, RP_LOCAL, 2 * MODES * NB * NB), lambda i: (i, 0, 0)),
+        in_specs=[smem(), smem(), smem(), vmem, vmem, vmem, hbm],
+        out_shape=[jax.ShapeDtypeStruct((Q * M_LOCAL, RE_LOCAL, LANES), BF)] * N_RP
+        + [jax.ShapeDtypeStruct((N_RE, 1, LANES), I32), jax.ShapeDtypeStruct((Q, K), I32)],
+        scratch_shapes=[
+            pltpu.VMEM((RE_LOCAL, RP_LOCAL, 2 * MODES * SIZE), BF),
+            pltpu.SemaphoreType.DMA((PIECES,)),
         ],
-        out_specs=[pl.BlockSpec(block, lambda i: (0, i, 0))] * N_RP,
-        out_shape=[jax.ShapeDtypeStruct((Q * M_LOCAL, RE_LOCAL, LANES), BF)] * N_RP,
         compiler_params=params(16),
         name="mix",
     )(
@@ -271,6 +292,8 @@
         in_hbm(q_coords.T),
         lax.axis_index("rp").reshape(1),
         in_hbm(rp_coords),
+        in_hbm(kq_owner.transpose(0, 2, 1)),
+        in_hbm(kq_row),
         in_hbm(wannier_table),
     )
     own = parts[0].reshape(ROWS, LANES)
@@ -279,24 +302,14 @@
         for s in range(1, N_RP)
     ]
 
-    requests, slots = pl.pallas_call(
-        requests_kernel,
-        out_shape=(
-            jax.ShapeDtypeStruct((N_RE, 1, LANES), I32),
-            jax.ShapeDtypeStruct((Q, K), I32),
-        ),
-        compiler_params=params(16),
-        name="requests",
-    )(in_hbm(kq_owner.transpose(0, 2, 1)), in_hbm(kq_row))
     wanted = lax.all_to_all(requests, "re", split_axis=0, concat_axis=0, tiled=True)
 
-    peers = 8
     spread = pl.pallas_call(
         sum_kernel,
-        grid=(N_RE // peers,),
-        in_specs=[whole((ROWS, LANES))] * N_RP,
-        out_specs=pl.BlockSpec((peers, ROWS, LANES), lambda i: (i, 0, 0)),
+        in_specs=[vmem] * N_RP,
+        out_specs=hbm,
         out_shape=pltpu.HBM((N_RE, PACK, LANES), BF),
+        scratch_shapes=[pltpu.VMEM((ROWS, LANES), BF), pltpu.SemaphoreType.DMA((N_RE,))],
         compiler_params=params(8),
         name="sum",
     )(own, *others)
@@ -328,8 +341,6 @@
     first = phase_tiles(k_coords[:, : FIRST * LANES], pltpu.VMEM)
     later = phase_tiles(k_coords[:, FIRST * LANES :], pltpu.HBM)
 
-    hbm = pl.BlockSpec(memory_space=pltpu.HBM)
-    vmem = pl.BlockSpec(memory_space=pltpu.VMEM)
     result = pl.pallas_call(
         final_kernel,
         in_specs=[vmem, vmem, vmem, hbm, vmem],

time: 65.5 us -> 65.5 us (level)
    pallas_call x3 -> x2, Pallas kernels: 6.96 us -> 6.53 us  [the longest x1 5.02 us: local(): pl.pallas_call(mix_kernel, in_specs=[smem(), smem(), smem(), vmem, vmem,...]
  transfers between devices with their start and end apart: 5 -> 5, of which waited for: 2 -> 2; matrix products, arithmetic and copies ran while one was open for 1% -> 1% of each run, Pallas kernels for 14% -> 11%
where the time goes in v6:
time: 65.5 us; the launch traced here: 65.1 us
  waiting for transfers between devices  27.5 us (42%)
  Pallas kernels  20.2 us (31%)
  starting transfers between devices  16.5 us (25%)
    all_to_all x1, waiting for transfers between devices, local(): lax.all_to_all(packed, 're', split_axis=0, concat_axis=0, tiled=True)  20.9 us
    all_to_all x1, starting transfers between devices, local(): lax.all_to_all(requests, 're', split_axis=0, concat_axis=0, tiled=True)  8.05 us
    pallas_call x1, Pallas kernels, local(): pl.pallas_call(final_kernel, in_specs=[vmem, vmem, vmem, hbm, vmem], out_...  6.75 us
    all_to_all x1, waiting for transfers between devices, local(): lax.all_to_all(requests, 're', split_axis=0, concat_axis=0, tiled=True)  6.61 us
    pallas_call x2, Pallas kernels, phase_tiles(): pl.pallas_call(phase_kernel, out_shape=space((tiles, RE, 2 * LANES), BF),...  5.4 us
    pallas_call x1, Pallas kernels, local(): pl.pallas_call(mix_kernel, in_specs=[smem(), smem(), smem(), vmem, vmem,...  5.02 us
    all_to_all x1, starting transfers between devices, local(): lax.all_to_all(packed, 're', split_axis=0, concat_axis=0, tiled=True)  4.31 us
    ppermute x3, starting transfers between devices, local(): lax.ppermute(parts[s].reshape(ROWS, LANES), 'rp', [(j, j ^ s) for j in ra...  4.18 us
  transfers between devices with their start and end apart: 5, of which 2 were waited for; matrix products, arithmetic and copies ran while one was open for 1% of the time, Pallas kernels for 11%

profile of v6, /device:TPU:0, one launch (start us, length us, event | category | flops | bytes accessed | tf_op | source)
XLA Modules:
  0.0 65.1 jit_solution(5592689014350618885)
XLA Ops:
  0.0 0.0 copy-start
  0.0 5.0 %mix.1 = (bf16[6,32,128]{2,1,0:T(8,128)(2,1)S(1)}, bf16[6,32,128]{2,1,0:T(8,128)(2,1)S(1)}, bf16[6,32,128]{2,1,0:T(8,128)(2,1)S(1)}, bf16[6,32,128]{2,1,0:T(8,12...) custom-call(f32[12,2,12]{2,1,0:T(2,128)} %bitcast.13, s32[2,3]{1,0:T(2,128)} %bitcast.15, s32[1]{0:T(128)} %bitcast.2.rank_ref, ...), custom_call_target="tpu_custom_call" | custom-call | tf_op jit(solution)/shard_map/mix/pallas_call | solution.py:279
  5.0 0.1 collective-permute-start
  5.1 4.0 %collective-permute-start.1 = (bf16[192,128]{1,0:T(8,128)(2,1)S(1)}, bf16[192,128]{1,0:T(8,128)(2,1)S(1)}, u32[]{:S(2)}, u32[]{:S(2)}) collective-permute-start(bf16[192,128]{1,0:T(8,128)(2,1)S(1)} %bitcast.11), channel_id=1, source_target_pairs={{0,2},{1,3},{2,0},{3,1},{4,6},{5,7},{6,4},{7,5},{8,10},{9,11},{10,... | collective-permute-start | bytes 147464 | tf_op jit(solution)/shard_map/ppermute | solution.py:301
  9.2 0.1 collective-permute-start.2
  9.2 8.0 %all-to-all-start = ((s32[32,1,128]{2,1,0:T(1,128)}), s32[32,1,128]{2,1,0:T(1,128)S(1)}, u32[]{:S(2)}, u32[]{:S(2)}) async-start(s32[32,1,128]{2,1,0:T(1,128)} %get-tuple-element.16), calls=%async_computation | async-start | bytes 32768 | tf_op jit(solution)/shard_map/all_to_all | solution.py:305
  17.3 0.0 collective-permute-done.one_ref
  17.3 0.0 collective-permute-done.1.two_ref
  17.3 0.0 collective-permute-done.2.three_ref
  17.3 1.5 %sum.1.packed_ref = bf16[32,240,128]{2,1,0:T(8,128)(2,1)} custom-call(bf16[192,128]{1,0:T(8,128)(2,1)S(1)} %bitcast.9, bf16[192,128]{1,0:T(8,128)(2,1)S(1)} %collective-permute-done.one_ref, bf16[192,128]{1,0:T(8,128)(2,1)S(1)} %collective-permute-done.1.two_ref, bf16[192,128]{1,0:T(8,128)(2,1)S(1)} %collective-permute-done.2.three_ref), custom_call_target="tpu_custom_call" | custom-call | tf_op jit(solution)/shard_map/sum/pallas_call | solution.py:307
  18.8 6.6 %all-to-all-done.request_ref = s32[32,1,128]{2,1,0:T(1,128)S(1)} async-done(((s32[32,1,128]{2,1,0:T(1,128)}), s32[32,1,128]{2,1,0:T(1,128)S(1)}, u32[]{:S(2)}, u32[]{:S(2)}) %all-to-all-start) | async-done | bytes 16416 | tf_op jit(solution)/shard_map/all_to_all | solution.py:305
  25.4 0.0 copy-done
  25.4 1.5 %lookup.1 = bf16[32,240,128]{2,1,0:T(8,128)(2,1)} custom-call(bf16[32,240,128]{2,1,0:T(8,128)(2,1)} %sum.1.packed_ref, s32[32,1,128]{2,1,0:T(1,128)S(1)} %all-to-all-done.request_ref, bf16[512,128]{1,0:T(8,128)(2,1)S(1)} %copy-done), custom_call_target="tpu_custom_call", output_to_operand_aliasing={{}: (0, {})} | custom-call | tf_op jit(solution)/shard_map/lookup/pallas_call | solution.py:316
  26.9 0.0 copy-start.1
  26.9 4.3 %all-to-all-start.1 = ((bf16[32,240,128]{2,1,0:T(8,128)(2,1)}), bf16[32,240,128]{2,1,0:T(8,128)(2,1)S(1)}, u32[]{:S(2)}, u32[]{:S(2)}) async-start(bf16[32,240,128]{2,1,0:T(8,128)(2,1)} %lookup.1), calls=%async_computation.1 | async-start | bytes 3932160 | tf_op jit(solution)/shard_map/all_to_all | solution.py:330
  31.3 0.0 copy-done.1
  31.3 0.6 fusion
  31.9 2.2 %phase.2.first_ref = bf16[2,1024,256]{2,1,0:T(8,128)(2,1)S(1)} custom-call(s32[3,1024]{1,0:T(4,128)} %re_ref.3, s32[3,256]{1,0:T(4,128)} %get-tuple-element.18.k_ref), custom_call_target="tpu_custom_call" | custom-call | tf_op jit(solution)/shard_map/phase/pallas_call | solution.py:334
  34.1 3.2 %phase.3.later_hbm = bf16[2,1024,256]{2,1,0:T(8,128)(2,1)} custom-call(s32[3,1024]{1,0:T(4,128)} %re_ref.3, s32[3,256]{1,0:T(4,128)} %get-tuple-element.17.k_ref), custom_call_target="tpu_custom_call" | custom-call | tf_op jit(solution)/shard_map/phase/pallas_call | solution.py:334
  37.3 20.9 %all-to-all-done.1.gathered_ref = bf16[32,240,128]{2,1,0:T(8,128)(2,1)S(1)} async-done(((bf16[32,240,128]{2,1,0:T(8,128)(2,1)}), bf16[32,240,128]{2,1,0:T(8,128)(2,1)S(1)}, u32[]{:S(2)}, u32[]{:S(2)}) %all-to-all-start.1) | async-done | bytes 1966112 | tf_op jit(solution)/shard_map/all_to_all | solution.py:330
  58.2 6.7 %final.1 = bf16[6,2,64,512]{3,2,1,0:T(8,128)(2,1)} custom-call(s32[2,512]{1,0:T(2,128)S(1)} %get-tuple-element.11.slot_ref, bf16[512,128]{1,0:T(8,128)(2,1)S(1)} %copy-done, bf16[2,1024,256]{2,1,0:T(8,128)(2,1)S(1)} %phase.2.first_ref, bf16[2,1024,256]{2,1,0:T(8,128)(2,1)} %phase.3.later_hbm, bf16[32,240,128]{2,1,0:T(8,128)(2,1)S(1)} %all-to-all-done.1.gathered_ref), custom_call_target="tpu_custom_call" | custom-call | tf_op jit(solution)/shard_map/final/pallas_call | solution.py:344
Async XLA Ops:
  0.0 25.4 %copy-start = (bf16[512,128]{1,0:T(8,128)(2,1)S(1)}, bf16[512,128]{1,0:T(8,128)(2,1)}, u32[]{:S(2)}) copy-start(bf16[512,128]{1,0:T(8,128)(2,1)} %rotations_ref.3) | copy-start | bytes 393220
  5.0 12.2 %collective-permute-start = (bf16[192,128]{1,0:T(8,128)(2,1)S(1)}, bf16[192,128]{1,0:T(8,128)(2,1)S(1)}, u32[]{:S(2)}, u32[]{:S(2)}) collective-permute-start(bf16[192,128]{1,0:T(8,128)(2,1)S(1)} %bitcast.12), channel_id=1, source_target_pairs={{0,1},{1,0},{2,3},{3,2},{4,5},{5,4},{6,7},{7,6},{8,9},{9,8},{10,11... | collective-permute-start | bytes 147464 | tf_op jit(solution)/shard_map/ppermute | solution.py:301
  5.1 12.2 %collective-permute-start.1 = (bf16[192,128]{1,0:T(8,128)(2,1)S(1)}, bf16[192,128]{1,0:T(8,128)(2,1)S(1)}, u32[]{:S(2)}, u32[]{:S(2)}) collective-permute-start(bf16[192,128]{1,0:T(8,128)(2,1)S(1)} %bitcast.11), channel_id=1, source_target_pairs={{0,2},{1,3},{2,0},{3,1},{4,6},{5,7},{6,4},{7,5},{8,10},{9,11},{10,... | collective-permute-start | bytes 147464 | tf_op jit(solution)/shard_map/ppermute | solution.py:301
  9.2 8.1 %collective-permute-start.2 = (bf16[192,128]{1,0:T(8,128)(2,1)S(1)}, bf16[192,128]{1,0:T(8,128)(2,1)S(1)}, u32[]{:S(2)}, u32[]{:S(2)}) collective-permute-start(bf16[192,128]{1,0:T(8,128)(2,1)S(1)} %bitcast.10), channel_id=1, source_target_pairs={{0,3},{1,2},{2,1},{3,0},{4,7},{5,6},{6,5},{7,4},{8,11},{9,10},{10,... | collective-permute-start | bytes 147464 | tf_op jit(solution)/shard_map/ppermute | solution.py:301
  9.2 16.2 %all-to-all-start = ((s32[32,1,128]{2,1,0:T(1,128)}), s32[32,1,128]{2,1,0:T(1,128)S(1)}, u32[]{:S(2)}, u32[]{:S(2)}) async-start(s32[32,1,128]{2,1,0:T(1,128)} %get-tuple-element.16), calls=%async_computation | async-start | bytes 32768 | tf_op jit(solution)/shard_map/all_to_all | solution.py:305
  26.9 4.3 %copy-start.1 = (s32[3,512]{1,0:T(4,128)S(1)}, s32[3,512]{1,0:T(4,128)}, u32[]{:S(2)}) copy-start(s32[3,512]{1,0:T(4,128)} %param.14) | copy-start | bytes 18436
  26.9 31.2 %all-to-all-start.1 = ((bf16[32,240,128]{2,1,0:T(8,128)(2,1)}), bf16[32,240,128]{2,1,0:T(8,128)(2,1)S(1)}, u32[]{:S(2)}, u32[]{:S(2)}) async-start(bf16[32,240,128]{2,1,0:T(8,128)(2,1)} %lookup.1), calls=%async_computation.1 | async-start | bytes 3932160 | tf_op jit(solution)/shard_map/all_to_all | solution.py:330

commit v7 on v5

--- a/solution.py
+++ b/solution.py
@@ -25,6 +25,7 @@
 LANES = 128
 TILES = K // LANES
 FIRST = 2
+CHUNK = 16
 SIZE = NB * NB
 TURN = 2.0 * math.pi
 SINE = [TURN ** n * s / math.factorial(n) for n, s in ((1, 1), (3, -1), (5, 1), (7, -1), (9, 1), (11, -1))]
@@ -52,7 +53,7 @@
     return cosine, sine
 
 
-def requests_kernel(owner_ref, row_ref, request_ref, slot_ref):
+def find_requests(owner_ref, row_ref, request_ref, slot_ref):
     before = (lax.broadcasted_iota(I32, (K, K), 0) < lax.broadcasted_iota(I32, (K, K), 1)).astype(F32).astype(BF)
     total = jnp.zeros((N_RE, LANES), F32)
     for q in range(Q):
@@ -61,9 +62,9 @@
         hit = lax.broadcasted_iota(I32, (N_RE, K), 0) == owner
         one_hot = hit.astype(F32)
         earlier = jnp.dot(one_hot.astype(BF), before, preferred_element_type=F32)
-        rank = jnp.sum(one_hot * earlier, axis=0, keepdims=True).astype(I32) + q * CAP
-        slot_ref[q : q + 1, :] = owner * CAP + rank - q * CAP
-        place = (lax.broadcasted_iota(I32, (LANES, K), 0) == rank).astype(F32).astype(BF)
+        rank = jnp.sum(one_hot * earlier, axis=0, keepdims=True).astype(I32)
+        slot_ref[q : q + 1, :] = owner * CAP + rank
+        place = (lax.broadcasted_iota(I32, (LANES, K), 0) == rank + q * CAP).astype(F32).astype(BF)
         high = (one_hot * (row >> 4).astype(F32)).astype(BF)
         low = (one_hot * (row & 15).astype(F32)).astype(BF)
         contract = (((1,), (1,)), ((), ()))
@@ -74,7 +75,16 @@
         request_ref[o] = total[o : o + 1, :]
 
 
-def mix_kernel(mode_ref, q_ref, rank_ref, rp_ref, table_ref, *out_refs):
+def mix_kernel(
+    mode_ref, q_ref, rank_ref, rp_ref, owner_ref, row_ref, table_ref,
+    own_ref, one_ref, two_ref, three_ref, request_ref, slot_ref,
+):
+    out_refs = own_ref, one_ref, two_ref, three_ref
+
+    @pl.when(pl.program_id(0) == 0)
+    def _():
+        find_requests(owner_ref, row_ref, request_ref, slot_ref)
+
     group = 8
     width = group * RP_LOCAL
     coords = jnp.concatenate([rp_ref[...]] * group, axis=1)
@@ -117,10 +127,15 @@
             out_refs[s][i] = jnp.concatenate(parts[s][i], axis=0).astype(BF)
 
 
-def sum_kernel(own_ref, one_ref, two_ref, three_ref, out_ref):
+def sum_kernel(own_ref, one_ref, two_ref, three_ref, out_hbm, total_ref, sem):
     total = own_ref[...].astype(F32) + one_ref[...].astype(F32)
     total += two_ref[...].astype(F32) + three_ref[...].astype(F32)
-    out_ref[...] = jnp.broadcast_to(total.astype(BF)[None], out_ref.shape)
+    total_ref[...] = total.astype(BF)
+    copies = [pltpu.make_async_copy(total_ref, out_hbm.at[p, :ROWS, :], sem.at[p]) for p in range(N_RE)]
+    for copy in copies:
+        copy.start()
+    for copy in copies:
+        copy.wait()
 
 
 def lookup_kernel(packed_ref, request_ref, rotations_ref, out_ref):
@@ -250,20 +265,24 @@
     kq_owner,
     kq_row,
 ):
-    chunk = 16
-    block = (Q * M_LOCAL, chunk, LANES)
-    parts = pl.pallas_call(
+    hbm = pl.BlockSpec(memory_space=pltpu.HBM)
+    vmem = pl.BlockSpec(memory_space=pltpu.VMEM)
+    part = pl.BlockSpec((Q * M_LOCAL, CHUNK, LANES), lambda i: (0, i, 0))
+    *parts, requests, slots = pl.pallas_call(
         mix_kernel,
-        grid=(RE_LOCAL // chunk,),
+        grid=(RE_LOCAL // CHUNK,),
         in_specs=[
             smem(),
             smem(),
             smem(),
             whole((3, RP_LOCAL)),
-            pl.BlockSpec((chunk, RP_LOCAL, 2 * MODES * NB * NB), lambda i: (i, 0, 0)),
+            whole((Q, 1, K)),
+            whole((Q, K)),
+            pl.BlockSpec((CHUNK, RP_LOCAL, 2 * MODES * SIZE), lambda i: (i, 0, 0)),
         ],
-        out_specs=[pl.BlockSpec(block, lambda i: (0, i, 0))] * N_RP,
-        out_shape=[jax.ShapeDtypeStruct((Q * M_LOCAL, RE_LOCAL, LANES), BF)] * N_RP,
+        out_specs=[part] * N_RP + [whole((N_RE, 1, LANES)), whole((Q, K))],
+        out_shape=[jax.ShapeDtypeStruct((Q * M_LOCAL, RE_LOCAL, LANES), BF)] * N_RP
+        + [jax.ShapeDtypeStruct((N_RE, 1, LANES), I32), jax.ShapeDtypeStruct((Q, K), I32)],
         compiler_params=params(16),
         name="mix",
     )(
@@ -271,6 +290,8 @@
         in_hbm(q_coords.T),
         lax.axis_index("rp").reshape(1),
         in_hbm(rp_coords),
+        in_hbm(kq_owner.transpose(0, 2, 1)),
+        in_hbm(kq_row),
         in_hbm(wannier_table),
     )
     own = parts[0].reshape(ROWS, LANES)
@@ -279,24 +300,14 @@
         for s in range(1, N_RP)
     ]
 
-    requests, slots = pl.pallas_call(
-        requests_kernel,
-        out_shape=(
-            jax.ShapeDtypeStruct((N_RE, 1, LANES), I32),
-            jax.ShapeDtypeStruct((Q, K), I32),
-        ),
-        compiler_params=params(16),
-        name="requests",
-    )(in_hbm(kq_owner.transpose(0, 2, 1)), in_hbm(kq_row))
     wanted = lax.all_to_all(requests, "re", split_axis=0, concat_axis=0, tiled=True)
 
-    peers = 8
     spread = pl.pallas_call(
         sum_kernel,
-        grid=(N_RE // peers,),
-        in_specs=[whole((ROWS, LANES))] * N_RP,
-        out_specs=pl.BlockSpec((peers, ROWS, LANES), lambda i: (i, 0, 0)),
+        in_specs=[vmem] * N_RP,
+        out_specs=hbm,
         out_shape=pltpu.HBM((N_RE, PACK, LANES), BF),
+        scratch_shapes=[pltpu.VMEM((ROWS, LANES), BF), pltpu.SemaphoreType.DMA((N_RE,))],
         compiler_params=params(8),
         name="sum",
     )(own, *others)
@@ -328,8 +339,6 @@
     first = phase_tiles(k_coords[:, : FIRST * LANES], pltpu.VMEM)
     later = phase_tiles(k_coords[:, FIRST * LANES :], pltpu.HBM)
 
-    hbm = pl.BlockSpec(memory_space=pltpu.HBM)
-    vmem = pl.BlockSpec(memory_space=pltpu.VMEM)
     result = pl.pallas_call(
         final_kernel,
         in_specs=[vmem, vmem, vmem, hbm, vmem],

time: 65.5 us -> 64.6 us (0.986)
  Pallas kernels: 20.6 us -> 19.6 us
    pallas_call x3 -> x2, Pallas kernels: 6.96 us -> 5.95 us  [the longest x1 4.44 us: local(): pl.pallas_call(mix_kernel, grid=(RE_LOCAL // CHUNK,), in_specs=[smem(), s...]
  transfers between devices with their start and end apart: 5 -> 5, of which waited for: 2 -> 2; matrix products, arithmetic and copies ran while one was open for 1% -> 1% of each run, Pallas kernels for 14% -> 11%
where the time goes in v7:
time: 64.6 us; the launch traced here: 64.2 us
  waiting for transfers between devices  27.6 us (43%)
  Pallas kernels  19.6 us (30%)
  starting transfers between devices  16.3 us (25%)
    all_to_all x1, waiting for transfers between devices, local(): lax.all_to_all(packed, 're', split_axis=0, concat_axis=0, tiled=True)  21 us
    all_to_all x1, starting transfers between devices, local(): lax.all_to_all(requests, 're', split_axis=0, concat_axis=0, tiled=True)  8.01 us
    pallas_call x1, Pallas kernels, local(): pl.pallas_call(final_kernel, in_specs=[vmem, vmem, vmem, hbm, vmem], out_...  6.77 us
    all_to_all x1, waiting for transfers between devices, local(): lax.all_to_all(requests, 're', split_axis=0, concat_axis=0, tiled=True)  6.61 us
    pallas_call x2, Pallas kernels, phase_tiles(): pl.pallas_call(phase_kernel, out_shape=space((tiles, RE, 2 * LANES), BF),...  5.4 us
    pallas_call x1, Pallas kernels, local(): pl.pallas_call(mix_kernel, grid=(RE_LOCAL // CHUNK,), in_specs=[smem(), s...  4.44 us
    all_to_all x1, starting transfers between devices, local(): lax.all_to_all(packed, 're', split_axis=0, concat_axis=0, tiled=True)  4.13 us
    ppermute x3, starting transfers between devices, local(): lax.ppermute(parts[s].reshape(ROWS, LANES), 'rp', [(j, j ^ s) for j in ra...  4.12 us
  transfers between devices with their start and end apart: 5, of which 2 were waited for; matrix products, arithmetic and copies ran while one was open for 1% of the time, Pallas kernels for 11%

profile of v7, /device:TPU:0, one launch (start us, length us, event | category | flops | bytes accessed | tf_op | source)
XLA Modules:
  0.0 64.2 jit_solution(15668098149806569042)
XLA Ops:
  0.0 0.0 copy-start
  0.0 4.4 %mix.1 = (bf16[6,32,128]{2,1,0:T(8,128)(2,1)S(1)}, bf16[6,32,128]{2,1,0:T(8,128)(2,1)S(1)}, bf16[6,32,128]{2,1,0:T(8,128)(2,1)S(1)}, bf16[6,32,128]{2,1,0:T(8,12...) custom-call(f32[12,2,12]{2,1,0:T(2,128)} %bitcast.13, s32[2,3]{1,0:T(2,128)} %bitcast.15, s32[1]{0:T(128)} %bitcast.2.rank_ref, ...), custom_call_target="tpu_custom_call" | custom-call | tf_op jit(solution)/shard_map/mix/pallas_call | solution.py:271
  4.4 0.0 collective-permute-start
  4.5 4.0 %collective-permute-start.1 = (bf16[192,128]{1,0:T(8,128)(2,1)S(1)}, bf16[192,128]{1,0:T(8,128)(2,1)S(1)}, u32[]{:S(2)}, u32[]{:S(2)}) collective-permute-start(bf16[192,128]{1,0:T(8,128)(2,1)S(1)} %bitcast.11), channel_id=1, source_target_pairs={{0,2},{1,3},{2,0},{3,1},{4,6},{5,7},{6,4},{7,5},{8,10},{9,11},{10,... | collective-permute-start | bytes 147464 | tf_op jit(solution)/shard_map/ppermute | solution.py:299
  8.4 0.1 collective-permute-start.2
  8.6 8.0 %all-to-all-start = ((s32[32,1,128]{2,1,0:T(1,128)}), s32[32,1,128]{2,1,0:T(1,128)S(1)}, u32[]{:S(2)}, u32[]{:S(2)}) async-start(s32[32,1,128]{2,1,0:T(1,128)} %get-tuple-element.16), calls=%async_computation | async-start | bytes 32768 | tf_op jit(solution)/shard_map/all_to_all | solution.py:303
  16.6 0.0 collective-permute-done.one_ref
  16.6 0.0 collective-permute-done.1.two_ref
  16.6 0.0 collective-permute-done.2.three_ref
  16.6 1.5 %sum.1.packed_ref = bf16[32,240,128]{2,1,0:T(8,128)(2,1)} custom-call(bf16[192,128]{1,0:T(8,128)(2,1)S(1)} %bitcast.9, bf16[192,128]{1,0:T(8,128)(2,1)S(1)} %collective-permute-done.one_ref, bf16[192,128]{1,0:T(8,128)(2,1)S(1)} %collective-permute-done.1.two_ref, bf16[192,128]{1,0:T(8,128)(2,1)S(1)} %collective-permute-done.2.three_ref), custom_call_target="tpu_custom_call" | custom-call | tf_op jit(solution)/shard_map/sum/pallas_call | solution.py:305
  18.1 6.6 %all-to-all-done.request_ref = s32[32,1,128]{2,1,0:T(1,128)S(1)} async-done(((s32[32,1,128]{2,1,0:T(1,128)}), s32[32,1,128]{2,1,0:T(1,128)S(1)}, u32[]{:S(2)}, u32[]{:S(2)}) %all-to-all-start) | async-done | bytes 16416 | tf_op jit(solution)/shard_map/all_to_all | solution.py:303
  24.7 0.0 copy-done
  24.8 1.5 %lookup.1 = bf16[32,240,128]{2,1,0:T(8,128)(2,1)} custom-call(bf16[32,240,128]{2,1,0:T(8,128)(2,1)} %sum.1.packed_ref, s32[32,1,128]{2,1,0:T(1,128)S(1)} %all-to-all-done.request_ref, bf16[512,128]{1,0:T(8,128)(2,1)S(1)} %copy-done), custom_call_target="tpu_custom_call", output_to_operand_aliasing={{}: (0, {})} | custom-call | tf_op jit(solution)/shard_map/lookup/pallas_call | solution.py:314
  26.3 0.0 copy-start.1
  26.3 4.1 %all-to-all-start.1 = ((bf16[32,240,128]{2,1,0:T(8,128)(2,1)}), bf16[32,240,128]{2,1,0:T(8,128)(2,1)S(1)}, u32[]{:S(2)}, u32[]{:S(2)}) async-start(bf16[32,240,128]{2,1,0:T(8,128)(2,1)} %lookup.1), calls=%async_computation.1 | async-start | bytes 3932160 | tf_op jit(solution)/shard_map/all_to_all | solution.py:328
  30.4 0.0 copy-done.1
  30.4 0.6 fusion
  31.0 2.2 %phase.2.first_ref = bf16[2,1024,256]{2,1,0:T(8,128)(2,1)S(1)} custom-call(s32[3,1024]{1,0:T(4,128)} %re_ref.3, s32[3,256]{1,0:T(4,128)} %get-tuple-element.18.k_ref), custom_call_target="tpu_custom_call" | custom-call | tf_op jit(solution)/shard_map/phase/pallas_call | solution.py:332
  33.2 3.2 %phase.3.later_hbm = bf16[2,1024,256]{2,1,0:T(8,128)(2,1)} custom-call(s32[3,1024]{1,0:T(4,128)} %re_ref.3, s32[3,256]{1,0:T(4,128)} %get-tuple-element.17.k_ref), custom_call_target="tpu_custom_call" | custom-call | tf_op jit(solution)/shard_map/phase/pallas_call | solution.py:332
  36.4 21.0 %all-to-all-done.1.gathered_ref = bf16[32,240,128]{2,1,0:T(8,128)(2,1)S(1)} async-done(((bf16[32,240,128]{2,1,0:T(8,128)(2,1)}), bf16[32,240,128]{2,1,0:T(8,128)(2,1)S(1)}, u32[]{:S(2)}, u32[]{:S(2)}) %all-to-all-start.1) | async-done | bytes 1966112 | tf_op jit(solution)/shard_map/all_to_all | solution.py:328
  57.4 6.8 %final.1 = bf16[6,2,64,512]{3,2,1,0:T(8,128)(2,1)} custom-call(s32[2,512]{1,0:T(2,128)S(1)} %get-tuple-element.11.slot_ref, bf16[512,128]{1,0:T(8,128)(2,1)S(1)} %copy-done, bf16[2,1024,256]{2,1,0:T(8,128)(2,1)S(1)} %phase.2.first_ref, bf16[2,1024,256]{2,1,0:T(8,128)(2,1)} %phase.3.later_hbm, bf16[32,240,128]{2,1,0:T(8,128)(2,1)S(1)} %all-to-all-done.1.gathered_ref), custom_call_target="tpu_custom_call" | custom-call | tf_op jit(solution)/shard_map/final/pallas_call | solution.py:342
Async XLA Ops:
  0.0 24.8 %copy-start = (bf16[512,128]{1,0:T(8,128)(2,1)S(1)}, bf16[512,128]{1,0:T(8,128)(2,1)}, u32[]{:S(2)}) copy-start(bf16[512,128]{1,0:T(8,128)(2,1)} %rotations_ref.3) | copy-start | bytes 393220
  4.4 12.1 %collective-permute-start = (bf16[192,128]{1,0:T(8,128)(2,1)S(1)}, bf16[192,128]{1,0:T(8,128)(2,1)S(1)}, u32[]{:S(2)}, u32[]{:S(2)}) collective-permute-start(bf16[192,128]{1,0:T(8,128)(2,1)S(1)} %bitcast.12), channel_id=1, source_target_pairs={{0,1},{1,0},{2,3},{3,2},{4,5},{5,4},{6,7},{7,6},{8,9},{9,8},{10,11... | collective-permute-start | bytes 147464 | tf_op jit(solution)/shard_map/ppermute | solution.py:299
  4.5 12.2 %collective-permute-start.1 = (bf16[192,128]{1,0:T(8,128)(2,1)S(1)}, bf16[192,128]{1,0:T(8,128)(2,1)S(1)}, u32[]{:S(2)}, u32[]{:S(2)}) collective-permute-start(bf16[192,128]{1,0:T(8,128)(2,1)S(1)} %bitcast.11), channel_id=1, source_target_pairs={{0,2},{1,3},{2,0},{3,1},{4,6},{5,7},{6,4},{7,5},{8,10},{9,11},{10,... | collective-permute-start | bytes 147464 | tf_op jit(solution)/shard_map/ppermute | solution.py:299
  8.4 8.2 %collective-permute-start.2 = (bf16[192,128]{1,0:T(8,128)(2,1)S(1)}, bf16[192,128]{1,0:T(8,128)(2,1)S(1)}, u32[]{:S(2)}, u32[]{:S(2)}) collective-permute-start(bf16[192,128]{1,0:T(8,128)(2,1)S(1)} %bitcast.10), channel_id=1, source_target_pairs={{0,3},{1,2},{2,1},{3,0},{4,7},{5,6},{6,5},{7,4},{8,11},{9,10},{10,... | collective-permute-start | bytes 147464 | tf_op jit(solution)/shard_map/ppermute | solution.py:299
  8.6 16.2 %all-to-all-start = ((s32[32,1,128]{2,1,0:T(1,128)}), s32[32,1,128]{2,1,0:T(1,128)S(1)}, u32[]{:S(2)}, u32[]{:S(2)}) async-start(s32[32,1,128]{2,1,0:T(1,128)} %get-tuple-element.16), calls=%async_computation | async-start | bytes 32768 | tf_op jit(solution)/shard_map/all_to_all | solution.py:303
  26.3 4.1 %copy-start.1 = (s32[3,512]{1,0:T(4,128)S(1)}, s32[3,512]{1,0:T(4,128)}, u32[]{:S(2)}) copy-start(s32[3,512]{1,0:T(4,128)} %param.14) | copy-start | bytes 18436
  26.3 31.2 %all-to-all-start.1 = ((bf16[32,240,128]{2,1,0:T(8,128)(2,1)}), bf16[32,240,128]{2,1,0:T(8,128)(2,1)S(1)}, u32[]{:S(2)}, u32[]{:S(2)}) async-start(bf16[32,240,128]{2,1,0:T(8,128)(2,1)} %lookup.1), calls=%async_computation.1 | async-start | bytes 3932160 | tf_op jit(solution)/shard_map/all_to_all | solution.py:328

commit v8 on v7

--- a/solution.py
+++ b/solution.py
@@ -19,9 +19,8 @@
 N_RP = 4
 M_LOCAL = MODES // N_RP
 CAP = 24
-SLOTS = Q * CAP
 ROWS = Q * M_LOCAL * RE_LOCAL
-PACK = ROWS + SLOTS
+PACK = ROWS + CAP
 LANES = 128
 TILES = K // LANES
 FIRST = 2
@@ -53,23 +52,20 @@
     return cosine, sine
 
 
-def find_requests(owner_ref, row_ref, request_ref, slot_ref):
+def find_requests(q, owner_ref, row_ref, request_ref, slot_ref):
     before = (lax.broadcasted_iota(I32, (K, K), 0) < lax.broadcasted_iota(I32, (K, K), 1)).astype(F32).astype(BF)
-    total = jnp.zeros((N_RE, LANES), F32)
-    for q in range(Q):
-        owner = owner_ref[q]
-        row = row_ref[q : q + 1, :]
-        hit = lax.broadcasted_iota(I32, (N_RE, K), 0) == owner
-        one_hot = hit.astype(F32)
-        earlier = jnp.dot(one_hot.astype(BF), before, preferred_element_type=F32)
-        rank = jnp.sum(one_hot * earlier, axis=0, keepdims=True).astype(I32)
-        slot_ref[q : q + 1, :] = owner * CAP + rank
-        place = (lax.broadcasted_iota(I32, (LANES, K), 0) == rank + q * CAP).astype(F32).astype(BF)
-        high = (one_hot * (row >> 4).astype(F32)).astype(BF)
-        low = (one_hot * (row & 15).astype(F32)).astype(BF)
-        contract = (((1,), (1,)), ((), ()))
-        total += 16.0 * lax.dot_general(high, place, contract, preferred_element_type=F32)
-        total += lax.dot_general(low, place, contract, preferred_element_type=F32)
+    owner = owner_ref[q]
+    row = row_ref[pl.ds(q, 1), :]
+    one_hot = (lax.broadcasted_iota(I32, (N_RE, K), 0) == owner).astype(F32)
+    earlier = jnp.dot(one_hot.astype(BF), before, preferred_element_type=F32)
+    rank = jnp.sum(one_hot * earlier, axis=0, keepdims=True).astype(I32)
+    slot_ref[...] = owner * CAP + rank
+    place = (lax.broadcasted_iota(I32, (LANES, K), 0) == rank).astype(F32).astype(BF)
+    high = (one_hot * (row >> 4).astype(F32)).astype(BF)
+    low = (one_hot * (row & 15).astype(F32)).astype(BF)
+    contract = (((1,), (1,)), ((), ()))
+    total = 16.0 * lax.dot_general(high, place, contract, preferred_element_type=F32)
+    total += lax.dot_general(low, place, contract, preferred_element_type=F32)
     total = total.astype(I32)
     for o in range(N_RE):
         request_ref[o] = total[o : o + 1, :]
@@ -83,7 +79,7 @@
 
     @pl.when(pl.program_id(0) == 0)
     def _():
-        find_requests(owner_ref, row_ref, request_ref, slot_ref)
+        find_requests(rank_ref[0] % Q, owner_ref, row_ref, request_ref, slot_ref)
 
     group = 8
     width = group * RP_LOCAL
@@ -139,12 +135,12 @@
 
 
 def lookup_kernel(packed_ref, request_ref, rotations_ref, out_ref):
-    peers = out_ref.shape[0]
     wanted = request_ref[:, 0, :].T
-    rows = lax.broadcasted_iota(I32, (SLOTS, K), 1)
-    one_hot = [(wanted[:SLOTS, p : p + 1] == rows).astype(F32).astype(BF) for p in range(peers)]
-    found = jnp.dot(jnp.concatenate(one_hot, axis=0), rotations_ref[...], preferred_element_type=F32)
-    out_ref[...] = found.reshape(peers, SLOTS, LANES).astype(BF)
+    rows = lax.broadcasted_iota(I32, (CAP, K), 1)
+    one_hot = [(wanted[:CAP, p : p + 1] == rows).astype(F32) for p in range(N_RE)]
+    one_hot = jnp.concatenate(one_hot, axis=0).astype(BF)
+    found = jnp.dot(one_hot, rotations_ref[...], preferred_element_type=F32)
+    out_ref[...] = found.reshape(N_RE, CAP, LANES).astype(BF)
 
 
 def phase_kernel(re_ref, k_ref, out_ref):
@@ -189,50 +185,50 @@
             out_ref[t, i, c, rows] = jnp.concatenate(results[c], axis=0).astype(BF)
 
 
-def final_kernel(
-    slot_ref, rotations_ref, first_ref, later_hbm, gathered_ref, out_hbm,
-    later_ref, near_ref, turned_ref, far_ref, coupling_ref, out_ref, later_sem, out_sem,
-):
+def far_kernel(slot_ref, gathered_ref, out_ref):
+    replies = gathered_ref[:, ROWS:, :].astype(F32).reshape(N_RE * CAP, LANES)
+    place = lax.broadcasted_iota(I32, (N_RE * CAP, K), 0)
+    one_hot = (place == slot_ref[...]).astype(F32).astype(BF)
+    out_ref[...] = jnp.dot(replies.T.astype(BF), one_hot, preferred_element_type=F32).astype(BF)
+
+
+def couple_kernel(first_ref, later_hbm, gathered_ref, out_ref, later_ref, turned_ref, later_sem):
     later = [pltpu.make_async_copy(later_hbm.at[t], later_ref.at[t], later_sem.at[t]) for t in range(TILES - FIRST)]
+    for copy in later:
+        copy.start()
+    for i in range(Q * M_LOCAL):
+        block = gathered_ref[:, i * RE_LOCAL : (i + 1) * RE_LOCAL, :].reshape(RE, LANES)
+        turned_ref[i] = block.T
+    for t in range(TILES):
+        if t >= FIRST:
+            later[t - FIRST].wait()
+        for i in range(Q * M_LOCAL):
+            phase = first_ref[t] if t < FIRST else later_ref[t - FIRST]
+            both = jnp.dot(turned_ref[i], phase, preferred_element_type=F32)
+            real = both[:SIZE, :LANES] - both[SIZE:, LANES:]
+            imag = both[:SIZE, LANES:] + both[SIZE:, :LANES]
+            out_ref[t, i, :SIZE] = real
+            out_ref[t, i, SIZE : 2 * SIZE] = imag
+            out_ref[t, i, 2 * SIZE :] = real + imag
+
+
+def final_kernel(rank_ref, rotations_ref, mine_ref, mate_ref, coupling_ref, out_hbm, near_ref, far_ref, out_ref, out_sem):
     out_copies = [
         pltpu.make_async_copy(out_ref.at[t], out_hbm.at[:, :, :, t * LANES : (t + 1) * LANES], out_sem.at[t])
         for t in range(TILES)
     ]
-    for copy in later:
-        copy.start()
     near = rotations_ref[...].astype(F32).T
     near_ref[: 2 * SIZE] = near
     near_ref[2 * SIZE :] = near[:SIZE] + near[SIZE:]
-    replies = gathered_ref[:, ROWS:, :].astype(F32)
-    place = lax.broadcasted_iota(I32, (N_RE * CAP, K), 0)
+    mine = mine_ref[...].astype(F32)
+    mate = mate_ref[...].astype(F32)
     for q in range(Q):
-        rows = replies[:, q * CAP : (q + 1) * CAP, :].reshape(N_RE * CAP, LANES)
-        one_hot = (place == slot_ref[q : q + 1, :]).astype(F32).astype(BF)
-        far = jnp.dot(rows.T.astype(BF), one_hot, preferred_element_type=F32)
+        far = jnp.where(rank_ref[0] % Q == q, mine, mate)
         far_ref[q, : 2 * SIZE] = far
         far_ref[q, 2 * SIZE :] = far[:SIZE] - far[SIZE:]
-    for i in range(Q * M_LOCAL):
-        block = gathered_ref[:, i * RE_LOCAL : (i + 1) * RE_LOCAL, :].reshape(RE, LANES)
-        turned_ref[i] = block.T
-
-    def couple(t, i):
-        phase = first_ref[t] if t < FIRST else later_ref[t - FIRST]
-        both = jnp.dot(turned_ref[i], phase, preferred_element_type=F32)
-        real = both[:SIZE, :LANES] - both[SIZE:, LANES:]
-        imag = both[:SIZE, LANES:] + both[SIZE:, :LANES]
-        coupling_ref[t % 2, i, :SIZE] = real
-        coupling_ref[t % 2, i, SIZE : 2 * SIZE] = imag
-        coupling_ref[t % 2, i, 2 * SIZE :] = real + imag
-
-    for i in range(Q * M_LOCAL):
-        couple(0, i)
     for t in range(TILES):
-        if FIRST <= t + 1 < TILES:
-            later[t + 1 - FIRST].wait()
         for i in range(Q * M_LOCAL):
-            if t + 1 < TILES:
-                couple(t + 1, i)
-            rotate(coupling_ref.at[t % 2, i], far_ref, near_ref, out_ref, i // M_LOCAL, i, t)
+            rotate(coupling_ref.at[t, i], far_ref, near_ref, out_ref, i // M_LOCAL, i, t)
         out_copies[t].start()
     for t in range(TILES):
         out_copies[t].wait()
@@ -267,6 +263,7 @@
 ):
     hbm = pl.BlockSpec(memory_space=pltpu.HBM)
     vmem = pl.BlockSpec(memory_space=pltpu.VMEM)
+    rank = lax.axis_index("rp").reshape(1)
     part = pl.BlockSpec((Q * M_LOCAL, CHUNK, LANES), lambda i: (0, i, 0))
     *parts, requests, slots = pl.pallas_call(
         mix_kernel,
@@ -280,15 +277,15 @@
             whole((Q, K)),
             pl.BlockSpec((CHUNK, RP_LOCAL, 2 * MODES * SIZE), lambda i: (i, 0, 0)),
         ],
-        out_specs=[part] * N_RP + [whole((N_RE, 1, LANES)), whole((Q, K))],
+        out_specs=[part] * N_RP + [whole((N_RE, 1, LANES)), whole((1, K))],
         out_shape=[jax.ShapeDtypeStruct((Q * M_LOCAL, RE_LOCAL, LANES), BF)] * N_RP
-        + [jax.ShapeDtypeStruct((N_RE, 1, LANES), I32), jax.ShapeDtypeStruct((Q, K), I32)],
+        + [jax.ShapeDtypeStruct((N_RE, 1, LANES), I32), jax.ShapeDtypeStruct((1, K), I32)],
         compiler_params=params(16),
         name="mix",
     )(
         in_hbm(mode_matrix.transpose(1, 0, 2)),
         in_hbm(q_coords.T),
-        lax.axis_index("rp").reshape(1),
+        rank,
         in_hbm(rp_coords),
         in_hbm(kq_owner.transpose(0, 2, 1)),
         in_hbm(kq_row),
@@ -319,7 +316,7 @@
             pl.BlockSpec(memory_space=pltpu.VMEM),
             pl.BlockSpec(memory_space=pltpu.VMEM),
         ],
-        out_specs=pl.BlockSpec((N_RE, SLOTS, LANES), lambda i: (0, ROWS // SLOTS, 0)),
+        out_specs=pl.BlockSpec((N_RE, CAP, LANES), lambda i: (0, ROWS // CAP, 0)),
         out_shape=pltpu.HBM((N_RE, PACK, LANES), BF),
         input_output_aliases={0: 0},
         compiler_params=params(8),
@@ -339,24 +336,41 @@
     first = phase_tiles(k_coords[:, : FIRST * LANES], pltpu.VMEM)
     later = phase_tiles(k_coords[:, FIRST * LANES :], pltpu.HBM)
 
+    slots, first, later = lax.optimization_barrier((slots, first, later))
+    far = pl.pallas_call(
+        far_kernel,
+        in_specs=[vmem, vmem],
+        out_shape=jax.ShapeDtypeStruct((LANES, K), BF),
+        compiler_params=params(16),
+        name="far",
+    )(slots, gathered)
+    mate = lax.ppermute(far, "rp", [(j, j ^ 1) for j in range(N_RP)])
+    coupling = pl.pallas_call(
+        couple_kernel,
+        in_specs=[vmem, hbm, vmem],
+        out_shape=pltpu.VMEM((TILES, Q * M_LOCAL, 3 * SIZE, LANES), F32),
+        scratch_shapes=[
+            pltpu.VMEM((TILES - FIRST, RE, 2 * LANES), BF),
+            pltpu.VMEM((Q * M_LOCAL, LANES, RE), BF),
+            pltpu.SemaphoreType.DMA((TILES - FIRST,)),
+        ],
+        compiler_params=params(16),
+        name="couple",
+    )(first, in_hbm(later), gathered)
     result = pl.pallas_call(
         final_kernel,
-        in_specs=[vmem, vmem, vmem, hbm, vmem],
+        in_specs=[smem(), vmem, vmem, vmem, vmem],
         out_specs=hbm,
         out_shape=jax.ShapeDtypeStruct((Q * M_LOCAL, 2, SIZE, K), BF),
         scratch_shapes=[
-            pltpu.VMEM((TILES - FIRST, RE, 2 * LANES), BF),
             pltpu.VMEM((3 * SIZE, K), F32),
-            pltpu.VMEM((Q * M_LOCAL, LANES, RE), BF),
             pltpu.VMEM((Q, 3 * SIZE, K), F32),
-            pltpu.VMEM((2, Q * M_LOCAL, 3 * SIZE, LANES), F32),
             pltpu.VMEM((TILES, Q * M_LOCAL, 2, SIZE, LANES), BF),
-            pltpu.SemaphoreType.DMA((TILES - FIRST,)),
             pltpu.SemaphoreType.DMA((TILES,)),
         ],
-        compiler_params=params(24),
+        compiler_params=params(16),
         name="final",
-    )(slots, rotations, first, in_hbm(later), gathered)
+    )(rank, rotations, far, mate, coupling)
     return result.reshape(Q, M_LOCAL, 2, NB * NB, K)
 
 

time: 64.6 us -> 63.9 us (0.989)
  the two profiles are of different devices: /device:TPU:0 before, /device:TPU:1 now
where the time goes in v8:
time: 63.9 us; the launch traced here: 63.5 us
  waiting for transfers between devices  23.7 us (37%)
  starting transfers between devices  19.9 us (31%)
  Pallas kernels  19.1 us (30%)
    all_to_all x1, waiting for transfers between devices, local(): lax.all_to_all(packed, 're', split_axis=0, concat_axis=0, tiled=True)  18.2 us
    all_to_all x1, starting transfers between devices, local(): lax.all_to_all(requests, 're', split_axis=0, concat_axis=0, tiled=True)  7.96 us
    all_to_all x1, waiting for transfers between devices, local(): lax.all_to_all(requests, 're', split_axis=0, concat_axis=0, tiled=True)  5.49 us
    pallas_call x2, Pallas kernels, phase_tiles(): pl.pallas_call(phase_kernel, out_shape=space((tiles, RE, 2 * LANES), BF),...  5.37 us
    ppermute x3, starting transfers between devices, local(): lax.ppermute(parts[s].reshape(ROWS, LANES), 'rp', [(j, j ^ s) for j in ra...  5.16 us
    pallas_call x1, Pallas kernels, local(): pl.pallas_call(final_kernel, in_specs=[smem(), vmem, vmem, vmem, vmem], o...  4.33 us
    pallas_call x1, Pallas kernels, local(): pl.pallas_call(mix_kernel, grid=(RE_LOCAL // CHUNK,), in_specs=[smem(), s...  4.15 us
    all_to_all x1, starting transfers between devices, local(): lax.all_to_all(packed, 're', split_axis=0, concat_axis=0, tiled=True)  4.12 us
  transfers between devices with their start and end apart: 6, of which 2 were waited for; matrix products, arithmetic and copies ran while one was open for 1% of the time, Pallas kernels for 14%

profile of v8, /device:TPU:1, one launch (start us, length us, event | category | flops | bytes accessed | tf_op | source)
XLA Modules:
  0.0 63.5 jit_solution(18426109653364300685)
XLA Ops:
  0.0 4.1 %mix.1 = (bf16[6,32,128]{2,1,0:T(8,128)(2,1)S(1)}, bf16[6,32,128]{2,1,0:T(8,128)(2,1)S(1)}, bf16[6,32,128]{2,1,0:T(8,128)(2,1)S(1)}, bf16[6,32,128]{2,1,0:T(8,12...) custom-call(f32[12,2,12]{2,1,0:T(2,128)} %bitcast.13, s32[2,3]{1,0:T(2,128)} %bitcast.15, s32[1]{0:T(128)} %bitcast.rank_ref, ...), custom_call_target="tpu_custom_call" | custom-call | tf_op jit(solution)/shard_map/mix/pallas_call | solution.py:268
  4.1 0.0 copy-start
  4.1 1.4 %collective-permute-start = (bf16[192,128]{1,0:T(8,128)(2,1)S(1)}, bf16[192,128]{1,0:T(8,128)(2,1)S(1)}, u32[]{:S(2)}, u32[]{:S(2)}) collective-permute-start(bf16[192,128]{1,0:T(8,128)(2,1)S(1)} %bitcast.12), channel_id=1, source_target_pairs={{0,1},{1,0},{2,3},{3,2},{4,5},{5,4},{6,7},{7,6},{8,9},{9,8},{10,11... | collective-permute-start | bytes 147464 | tf_op jit(solution)/shard_map/ppermute | solution.py:296
  5.6 3.7 %collective-permute-start.1 = (bf16[192,128]{1,0:T(8,128)(2,1)S(1)}, bf16[192,128]{1,0:T(8,128)(2,1)S(1)}, u32[]{:S(2)}, u32[]{:S(2)}) collective-permute-start(bf16[192,128]{1,0:T(8,128)(2,1)S(1)} %bitcast.11), channel_id=1, source_target_pairs={{0,2},{1,3},{2,0},{3,1},{4,6},{5,7},{6,4},{7,5},{8,10},{9,11},{10,... | collective-permute-start | bytes 147464 | tf_op jit(solution)/shard_map/ppermute | solution.py:296
  9.3 0.0 collective-permute-start.2
  9.3 8.0 %all-to-all-start = ((s32[32,1,128]{2,1,0:T(1,128)}), s32[32,1,128]{2,1,0:T(1,128)S(1)}, u32[]{:S(2)}, u32[]{:S(2)}) async-start(s32[32,1,128]{2,1,0:T(1,128)} %get-tuple-element.20), calls=%async_computation | async-start | bytes 32768 | tf_op jit(solution)/shard_map/all_to_all | solution.py:300
  17.3 0.0 collective-permute-done.one_ref
  17.3 0.0 collective-permute-done.1.two_ref
  17.3 0.0 collective-permute-done.2.three_ref
  17.3 1.5 %sum.1.packed_ref = bf16[32,216,128]{2,1,0:T(8,128)(2,1)} custom-call(bf16[192,128]{1,0:T(8,128)(2,1)S(1)} %bitcast.9, bf16[192,128]{1,0:T(8,128)(2,1)S(1)} %collective-permute-done.one_ref, bf16[192,128]{1,0:T(8,128)(2,1)S(1)} %collective-permute-done.1.two_ref, bf16[192,128]{1,0:T(8,128)(2,1)S(1)} %collective-permute-done.2.three_ref), custom_call_target="tpu_custom_call" | custom-call | tf_op jit(solution)/shard_map/sum/pallas_call | solution.py:302
  18.8 5.5 %all-to-all-done.request_ref = s32[32,1,128]{2,1,0:T(1,128)S(1)} async-done(((s32[32,1,128]{2,1,0:T(1,128)}), s32[32,1,128]{2,1,0:T(1,128)S(1)}, u32[]{:S(2)}, u32[]{:S(2)}) %all-to-all-start) | async-done | bytes 16416 | tf_op jit(solution)/shard_map/all_to_all | solution.py:300
  24.3 0.0 copy-done
  24.3 1.2 %lookup.1 = bf16[32,216,128]{2,1,0:T(8,128)(2,1)} custom-call(bf16[32,216,128]{2,1,0:T(8,128)(2,1)} %sum.1.packed_ref, s32[32,1,128]{2,1,0:T(1,128)S(1)} %all-to-all-done.request_ref, bf16[512,128]{1,0:T(8,128)(2,1)S(1)} %copy-done), custom_call_target="tpu_custom_call", output_to_operand_aliasing={{}: (0, {})} | custom-call | tf_op jit(solution)/shard_map/lookup/pallas_call | solution.py:311
  25.5 0.0 copy-start.1
  25.5 4.1 %all-to-all-start.1 = ((bf16[32,216,128]{2,1,0:T(8,128)(2,1)}), bf16[32,216,128]{2,1,0:T(8,128)(2,1)S(1)}, u32[]{:S(2)}, u32[]{:S(2)}) async-start(bf16[32,216,128]{2,1,0:T(8,128)(2,1)} %lookup.1), calls=%async_computation.1 | async-start | bytes 3538944 | tf_op jit(solution)/shard_map/all_to_all | solution.py:325
  29.6 0.0 copy-done.1
  29.6 0.6 fusion
  30.2 2.2 %phase.2.first_ref = bf16[2,1024,256]{2,1,0:T(8,128)(2,1)S(1)} custom-call(s32[3,1024]{1,0:T(4,128)} %re_ref.3, s32[3,256]{1,0:T(4,128)} %get-tuple-element.24.k_ref), custom_call_target="tpu_custom_call" | custom-call | tf_op jit(solution)/shard_map/phase/pallas_call | solution.py:329
  32.4 3.2 %phase.3.later_hbm = bf16[2,1024,256]{2,1,0:T(8,128)(2,1)} custom-call(s32[3,1024]{1,0:T(4,128)} %re_ref.3, s32[3,256]{1,0:T(4,128)} %get-tuple-element.23.k_ref), custom_call_target="tpu_custom_call" | custom-call | tf_op jit(solution)/shard_map/phase/pallas_call | solution.py:329
  35.6 18.2 %all-to-all-done.1.gathered_ref = bf16[32,216,128]{2,1,0:T(8,128)(2,1)S(1)} async-done(((bf16[32,216,128]{2,1,0:T(8,128)(2,1)}), bf16[32,216,128]{2,1,0:T(8,128)(2,1)S(1)}, u32[]{:S(2)}, u32[]{:S(2)}) %all-to-all-start.1) | async-done | bytes 1769504 | tf_op jit(solution)/shard_map/all_to_all | solution.py:325
  53.8 0.4 far.1.mine_ref
  54.1 2.7 %collective-permute-start.3 = (bf16[128,512]{1,0:T(8,128)(2,1)S(1)}, bf16[128,512]{1,0:T(8,128)(2,1)S(1)}, u32[]{:S(2)}, u32[]{:S(2)}) collective-permute-start(bf16[128,512]{1,0:T(8,128)(2,1)S(1)} %far.1.mine_ref), channel_id=1, source_target_pairs={{0,1},{1,0},{2,3},{3,2},{4,5},{5,4},{6,7},{7,6},{8,9},{9,8},{10,11... | collective-permute-start | bytes 393224 | tf_op jit(solution)/shard_map/ppermute | solution.py:347
  56.8 2.2 %couple.1.coupling_ref = f32[4,6,192,128]{3,2,1,0:T(8,128)S(1)} custom-call(bf16[2,1024,256]{2,1,0:T(8,128)(2,1)S(1)} %phase.2.first_ref, bf16[2,1024,256]{2,1,0:T(8,128)(2,1)} %phase.3.later_hbm, bf16[32,216,128]{2,1,0:T(8,128)(2,1)S(1)} %all-to-all-done.1.gathered_ref), custom_call_target="tpu_custom_call" | custom-call | tf_op jit(solution)/shard_map/couple/pallas_call | solution.py:348
  59.0 0.0 collective-permute-done.3.mate_ref
  59.1 4.3 %final.1 = bf16[6,2,64,512]{3,2,1,0:T(8,128)(2,1)} custom-call(s32[1]{0:T(128)} %bitcast.rank_ref, bf16[512,128]{1,0:T(8,128)(2,1)S(1)} %copy-done, bf16[128,512]{1,0:T(8,128)(2,1)S(1)} %far.1.mine_ref, bf16[128,512]{1,0:T(8,128)(2,1)S(1)} %collective-permute-done.3.mate_ref, f32[4,6,192,128]{3,2,1,0:T(8,128)S(1)} %couple.1.coupling_ref), custom_call_target="tpu_custom_call" | custom-call | tf_op jit(solution)/shard_map/final/pallas_call | solution.py:360
Async XLA Ops:
  4.1 20.1 %copy-start = (bf16[512,128]{1,0:T(8,128)(2,1)S(1)}, bf16[512,128]{1,0:T(8,128)(2,1)}, u32[]{:S(2)}) copy-start(bf16[512,128]{1,0:T(8,128)(2,1)} %rotations_ref.3) | copy-start | bytes 393220
  4.1 13.1 %collective-permute-start = (bf16[192,128]{1,0:T(8,128)(2,1)S(1)}, bf16[192,128]{1,0:T(8,128)(2,1)S(1)}, u32[]{:S(2)}, u32[]{:S(2)}) collective-permute-start(bf16[192,128]{1,0:T(8,128)(2,1)S(1)} %bitcast.12), channel_id=1, source_target_pairs={{0,1},{1,0},{2,3},{3,2},{4,5},{5,4},{6,7},{7,6},{8,9},{9,8},{10,11... | collective-permute-start | bytes 147464 | tf_op jit(solution)/shard_map/ppermute | solution.py:296
  5.6 11.7 %collective-permute-start.1 = (bf16[192,128]{1,0:T(8,128)(2,1)S(1)}, bf16[192,128]{1,0:T(8,128)(2,1)S(1)}, u32[]{:S(2)}, u32[]{:S(2)}) collective-permute-start(bf16[192,128]{1,0:T(8,128)(2,1)S(1)} %bitcast.11), channel_id=1, source_target_pairs={{0,2},{1,3},{2,0},{3,1},{4,6},{5,7},{6,4},{7,5},{8,10},{9,11},{10,... | collective-permute-start | bytes 147464 | tf_op jit(solution)/shard_map/ppermute | solution.py:296
  9.3 8.0 %collective-permute-start.2 = (bf16[192,128]{1,0:T(8,128)(2,1)S(1)}, bf16[192,128]{1,0:T(8,128)(2,1)S(1)}, u32[]{:S(2)}, u32[]{:S(2)}) collective-permute-start(bf16[192,128]{1,0:T(8,128)(2,1)S(1)} %bitcast.10), channel_id=1, source_target_pairs={{0,3},{1,2},{2,1},{3,0},{4,7},{5,6},{6,5},{7,4},{8,11},{9,10},{10,... | collective-permute-start | bytes 147464 | tf_op jit(solution)/shard_map/ppermute | solution.py:296
  9.3 15.0 %all-to-all-start = ((s32[32,1,128]{2,1,0:T(1,128)}), s32[32,1,128]{2,1,0:T(1,128)S(1)}, u32[]{:S(2)}, u32[]{:S(2)}) async-start(s32[32,1,128]{2,1,0:T(1,128)} %get-tuple-element.20), calls=%async_computation | async-start | bytes 32768 | tf_op jit(solution)/shard_map/all_to_all | solution.py:300
  25.5 4.1 %copy-start.1 = (s32[3,512]{1,0:T(4,128)S(1)}, s32[3,512]{1,0:T(4,128)}, u32[]{:S(2)}) copy-start(s32[3,512]{1,0:T(4,128)} %param.14) | copy-start | bytes 18436
  25.5 28.3 %all-to-all-start.1 = ((bf16[32,216,128]{2,1,0:T(8,128)(2,1)}), bf16[32,216,128]{2,1,0:T(8,128)(2,1)S(1)}, u32[]{:S(2)}, u32[]{:S(2)}) async-start(bf16[32,216,128]{2,1,0:T(8,128)(2,1)} %lookup.1), calls=%async_computation.1 | async-start | bytes 3538944 | tf_op jit(solution)/shard_map/all_to_all | solution.py:325
  54.1 4.9 %collective-permute-start.3 = (bf16[128,512]{1,0:T(8,128)(2,1)S(1)}, bf16[128,512]{1,0:T(8,128)(2,1)S(1)}, u32[]{:S(2)}, u32[]{:S(2)}) collective-permute-start(bf16[128,512]{1,0:T(8,128)(2,1)S(1)} %far.1.mine_ref), channel_id=1, source_target_pairs={{0,1},{1,0},{2,3},{3,2},{4,5},{5,4},{6,7},{7,6},{8,9},{9,8},{10,11... | collective-permute-start | bytes 393224 | tf_op jit(solution)/shard_map/ppermute | solution.py:347

commit v9 on v8

--- a/solution.py
+++ b/solution.py
@@ -212,14 +212,24 @@
             out_ref[t, i, 2 * SIZE :] = real + imag
 
 
-def final_kernel(rank_ref, rotations_ref, mine_ref, mate_ref, coupling_ref, out_hbm, near_ref, far_ref, out_ref, out_sem):
-    out_copies = [
-        pltpu.make_async_copy(out_ref.at[t], out_hbm.at[:, :, :, t * LANES : (t + 1) * LANES], out_sem.at[t])
-        for t in range(TILES)
-    ]
+def near_kernel(rotations_ref, near_ref):
     near = rotations_ref[...].astype(F32).T
     near_ref[: 2 * SIZE] = near
     near_ref[2 * SIZE :] = near[:SIZE] + near[SIZE:]
+
+
+def final_kernel(rank_ref, near_ref, mine_ref, mate_ref, coupling_ref, out_hbm, far_ref, out_ref, out_sem):
+    out_copies = [
+        [
+            pltpu.make_async_copy(
+                out_ref.at[t, q * M_LOCAL : (q + 1) * M_LOCAL],
+                out_hbm.at[q * M_LOCAL : (q + 1) * M_LOCAL, :, :, t * LANES : (t + 1) * LANES],
+                out_sem.at[t, q],
+            )
+            for q in range(Q)
+        ]
+        for t in range(TILES)
+    ]
     mine = mine_ref[...].astype(F32)
     mate = mate_ref[...].astype(F32)
     for q in range(Q):
@@ -227,11 +237,13 @@
         far_ref[q, : 2 * SIZE] = far
         far_ref[q, 2 * SIZE :] = far[:SIZE] - far[SIZE:]
     for t in range(TILES):
-        for i in range(Q * M_LOCAL):
-            rotate(coupling_ref.at[t, i], far_ref, near_ref, out_ref, i // M_LOCAL, i, t)
-        out_copies[t].start()
+        for q in range(Q):
+            for i in range(q * M_LOCAL, (q + 1) * M_LOCAL):
+                rotate(coupling_ref.at[t, i], far_ref, near_ref, out_ref, q, i, t)
+            out_copies[t][q].start()
     for t in range(TILES):
-        out_copies[t].wait()
+        for q in range(Q):
+            out_copies[t][q].wait()
 
 
 def whole(shape):
@@ -336,7 +348,14 @@
     first = phase_tiles(k_coords[:, : FIRST * LANES], pltpu.VMEM)
     later = phase_tiles(k_coords[:, FIRST * LANES :], pltpu.HBM)
 
-    slots, first, later = lax.optimization_barrier((slots, first, later))
+    near = pl.pallas_call(
+        near_kernel,
+        in_specs=[vmem],
+        out_shape=pltpu.VMEM((3 * SIZE, K), F32),
+        compiler_params=params(8),
+        name="near",
+    )(rotations)
+    slots, first, later, near = lax.optimization_barrier((slots, first, later, near))
     far = pl.pallas_call(
         far_kernel,
         in_specs=[vmem, vmem],
@@ -363,14 +382,13 @@
         out_specs=hbm,
         out_shape=jax.ShapeDtypeStruct((Q * M_LOCAL, 2, SIZE, K), BF),
         scratch_shapes=[
-            pltpu.VMEM((3 * SIZE, K), F32),
             pltpu.VMEM((Q, 3 * SIZE, K), F32),
             pltpu.VMEM((TILES, Q * M_LOCAL, 2, SIZE, LANES), BF),
-            pltpu.SemaphoreType.DMA((TILES,)),
+            pltpu.SemaphoreType.DMA((TILES, Q)),
         ],
         compiler_params=params(16),
         name="final",
-    )(rank, rotations, far, mate, coupling)
+    )(rank, near, far, mate, coupling)
     return result.reshape(Q, M_LOCAL, 2, NB * NB, K)
 
 

time: 63.9 us -> 62.8 us (0.983)
  Pallas kernels: 19.1 us -> 18.4 us
    pallas_call x1, Pallas kernels: 4.33 us -> 3.55 us  [local(): pl.pallas_call(final_kernel, in_specs=[smem(), vmem, vmem, vmem, vmem], o...]
  transfers between devices with their start and end apart: 6 -> 6, of which waited for: 2 -> 2; matrix products, arithmetic and copies ran while one was open for 1% -> 1% of each run, Pallas kernels for 14% -> 15%
where the time goes in v9:
time: 62.8 us; the launch traced here: 62.4 us
  waiting for transfers between devices  23.6 us (38%)
  starting transfers between devices  19.7 us (31%)
  Pallas kernels  18.4 us (29%)
    all_to_all x1, waiting for transfers between devices, local(): lax.all_to_all(packed, 're', split_axis=0, concat_axis=0, tiled=True)  18.1 us
    all_to_all x1, starting transfers between devices, local(): lax.all_to_all(requests, 're', split_axis=0, concat_axis=0, tiled=True)  7.95 us
    all_to_all x1, waiting for transfers between devices, local(): lax.all_to_all(requests, 're', split_axis=0, concat_axis=0, tiled=True)  5.49 us
    pallas_call x2, Pallas kernels, phase_tiles(): pl.pallas_call(phase_kernel, out_shape=space((tiles, RE, 2 * LANES), BF),...  5.36 us
    ppermute x3, starting transfers between devices, local(): lax.ppermute(parts[s].reshape(ROWS, LANES), 'rp', [(j, j ^ s) for j in ra...  5.16 us
    pallas_call x1, Pallas kernels, local(): pl.pallas_call(mix_kernel, grid=(RE_LOCAL // CHUNK,), in_specs=[smem(), s...  4.15 us
    all_to_all x1, starting transfers between devices, local(): lax.all_to_all(packed, 're', split_axis=0, concat_axis=0, tiled=True)  4.12 us
    pallas_call x1, Pallas kernels, local(): pl.pallas_call(final_kernel, in_specs=[smem(), vmem, vmem, vmem, vmem], o...  3.55 us
  transfers between devices with their start and end apart: 6, of which 2 were waited for; matrix products, arithmetic and copies ran while one was open for 1% of the time, Pallas kernels for 15%

profile of v9, /device:TPU:1, one launch (start us, length us, event | category | flops | bytes accessed | tf_op | source)
XLA Modules:
  0.0 62.4 jit_solution(10689299998942863938)
XLA Ops:
  0.0 4.1 %mix.1 = (bf16[6,32,128]{2,1,0:T(8,128)(2,1)S(1)}, bf16[6,32,128]{2,1,0:T(8,128)(2,1)S(1)}, bf16[6,32,128]{2,1,0:T(8,128)(2,1)S(1)}, bf16[6,32,128]{2,1,0:T(8,12...) custom-call(f32[12,2,12]{2,1,0:T(2,128)} %bitcast.13, s32[2,3]{1,0:T(2,128)} %bitcast.15, s32[1]{0:T(128)} %bitcast.rank_ref, ...), custom_call_target="tpu_custom_call" | custom-call | tf_op jit(solution)/shard_map/mix/pallas_call | solution.py:280
  4.1 0.0 copy-start
  4.2 1.4 %collective-permute-start = (bf16[192,128]{1,0:T(8,128)(2,1)S(1)}, bf16[192,128]{1,0:T(8,128)(2,1)S(1)}, u32[]{:S(2)}, u32[]{:S(2)}) collective-permute-start(bf16[192,128]{1,0:T(8,128)(2,1)S(1)} %bitcast.12), channel_id=1, source_target_pairs={{0,1},{1,0},{2,3},{3,2},{4,5},{5,4},{6,7},{7,6},{8,9},{9,8},{10,11... | collective-permute-start | bytes 147464 | tf_op jit(solution)/shard_map/ppermute | solution.py:308
  5.6 3.7 %collective-permute-start.1 = (bf16[192,128]{1,0:T(8,128)(2,1)S(1)}, bf16[192,128]{1,0:T(8,128)(2,1)S(1)}, u32[]{:S(2)}, u32[]{:S(2)}) collective-permute-start(bf16[192,128]{1,0:T(8,128)(2,1)S(1)} %bitcast.11), channel_id=1, source_target_pairs={{0,2},{1,3},{2,0},{3,1},{4,6},{5,7},{6,4},{7,5},{8,10},{9,11},{10,... | collective-permute-start | bytes 147464 | tf_op jit(solution)/shard_map/ppermute | solution.py:308
  9.3 0.0 collective-permute-start.2
  9.3 8.0 %all-to-all-start = ((s32[32,1,128]{2,1,0:T(1,128)}), s32[32,1,128]{2,1,0:T(1,128)S(1)}, u32[]{:S(2)}, u32[]{:S(2)}) async-start(s32[32,1,128]{2,1,0:T(1,128)} %get-tuple-element.22), calls=%async_computation | async-start | bytes 32768 | tf_op jit(solution)/shard_map/all_to_all | solution.py:312
  17.3 0.0 collective-permute-done.one_ref
  17.3 0.0 collective-permute-done.1.two_ref
  17.3 0.0 collective-permute-done.2.three_ref
  17.3 1.5 %sum.1.packed_ref = bf16[32,216,128]{2,1,0:T(8,128)(2,1)} custom-call(bf16[192,128]{1,0:T(8,128)(2,1)S(1)} %bitcast.9, bf16[192,128]{1,0:T(8,128)(2,1)S(1)} %collective-permute-done.one_ref, bf16[192,128]{1,0:T(8,128)(2,1)S(1)} %collective-permute-done.1.two_ref, bf16[192,128]{1,0:T(8,128)(2,1)S(1)} %collective-permute-done.2.three_ref), custom_call_target="tpu_custom_call" | custom-call | tf_op jit(solution)/shard_map/sum/pallas_call | solution.py:314
  18.8 5.5 %all-to-all-done.request_ref = s32[32,1,128]{2,1,0:T(1,128)S(1)} async-done(((s32[32,1,128]{2,1,0:T(1,128)}), s32[32,1,128]{2,1,0:T(1,128)S(1)}, u32[]{:S(2)}, u32[]{:S(2)}) %all-to-all-start) | async-done | bytes 16416 | tf_op jit(solution)/shard_map/all_to_all | solution.py:312
  24.3 0.0 copy-done
  24.3 1.2 %lookup.1 = bf16[32,216,128]{2,1,0:T(8,128)(2,1)} custom-call(bf16[32,216,128]{2,1,0:T(8,128)(2,1)} %sum.1.packed_ref, s32[32,1,128]{2,1,0:T(1,128)S(1)} %all-to-all-done.request_ref, bf16[512,128]{1,0:T(8,128)(2,1)S(1)} %copy-done), custom_call_target="tpu_custom_call", output_to_operand_aliasing={{}: (0, {})} | custom-call | tf_op jit(solution)/shard_map/lookup/pallas_call | solution.py:323
  25.5 0.0 copy-start.1
  25.5 4.1 %all-to-all-start.1 = ((bf16[32,216,128]{2,1,0:T(8,128)(2,1)}), bf16[32,216,128]{2,1,0:T(8,128)(2,1)S(1)}, u32[]{:S(2)}, u32[]{:S(2)}) async-start(bf16[32,216,128]{2,1,0:T(8,128)(2,1)} %lookup.1), calls=%async_computation.1 | async-start | bytes 3538944 | tf_op jit(solution)/shard_map/all_to_all | solution.py:337
  29.6 0.1 near.1.near_ref
  29.7 0.0 copy-done.1
  29.7 0.6 fusion
  30.3 2.2 %phase.2.first_ref = bf16[2,1024,256]{2,1,0:T(8,128)(2,1)S(1)} custom-call(s32[3,1024]{1,0:T(4,128)} %re_ref.3, s32[3,256]{1,0:T(4,128)} %get-tuple-element.26.k_ref), custom_call_target="tpu_custom_call" | custom-call | tf_op jit(solution)/shard_map/phase/pallas_call | solution.py:341
  32.5 3.2 %phase.3.later_hbm = bf16[2,1024,256]{2,1,0:T(8,128)(2,1)} custom-call(s32[3,1024]{1,0:T(4,128)} %re_ref.3, s32[3,256]{1,0:T(4,128)} %get-tuple-element.25.k_ref), custom_call_target="tpu_custom_call" | custom-call | tf_op jit(solution)/shard_map/phase/pallas_call | solution.py:341
  35.7 18.1 %all-to-all-done.1.gathered_ref = bf16[32,216,128]{2,1,0:T(8,128)(2,1)S(1)} async-done(((bf16[32,216,128]{2,1,0:T(8,128)(2,1)}), bf16[32,216,128]{2,1,0:T(8,128)(2,1)S(1)}, u32[]{:S(2)}, u32[]{:S(2)}) %all-to-all-start.1) | async-done | bytes 1769504 | tf_op jit(solution)/shard_map/all_to_all | solution.py:337
  53.8 0.4 far.1.mine_ref
  54.1 2.5 %collective-permute-start.3 = (bf16[128,512]{1,0:T(8,128)(2,1)S(1)}, bf16[128,512]{1,0:T(8,128)(2,1)S(1)}, u32[]{:S(2)}, u32[]{:S(2)}) collective-permute-start(bf16[128,512]{1,0:T(8,128)(2,1)S(1)} %far.1.mine_ref), channel_id=1, source_target_pairs={{0,1},{1,0},{2,3},{3,2},{4,5},{5,4},{6,7},{7,6},{8,9},{9,8},{10,11... | collective-permute-start | bytes 393224 | tf_op jit(solution)/shard_map/ppermute | solution.py:366
  56.6 2.2 %couple.1.coupling_ref = f32[4,6,192,128]{3,2,1,0:T(8,128)S(1)} custom-call(bf16[2,1024,256]{2,1,0:T(8,128)(2,1)S(1)} %phase.2.first_ref, bf16[2,1024,256]{2,1,0:T(8,128)(2,1)} %phase.3.later_hbm, bf16[32,216,128]{2,1,0:T(8,128)(2,1)S(1)} %all-to-all-done.1.gathered_ref), custom_call_target="tpu_custom_call" | custom-call | tf_op jit(solution)/shard_map/couple/pallas_call | solution.py:367
  58.9 0.0 collective-permute-done.3.mate_ref
  58.9 3.5 %final.1 = bf16[6,2,64,512]{3,2,1,0:T(8,128)(2,1)} custom-call(s32[1]{0:T(128)} %bitcast.rank_ref, f32[192,512]{1,0:T(8,128)S(1)} %near.1.near_ref, bf16[128,512]{1,0:T(8,128)(2,1)S(1)} %far.1.mine_ref, bf16[128,512]{1,0:T(8,128)(2,1)S(1)} %collective-permute-done.3.mate_ref, f32[4,6,192,128]{3,2,1,0:T(8,128)S(1)} %couple.1.coupling_ref), custom_call_target="tpu_custom_call" | custom-call | tf_op jit(solution)/shard_map/final/pallas_call | solution.py:379
Async XLA Ops:
  4.1 20.1 %copy-start = (bf16[512,128]{1,0:T(8,128)(2,1)S(1)}, bf16[512,128]{1,0:T(8,128)(2,1)}, u32[]{:S(2)}) copy-start(bf16[512,128]{1,0:T(8,128)(2,1)} %rotations_ref.3) | copy-start | bytes 393220
  4.2 13.1 %collective-permute-start = (bf16[192,128]{1,0:T(8,128)(2,1)S(1)}, bf16[192,128]{1,0:T(8,128)(2,1)S(1)}, u32[]{:S(2)}, u32[]{:S(2)}) collective-permute-start(bf16[192,128]{1,0:T(8,128)(2,1)S(1)} %bitcast.12), channel_id=1, source_target_pairs={{0,1},{1,0},{2,3},{3,2},{4,5},{5,4},{6,7},{7,6},{8,9},{9,8},{10,11... | collective-permute-start | bytes 147464 | tf_op jit(solution)/shard_map/ppermute | solution.py:308
  5.6 11.7 %collective-permute-start.1 = (bf16[192,128]{1,0:T(8,128)(2,1)S(1)}, bf16[192,128]{1,0:T(8,128)(2,1)S(1)}, u32[]{:S(2)}, u32[]{:S(2)}) collective-permute-start(bf16[192,128]{1,0:T(8,128)(2,1)S(1)} %bitcast.11), channel_id=1, source_target_pairs={{0,2},{1,3},{2,0},{3,1},{4,6},{5,7},{6,4},{7,5},{8,10},{9,11},{10,... | collective-permute-start | bytes 147464 | tf_op jit(solution)/shard_map/ppermute | solution.py:308
  9.3 8.0 %collective-permute-start.2 = (bf16[192,128]{1,0:T(8,128)(2,1)S(1)}, bf16[192,128]{1,0:T(8,128)(2,1)S(1)}, u32[]{:S(2)}, u32[]{:S(2)}) collective-permute-start(bf16[192,128]{1,0:T(8,128)(2,1)S(1)} %bitcast.10), channel_id=1, source_target_pairs={{0,3},{1,2},{2,1},{3,0},{4,7},{5,6},{6,5},{7,4},{8,11},{9,10},{10,... | collective-permute-start | bytes 147464 | tf_op jit(solution)/shard_map/ppermute | solution.py:308
  9.3 15.0 %all-to-all-start = ((s32[32,1,128]{2,1,0:T(1,128)}), s32[32,1,128]{2,1,0:T(1,128)S(1)}, u32[]{:S(2)}, u32[]{:S(2)}) async-start(s32[32,1,128]{2,1,0:T(1,128)} %get-tuple-element.22), calls=%async_computation | async-start | bytes 32768 | tf_op jit(solution)/shard_map/all_to_all | solution.py:312
  25.5 4.2 %copy-start.1 = (s32[3,512]{1,0:T(4,128)S(1)}, s32[3,512]{1,0:T(4,128)}, u32[]{:S(2)}) copy-start(s32[3,512]{1,0:T(4,128)} %param.14) | copy-start | bytes 18436
  25.5 28.3 %all-to-all-start.1 = ((bf16[32,216,128]{2,1,0:T(8,128)(2,1)}), bf16[32,216,128]{2,1,0:T(8,128)(2,1)S(1)}, u32[]{:S(2)}, u32[]{:S(2)}) async-start(bf16[32,216,128]{2,1,0:T(8,128)(2,1)} %lookup.1), calls=%async_computation.1 | async-start | bytes 3538944 | tf_op jit(solution)/shard_map/all_to_all | solution.py:337
  54.1 4.7 %collective-permute-start.3 = (bf16[128,512]{1,0:T(8,128)(2,1)S(1)}, bf16[128,512]{1,0:T(8,128)(2,1)S(1)}, u32[]{:S(2)}, u32[]{:S(2)}) collective-permute-start(bf16[128,512]{1,0:T(8,128)(2,1)S(1)} %far.1.mine_ref), channel_id=1, source_target_pairs={{0,1},{1,0},{2,3},{3,2},{4,5},{5,4},{6,7},{7,6},{8,9},{9,8},{10,11... | collective-permute-start | bytes 393224 | tf_op jit(solution)/shard_map/ppermute | solution.py:366
